TPU v7x, 128 devices: a whole 4x4x4 slice. The times are simulated.
128 devices in a mesh: lon: 16 (over z, x_hi, core), lat: 8 (over x_lo, y).
Axes of the slice: x: 4 (x_hi: 2, x_lo: 2; x = x_hi * 2 + x_lo), y: 4, z: 4, core: 2. Of those that a mesh axis runs over, the one named last changes fastest.
Arguments:
- innovations: bfloat16 [7, 16384, 16, 128], P(None, ('lon', 'lat')), may hold values from -6 to 6
- fractions: bfloat16 [7, 16384, 2, 128], P(None, ('lon', 'lat')), may hold values from 0 to 1
- cell_index: int32 [7, 16384, 128], P(None, ('lon', 'lat')), may hold values from 0 to 238, as said below
- counts: int32 [7, 16384, 2], P(None, ('lon', 'lat')), may hold values from 0 to 64, as said below
- blocks: int32 [7, 16384, 2], P(None, ('lon', 'lat')), may hold values from 0 to 15
- u_wind: float32 [4, 256, 2048], P(None, 'lat', 'lon'), may hold values from -0.5 to 0.5
- v_wind: float32 [4, 256, 2048], P(None, 'lat', 'lon'), may hold values from -0.5 to 0.5
- channel_mix: float32 [16, 16], replicated
Outputs:
- gradient: float32 [4, 4, 256, 2048], P(None, None, 'lat', 'lon')
Inputs may be any that keep to these rules, and one draw needn't show every extreme that they name: Row and column of a cell inside its tile, cell_index // 16 and cell_index % 16, are each at most 14. `counts`: in every draw some receiving device gets 64 live observations in every tile from every sender.
All inputs are finite; a program needn't handle non-finite values.
Results may differ from a plain program's by a relative error of at most 0.0003.
Values may be sent and summed in bfloat16 or wider, within the bound.
No kernel may reach another device: no remote copies, remote signals or barrier semaphores. Data moves between devices by JAX's collectives and lax.ppermute only.
A program may use at most 192 MiB of HBM per device.

v0:
```python
import jax
import jax.numpy as jnp
from jax import lax
from jax.sharding import PartitionSpec as P

VARS = 4
LEV = 4
CH = 16
TILE = 16


KAPPA = 0.125
HIGHEST = lax.Precision.HIGHEST


def with_halo(array, sides, width, wrap):
    for axis, dim in sides:
        count, length = (lax.axis_size(axis), array.shape[dim])
        up = [(i, (i + 1) % count) for i in range(count if wrap else count - 1)]
        down = [(j, i) for i, j in up]
        last = lax.slice_in_dim(array, length - width, length, axis=dim)
        leading = lax.slice_in_dim(array, 0, width, axis=dim)
        before = lax.ppermute(last, axis, up)
        after = lax.ppermute(leading, axis, down)
        array = jnp.concatenate([before, array, after], axis=dim)
    return array


def build_tiles(values, fractions, cell_index, counts):
    targets, channels, width = values.shape
    slot_count = counts.shape[1]
    per_tile = width // slot_count
    within = lax.broadcasted_iota(jnp.int32, (1, 1, per_tile), 2)
    is_live = within < counts[:, :, None]
    frac_y = (
        fractions[:, 0, :].astype(jnp.float32).reshape(targets, slot_count, per_tile)[..., None]
    )
    frac_x = (
        fractions[:, 1, :].astype(jnp.float32).reshape(targets, slot_count, per_tile)[..., None]
    )
    corner = cell_index.reshape(targets, slot_count, per_tile)[..., None]
    position = lax.broadcasted_iota(jnp.int32, (1, 1, 1, TILE * TILE), 3)
    weight = jnp.where(position == corner, (1.0 - frac_y) * (1.0 - frac_x), 0.0)
    weight = weight + jnp.where(position == corner + 1, (1.0 - frac_y) * frac_x, 0.0)
    weight = weight + jnp.where(position == corner + TILE, frac_y * (1.0 - frac_x), 0.0)
    weight = weight + jnp.where(position == corner + TILE + 1, frac_y * frac_x, 0.0)
    weight = jnp.where(is_live[..., None], weight, 0.0)
    innov_f32 = values.reshape(targets, channels, slot_count, per_tile).astype(jnp.float32)
    return jnp.einsum("dcaj,dajp->dacp", innov_f32, weight, precision=HIGHEST)


def build_slot(members):
    return build_tiles(members[0], members[1], members[2], members[3])


def place_tiles(tile_sets, tile_blocks, lat_cells, lon_cells):
    block_rows = lat_cells // TILE
    block_cols = lon_cells // TILE
    block_ids = lax.broadcasted_iota(jnp.int32, (1, 1, 1, block_rows * block_cols), 3)
    onehot = jnp.where(tile_blocks[..., None] == block_ids, 1.0, 0.0).astype(jnp.float32)
    summed = jnp.einsum("sdab,sdacp->scbp", onehot, tile_sets, precision=HIGHEST)
    slot_total = summed.shape[0]
    summed = summed.reshape(slot_total, VARS, LEV, block_rows, block_cols, TILE, TILE)
    summed = jnp.transpose(summed, (0, 1, 2, 3, 5, 4, 6))
    return summed.reshape(slot_total, VARS, LEV, lat_cells, lon_cells)


def shards(innovations, fractions, cell_index, counts, blocks, u_wind, v_wind, channel_mix):
    lat_cells = u_wind.shape[1]
    lon_cells = u_wind.shape[2]
    own_tiles = lax.map(build_slot, (innovations, fractions, cell_index, counts))
    got_blocks = lax.all_to_all(blocks, ("lon", "lat"), split_axis=1, concat_axis=1, tiled=True)
    tile_sets = lax.all_to_all(own_tiles, ("lon", "lat"), split_axis=1, concat_axis=1, tiled=True)
    forcing = place_tiles(tile_sets, got_blocks, lat_cells, lon_cells)
    slot_total = forcing.shape[0]
    adjoint_field = forcing[slot_total - 1]
    for later in range(slot_total - 2, -1, -1):
        mixed = jnp.einsum(
            "dc,dn->cn",
            channel_mix,
            adjoint_field.reshape(CH, lat_cells * lon_cells),
            precision=HIGHEST,
        )
        mixed = mixed.reshape(VARS, LEV, lat_cells, lon_cells)
        east_flux = u_wind[None] * mixed
        north_flux = v_wind[None] * mixed
        cycle_pad = with_halo(jnp.stack([mixed, east_flux]), (("lon", 4),), 1, True)
        band_pad = with_halo(jnp.stack([mixed, north_flux]), (("lat", 3),), 1, False)
        lon_after = cycle_pad[0, :, :, :, 2:]
        lon_before = cycle_pad[0, :, :, :, :-2]
        east_after = cycle_pad[1, :, :, :, 2:]
        east_before = cycle_pad[1, :, :, :, :-2]
        lat_after = band_pad[0, :, :, 2:, :]
        lat_before = band_pad[0, :, :, :-2, :]
        north_after = band_pad[1, :, :, 2:, :]
        north_before = band_pad[1, :, :, :-2, :]
        spread = lon_after + lon_before + lat_after + lat_before
        carry_term = 0.5 * (east_after - east_before) + 0.5 * (north_after - north_before)
        adjoint_field = (1.0 - 4.0 * KAPPA) * mixed + KAPPA * spread + carry_term + forcing[later]
    return adjoint_field


def solution(mesh):
    in_specs = (
        P(None, ("lon", "lat"), None, None),
        P(None, ("lon", "lat"), None, None),
        P(None, ("lon", "lat"), None),
        P(None, ("lon", "lat"), None),
        P(None, ("lon", "lat"), None),
        P(None, "lat", "lon"),
        P(None, "lat", "lon"),
        P(),
    )
    out_specs = P(None, None, "lat", "lon")
    return jax.shard_map(shards, mesh=mesh, in_specs=in_specs, out_specs=out_specs, check_vma=False)
```

profile of v0, /device:TPU:2, one launch (start us, length us, event | category | flops | bytes accessed | tf_op | source)
XLA Modules:
  0.0 1119.8 jit_solution(865921136315395198)
XLA Ops:
  1.5 11.0 all-to-all-start.1
  12.5 424.5 %while.12 = (s32[]{:T(128)}, f32[7,128,2,16,256]{4,2,3,0,1:T(2,128)}, bf16[7,128,16,128]{3,2,1,0:T(8,128)(2,1)}, s32[7,128,2]{1,2,0:T(2,128)}, s32[7,128,128]{2,...) while((s32[]{:T(128)}, f32[7,128,2,16,256]{4,2,3,0,1:T(2,128)}, ...), condition=%wide.region_1.2_spmd, body=%wide.region_0.1_spmd.sunk | while | flops 855834624 | bytes 19109468 | solution.py:71
  19.7 47.3 %fusion.142 = f32[1,128,2,16,256]{4,3,2,1,0:T(8,128)S(1)} fusion(bf16[128,16,2,64]{3,1,2,0:T(8,128)(2,1)S(1)} %copy.157, f32[128,2,64]{2,1,0:T(2,128)S(1)} %copy.159, s32[128,2,64]{2,1,0:T(2,128)S(1)} %copy.161, f32[128,2,64]{2,1,0:T(2,128)S(1)} %copy.162, s32[128,2,64]{2,1,0:T(2,128)S(1)} %copy.163, f32[128,2,64]{2,1,0:T(2,128)S(1)} %copy.164, ...), kind=kOutput, calls=%fused_computation.24.clone.2 | convolution fusion | flops 855638016 | bytes 5259264 | tf_op jit(solution)/shard_map/while/body/eval_jaxpr/dcaj,dajp->dacp/dot_general | solution.py:49
  67.0 6.2 copy_dynamic-update-slice_fusion.2
  80.4 47.3 %fusion.142 = f32[1,128,2,16,256]{4,3,2,1,0:T(8,128)S(1)} fusion(bf16[128,16,2,64]{3,1,2,0:T(8,128)(2,1)S(1)} %copy.157, f32[128,2,64]{2,1,0:T(2,128)S(1)} %copy.159, s32[128,2,64]{2,1,0:T(2,128)S(1)} %copy.161, f32[128,2,64]{2,1,0:T(2,128)S(1)} %copy.162, s32[128,2,64]{2,1,0:T(2,128)S(1)} %copy.163, f32[128,2,64]{2,1,0:T(2,128)S(1)} %copy.164, ...), kind=kOutput, calls=%fused_computation.24.clone.2 | convolution fusion | flops 855638016 | bytes 5259264 | tf_op jit(solution)/shard_map/while/body/eval_jaxpr/dcaj,dajp->dacp/dot_general | solution.py:49
  141.0 47.3 %fusion.142 = f32[1,128,2,16,256]{4,3,2,1,0:T(8,128)S(1)} fusion(bf16[128,16,2,64]{3,1,2,0:T(8,128)(2,1)S(1)} %copy.157, f32[128,2,64]{2,1,0:T(2,128)S(1)} %copy.159, s32[128,2,64]{2,1,0:T(2,128)S(1)} %copy.161, f32[128,2,64]{2,1,0:T(2,128)S(1)} %copy.162, s32[128,2,64]{2,1,0:T(2,128)S(1)} %copy.163, f32[128,2,64]{2,1,0:T(2,128)S(1)} %copy.164, ...), kind=kOutput, calls=%fused_computation.24.clone.2 | convolution fusion | flops 855638016 | bytes 5259264 | tf_op jit(solution)/shard_map/while/body/eval_jaxpr/dcaj,dajp->dacp/dot_general | solution.py:49
  201.6 47.3 %fusion.142 = f32[1,128,2,16,256]{4,3,2,1,0:T(8,128)S(1)} fusion(bf16[128,16,2,64]{3,1,2,0:T(8,128)(2,1)S(1)} %copy.157, f32[128,2,64]{2,1,0:T(2,128)S(1)} %copy.159, s32[128,2,64]{2,1,0:T(2,128)S(1)} %copy.161, f32[128,2,64]{2,1,0:T(2,128)S(1)} %copy.162, s32[128,2,64]{2,1,0:T(2,128)S(1)} %copy.163, f32[128,2,64]{2,1,0:T(2,128)S(1)} %copy.164, ...), kind=kOutput, calls=%fused_computation.24.clone.2 | convolution fusion | flops 855638016 | bytes 5259264 | tf_op jit(solution)/shard_map/while/body/eval_jaxpr/dcaj,dajp->dacp/dot_general | solution.py:49
  262.2 47.3 %fusion.142 = f32[1,128,2,16,256]{4,3,2,1,0:T(8,128)S(1)} fusion(bf16[128,16,2,64]{3,1,2,0:T(8,128)(2,1)S(1)} %copy.157, f32[128,2,64]{2,1,0:T(2,128)S(1)} %copy.159, s32[128,2,64]{2,1,0:T(2,128)S(1)} %copy.161, f32[128,2,64]{2,1,0:T(2,128)S(1)} %copy.162, s32[128,2,64]{2,1,0:T(2,128)S(1)} %copy.163, f32[128,2,64]{2,1,0:T(2,128)S(1)} %copy.164, ...), kind=kOutput, calls=%fused_computation.24.clone.2 | convolution fusion | flops 855638016 | bytes 5259264 | tf_op jit(solution)/shard_map/while/body/eval_jaxpr/dcaj,dajp->dacp/dot_general | solution.py:49
  322.9 47.3 %fusion.142 = f32[1,128,2,16,256]{4,3,2,1,0:T(8,128)S(1)} fusion(bf16[128,16,2,64]{3,1,2,0:T(8,128)(2,1)S(1)} %copy.157, f32[128,2,64]{2,1,0:T(2,128)S(1)} %copy.159, s32[128,2,64]{2,1,0:T(2,128)S(1)} %copy.161, f32[128,2,64]{2,1,0:T(2,128)S(1)} %copy.162, s32[128,2,64]{2,1,0:T(2,128)S(1)} %copy.163, f32[128,2,64]{2,1,0:T(2,128)S(1)} %copy.164, ...), kind=kOutput, calls=%fused_computation.24.clone.2 | convolution fusion | flops 855638016 | bytes 5259264 | tf_op jit(solution)/shard_map/while/body/eval_jaxpr/dcaj,dajp->dacp/dot_general | solution.py:49
  383.5 47.3 %fusion.142 = f32[1,128,2,16,256]{4,3,2,1,0:T(8,128)S(1)} fusion(bf16[128,16,2,64]{3,1,2,0:T(8,128)(2,1)S(1)} %copy.157, f32[128,2,64]{2,1,0:T(2,128)S(1)} %copy.159, s32[128,2,64]{2,1,0:T(2,128)S(1)} %copy.161, f32[128,2,64]{2,1,0:T(2,128)S(1)} %copy.162, s32[128,2,64]{2,1,0:T(2,128)S(1)} %copy.163, f32[128,2,64]{2,1,0:T(2,128)S(1)} %copy.164, ...), kind=kOutput, calls=%fused_computation.24.clone.2 | convolution fusion | flops 855638016 | bytes 5259264 | tf_op jit(solution)/shard_map/while/body/eval_jaxpr/dcaj,dajp->dacp/dot_general | solution.py:49
  437.0 10.5 all-to-all-start
  448.5 420.1 %all-to-all-done = f32[7,128,2,16,256]{4,2,3,0,1:T(2,128)} async-done(((f32[7,128,2,16,256]{4,2,3,0,1:T(2,128)}), f32[7,128,2,16,256]{4,2,3,0,1:T(2,128)}, u32[]{:S(2)}, u32[]{:S(2)}) %all-to-all-start) | async-done | bytes 29360160 | tf_op jit(solution)/shard_map/all_to_all | solution.py:73
  868.6 29.5 %fusion.26 = f32[7,16,16,256]{3,2,1,0:T(8,128)S(1)} fusion(f32[7,128,2,16,256]{4,2,3,0,1:T(2,128)} %all-to-all-done, s32[7,128,2]{1,2,0:T(2,128)S(1)} %copy.66), kind=kOutput, calls=%fused_computation.43 | convolution fusion | flops 1409343488 | bytes 31202304 | tf_op jit(solution)/shard_map/sdab,sdacp->scbp/dot_general | solution.py:61
  898.1 8.3 reshape.386
  906.4 17.7 %copy.140 = f32[7,4,4,2,8,16,16]{6,4,5,3,2,1,0:T(8,128)} copy(f32[7,4,4,2,8,16,16]{6,5,4,3,2,1,0:T(8,128)} %reshape.386) | data formatting | bytes 3670016 | tf_op jit(solution)/shard_map/reshape | solution.py:63
  924.1 10.5 fusion.120
  940.2 8.6 collective-permute-start.3
  950.0 16.0 %collective-permute-start = (f32[2,4,4,32,1]{4,3,2,1,0:T(8,128)}, f32[2,4,4,32,1]{4,3,2,1,0:T(8,128)}, u32[]{:S(2)}, u32[]{:S(2)}) collective-permute-start(f32[2,4,4,32,1]{4,3,2,1,0:T(8,128)} %get-tuple-element.155), channel_id=1, source_target_pairs={{8,0},{16,8},{24,16},{32,24},{40,32},{48,40},{56,48},{64,56},{72,6... | collective-permute-start | bytes 12296 | tf_op jit(solution)/shard_map/ppermute | solution.py:24
  983.4 6.4 collective-permute-start.6
  997.2 8.1 collective-permute-done.4
  1027.5 6.8 collective-permute-done.8
  1041.3 6.3 collective-permute-start.14
  1057.0 8.1 collective-permute-done.12
  1071.5 6.4 collective-permute-start.18
  (255 shorter events, 207.0 us)
Async XLA Ops:
  1.5 435.5 %all-to-all-start.1 = ((s32[7,128,2]{0,2,1:T(2,128)}), s32[7,128,2]{0,2,1:T(2,128)}, u32[]{:S(2)}, u32[]{:S(2)}) async-start(s32[7,128,2]{0,2,1:T(2,128)} %copy.65), calls=%async_computation.1 | async-start | bytes 262144 | tf_op jit(solution)/shard_map/all_to_all | solution.py:72
  437.0 431.6 %all-to-all-start = ((f32[7,128,2,16,256]{4,2,3,0,1:T(2,128)}), f32[7,128,2,16,256]{4,2,3,0,1:T(2,128)}, u32[]{:S(2)}, u32[]{:S(2)}) async-start(f32[7,128,2,16,256]{4,2,3,0,1:T(2,128)} %get-tuple-element.82), calls=%async_computation | async-start | bytes 58720256 | tf_op jit(solution)/shard_map/all_to_all | solution.py:73
  938.3 40.6 %collective-permute-start.2 = (f32[2,4,4,1,128]{4,3,2,1,0:T(1,128)S(1)}, f32[2,4,4,1,128]{4,3,2,1,0:T(1,128)S(1)}, u32[]{:S(2)}, u32[]{:S(2)}) collective-permute-start(f32[2,4,4,1,128]{4,3,2,1,0:T(1,128)S(1)} %get-tuple-element.157), channel_id=1, source_target_pairs={{1,0},{2,1},{3,2},{4,3},{5,4},{6,5},{7,6},{9,8},{10,9},{11,10},{12... | collective-permute-start | bytes 49160 | tf_op jit(solution)/shard_map/ppermute | solution.py:24
  940.2 38.7 %collective-permute-start.3 = (f32[2,4,4,1,128]{4,3,2,1,0:T(1,128)S(1)}, f32[2,4,4,1,128]{4,3,2,1,0:T(1,128)S(1)}, u32[]{:S(2)}, u32[]{:S(2)}) collective-permute-start(f32[2,4,4,1,128]{4,3,2,1,0:T(1,128)S(1)} %get-tuple-element.158), channel_id=1, source_target_pairs={{0,1},{1,2},{2,3},{3,4},{4,5},{5,6},{6,7},{8,9},{9,10},{10,11},{11... | collective-permute-start | bytes 49160 | tf_op jit(solution)/shard_map/ppermute | solution.py:23
  950.0 23.0 %collective-permute-start = (f32[2,4,4,32,1]{4,3,2,1,0:T(8,128)}, f32[2,4,4,32,1]{4,3,2,1,0:T(8,128)}, u32[]{:S(2)}, u32[]{:S(2)}) collective-permute-start(f32[2,4,4,32,1]{4,3,2,1,0:T(8,128)} %get-tuple-element.155), channel_id=1, source_target_pairs={{8,0},{16,8},{24,16},{32,24},{40,32},{48,40},{56,48},{64,56},{72,6... | collective-permute-start | bytes 12296 | tf_op jit(solution)/shard_map/ppermute | solution.py:24
  966.0 12.9 %collective-permute-start.1 = (f32[2,4,4,32,1]{4,3,2,1,0:T(8,128)}, f32[2,4,4,32,1]{4,3,2,1,0:T(8,128)}, u32[]{:S(2)}, u32[]{:S(2)}) collective-permute-start(f32[2,4,4,32,1]{4,3,2,1,0:T(8,128)} %get-tuple-element.156), channel_id=1, source_target_pairs={{0,8},{8,16},{16,24},{24,32},{32,40},{40,48},{48,56},{56,64},{64,7... | collective-permute-start | bytes 12296 | tf_op jit(solution)/shard_map/ppermute | solution.py:23
  983.4 22.0 %collective-permute-start.6 = (f32[2,4,4,1,128]{4,3,2,1,0:T(1,128)S(1)}, f32[2,4,4,1,128]{4,3,2,1,0:T(1,128)S(1)}, u32[]{:S(2)}, u32[]{:S(2)}) collective-permute-start(f32[2,4,4,1,128]{4,3,2,1,0:T(1,128)S(1)} %get-tuple-element.153), channel_id=1, source_target_pairs={{1,0},{2,1},{3,2},{4,3},{5,4},{6,5},{7,6},{9,8},{10,9},{11,10},{12... | collective-permute-start | bytes 49160 | tf_op jit(solution)/shard_map/ppermute | solution.py:24
  989.8 15.6 %collective-permute-start.7 = (f32[2,4,4,1,128]{4,3,2,1,0:T(1,128)S(1)}, f32[2,4,4,1,128]{4,3,2,1,0:T(1,128)S(1)}, u32[]{:S(2)}, u32[]{:S(2)}) collective-permute-start(f32[2,4,4,1,128]{4,3,2,1,0:T(1,128)S(1)} %get-tuple-element.154), channel_id=1, source_target_pairs={{0,1},{1,2},{2,3},{3,4},{4,5},{5,6},{6,7},{8,9},{9,10},{10,11},{11... | collective-permute-start | bytes 49160 | tf_op jit(solution)/shard_map/ppermute | solution.py:23
  992.9 12.5 %collective-permute-start.4 = (f32[2,4,4,32,1]{4,3,2,1,0:T(8,128)}, f32[2,4,4,32,1]{4,3,2,1,0:T(8,128)}, u32[]{:S(2)}, u32[]{:S(2)}) collective-permute-start(f32[2,4,4,32,1]{4,3,2,1,0:T(8,128)} %get-tuple-element.151), channel_id=1, source_target_pairs={{8,0},{16,8},{24,16},{32,24},{40,32},{48,40},{56,48},{64,56},{72,6... | collective-permute-start | bytes 12296 | tf_op jit(solution)/shard_map/ppermute | solution.py:24
  992.9 12.5 %collective-permute-start.5 = (f32[2,4,4,32,1]{4,3,2,1,0:T(8,128)}, f32[2,4,4,32,1]{4,3,2,1,0:T(8,128)}, u32[]{:S(2)}, u32[]{:S(2)}) collective-permute-start(f32[2,4,4,32,1]{4,3,2,1,0:T(8,128)} %get-tuple-element.152), channel_id=1, source_target_pairs={{0,8},{8,16},{16,24},{24,32},{32,40},{40,48},{48,56},{56,64},{64,7... | collective-permute-start | bytes 12296 | tf_op jit(solution)/shard_map/ppermute | solution.py:23
  1009.9 26.2 %collective-permute-start.10 = (f32[2,4,4,1,128]{4,3,2,1,0:T(1,128)S(1)}, f32[2,4,4,1,128]{4,3,2,1,0:T(1,128)S(1)}, u32[]{:S(2)}, u32[]{:S(2)}) collective-permute-start(f32[2,4,4,1,128]{4,3,2,1,0:T(1,128)S(1)} %get-tuple-element.149), channel_id=1, source_target_pairs={{1,0},{2,1},{3,2},{4,3},{5,4},{6,5},{7,6},{9,8},{10,9},{11,10},{12... | collective-permute-start | bytes 49160 | tf_op jit(solution)/shard_map/ppermute | solution.py:24
  1016.0 20.2 %collective-permute-start.11 = (f32[2,4,4,1,128]{4,3,2,1,0:T(1,128)S(1)}, f32[2,4,4,1,128]{4,3,2,1,0:T(1,128)S(1)}, u32[]{:S(2)}, u32[]{:S(2)}) collective-permute-start(f32[2,4,4,1,128]{4,3,2,1,0:T(1,128)S(1)} %get-tuple-element.150), channel_id=1, source_target_pairs={{0,1},{1,2},{2,3},{3,4},{4,5},{5,6},{6,7},{8,9},{9,10},{10,11},{11... | collective-permute-start | bytes 49160 | tf_op jit(solution)/shard_map/ppermute | solution.py:23
  1019.1 15.2 %collective-permute-start.8 = (f32[2,4,4,32,1]{4,3,2,1,0:T(8,128)}, f32[2,4,4,32,1]{4,3,2,1,0:T(8,128)}, u32[]{:S(2)}, u32[]{:S(2)}) collective-permute-start(f32[2,4,4,32,1]{4,3,2,1,0:T(8,128)} %get-tuple-element.147), channel_id=1, source_target_pairs={{8,0},{16,8},{24,16},{32,24},{40,32},{48,40},{56,48},{64,56},{72,6... | collective-permute-start | bytes 12296 | tf_op jit(solution)/shard_map/ppermute | solution.py:24
  1023.6 12.5 %collective-permute-start.9 = (f32[2,4,4,32,1]{4,3,2,1,0:T(8,128)}, f32[2,4,4,32,1]{4,3,2,1,0:T(8,128)}, u32[]{:S(2)}, u32[]{:S(2)}) collective-permute-start(f32[2,4,4,32,1]{4,3,2,1,0:T(8,128)} %get-tuple-element.148), channel_id=1, source_target_pairs={{0,8},{8,16},{16,24},{24,32},{32,40},{40,48},{48,56},{56,64},{64,7... | collective-permute-start | bytes 12296 | tf_op jit(solution)/shard_map/ppermute | solution.py:23
  1041.3 25.1 %collective-permute-start.14 = (f32[2,4,4,1,128]{4,3,2,1,0:T(1,128)}, f32[2,4,4,1,128]{4,3,2,1,0:T(1,128)}, u32[]{:S(2)}, u32[]{:S(2)}) collective-permute-start(f32[2,4,4,1,128]{4,3,2,1,0:T(1,128)} %get-tuple-element.145), channel_id=1, source_target_pairs={{1,0},{2,1},{3,2},{4,3},{5,4},{6,5},{7,6},{9,8},{10,9},{11,10},{12... | collective-permute-start | bytes 49160 | tf_op jit(solution)/shard_map/ppermute | solution.py:24
  1047.6 18.8 %collective-permute-start.15 = (f32[2,4,4,1,128]{4,3,2,1,0:T(1,128)}, f32[2,4,4,1,128]{4,3,2,1,0:T(1,128)}, u32[]{:S(2)}, u32[]{:S(2)}) collective-permute-start(f32[2,4,4,1,128]{4,3,2,1,0:T(1,128)} %get-tuple-element.146), channel_id=1, source_target_pairs={{0,1},{1,2},{2,3},{3,4},{4,5},{5,6},{6,7},{8,9},{9,10},{10,11},{11... | collective-permute-start | bytes 49160 | tf_op jit(solution)/shard_map/ppermute | solution.py:23
  1050.7 14.4 %collective-permute-start.12 = (f32[2,4,4,32,1]{4,3,2,1,0:T(8,128)}, f32[2,4,4,32,1]{4,3,2,1,0:T(8,128)}, u32[]{:S(2)}, u32[]{:S(2)}) collective-permute-start(f32[2,4,4,32,1]{4,3,2,1,0:T(8,128)} %get-tuple-element.143), channel_id=1, source_target_pairs={{8,0},{16,8},{24,16},{32,24},{40,32},{48,40},{56,48},{64,56},{72,6... | collective-permute-start | bytes 12296 | tf_op jit(solution)/shard_map/ppermute | solution.py:24
  1053.7 12.7 %collective-permute-start.13 = (f32[2,4,4,32,1]{4,3,2,1,0:T(8,128)}, f32[2,4,4,32,1]{4,3,2,1,0:T(8,128)}, u32[]{:S(2)}, u32[]{:S(2)}) collective-permute-start(f32[2,4,4,32,1]{4,3,2,1,0:T(8,128)} %get-tuple-element.144), channel_id=1, source_target_pairs={{0,8},{8,16},{16,24},{24,32},{32,40},{40,48},{48,56},{56,64},{64,7... | collective-permute-start | bytes 12296 | tf_op jit(solution)/shard_map/ppermute | solution.py:23
  1071.5 24.7 %collective-permute-start.18 = (f32[2,4,4,1,128]{4,3,2,1,0:T(1,128)}, f32[2,4,4,1,128]{4,3,2,1,0:T(1,128)}, u32[]{:S(2)}, u32[]{:S(2)}) collective-permute-start(f32[2,4,4,1,128]{4,3,2,1,0:T(1,128)} %get-tuple-element.141), channel_id=1, source_target_pairs={{1,0},{2,1},{3,2},{4,3},{5,4},{6,5},{7,6},{9,8},{10,9},{11,10},{12... | collective-permute-start | bytes 49160 | tf_op jit(solution)/shard_map/ppermute | solution.py:24
  1077.9 18.4 %collective-permute-start.19 = (f32[2,4,4,1,128]{4,3,2,1,0:T(1,128)}, f32[2,4,4,1,128]{4,3,2,1,0:T(1,128)}, u32[]{:S(2)}, u32[]{:S(2)}) collective-permute-start(f32[2,4,4,1,128]{4,3,2,1,0:T(1,128)} %get-tuple-element.142), channel_id=1, source_target_pairs={{0,1},{1,2},{2,3},{3,4},{4,5},{5,6},{6,7},{8,9},{9,10},{10,11},{11... | collective-permute-start | bytes 49160 | tf_op jit(solution)/shard_map/ppermute | solution.py:23
  1081.0 12.9 %collective-permute-start.16 = (f32[2,4,4,32,1]{4,3,2,1,0:T(8,128)}, f32[2,4,4,32,1]{4,3,2,1,0:T(8,128)}, u32[]{:S(2)}, u32[]{:S(2)}) collective-permute-start(f32[2,4,4,32,1]{4,3,2,1,0:T(8,128)} %get-tuple-element.139), channel_id=1, source_target_pairs={{8,0},{16,8},{24,16},{32,24},{40,32},{48,40},{56,48},{64,56},{72,6... | collective-permute-start | bytes 12296 | tf_op jit(solution)/shard_map/ppermute | solution.py:24
  1083.7 12.5 %collective-permute-start.17 = (f32[2,4,4,32,1]{4,3,2,1,0:T(8,128)}, f32[2,4,4,32,1]{4,3,2,1,0:T(8,128)}, u32[]{:S(2)}, u32[]{:S(2)}) collective-permute-start(f32[2,4,4,32,1]{4,3,2,1,0:T(8,128)} %get-tuple-element.140), channel_id=1, source_target_pairs={{0,8},{8,16},{16,24},{24,32},{32,40},{40,48},{48,56},{56,64},{64,7... | collective-permute-start | bytes 12296 | tf_op jit(solution)/shard_map/ppermute | solution.py:23
  1100.0 12.4 %collective-permute-start.20 = (f32[2,4,4,32,1]{4,3,2,1,0:T(8,128)S(1)}, f32[2,4,4,32,1]{4,3,2,1,0:T(8,128)S(1)}, u32[]{:S(2)}, u32[]{:S(2)}) collective-permute-start(f32[2,4,4,32,1]{4,3,2,1,0:T(8,128)S(1)} %get-tuple-element.135), channel_id=1, source_target_pairs={{8,0},{16,8},{24,16},{32,24},{40,32},{48,40},{56,48},{64,56},{72,6... | collective-permute-start | bytes 12296 | tf_op jit(solution)/shard_map/ppermute | solution.py:24
  1103.2 12.4 %collective-permute-start.21 = (f32[2,4,4,32,1]{4,3,2,1,0:T(8,128)S(1)}, f32[2,4,4,32,1]{4,3,2,1,0:T(8,128)S(1)}, u32[]{:S(2)}, u32[]{:S(2)}) collective-permute-start(f32[2,4,4,32,1]{4,3,2,1,0:T(8,128)S(1)} %get-tuple-element.136), channel_id=1, source_target_pairs={{0,8},{8,16},{16,24},{24,32},{32,40},{40,48},{48,56},{56,64},{64,7... | collective-permute-start | bytes 12296 | tf_op jit(solution)/shard_map/ppermute | solution.py:23
  (6 other events, 1015.4 us)
where the time goes:
time: 1130 us; the launch traced here: 1120 us
  waiting for transfers between devices  470 us (42%)
  matrix products  368 us (33%)
  local copies, waits for them, and re-layouts  153 us (14%)
  starting transfers between devices  103 us (9%)
  other arithmetic  24.8 us (2%)
    all_to_all x1, waiting for transfers between devices, shards(): lax.all_to_all(own_tiles, ('lon', 'lat'), split_axis=1, concat_axis=1, ti...  420 us
    dot_general x7, matrix products, build_tiles(): return jnp.einsum('dcaj,dajp->dacp', innov_f32, weight, precision=HIGHEST)  331 us
    ppermute x12, starting transfers between devices, with_halo(): after = lax.ppermute(leading, axis, down)  62.3 us
    dynamic_update_slice x7, local copies, waits for them, and re-layouts, shards(): lax.map(build_slot, (innovations, fractions, cell_index, counts))  43.1 us
    ppermute x12, waiting for transfers between devices, with_halo(): after = lax.ppermute(leading, axis, down)  32.9 us
    dynamic_slice x56, local copies, waits for them, and re-layouts, shards(): lax.map(build_slot, (innovations, fractions, cell_index, counts))  30.1 us
    dot_general x1, matrix products, place_tiles(): jnp.einsum('sdab,sdacp->scbp', onehot, tile_sets, precision=HIGHEST)  29.5 us
    reshape x2, local copies, waits for them, and re-layouts, place_tiles(): summed.reshape(slot_total, VARS, LEV, block_rows, block_cols, TILE, TILE)  26 us
  transfers between devices with their start and end apart: 26, of which 14 were waited for; matrix products, arithmetic and copies ran while one was open for 40% of the time, Pallas kernels for 0%

commit v1 on v0

v1 whole, which is shorter than its diff:
```python
import functools

import jax
import jax.numpy as jnp
from jax import lax
from jax.experimental import pallas as pl
from jax.experimental.pallas import tpu as pltpu
from jax.sharding import PartitionSpec as P

VARS = 4
LEV = 4
CH = 16
TILE = 16
LANES = 128
KAPPA = 0.125
AXES = ("lon", "lat")
F32 = jnp.float32
BF16 = jnp.bfloat16


def offsets_of(widths):
    starts, total = [], 0
    for width in widths:
        starts.append(total)
        total += width
    return starts, total


def pack_rows(slots):
    used = slots * (CH + 3) + 1
    return used, -(-used // 8) * 8


def build_payload(innovations, fractions, cell_index, counts, blocks):
    slots, targets, channels, width = innovations.shape
    tiles = counts.shape[2]
    per_tile = width // tiles
    lane = lax.broadcasted_iota(jnp.int32, (1, 1, width), 2)
    first = lane < per_tile
    count_lane = jnp.where(first, counts[:, :, 0:1], counts[:, :, 1:2])
    block_lane = jnp.where(first, blocks[:, :, 0:1], blocks[:, :, 1:2])
    is_live = (lane & (per_tile - 1)) < count_lane
    values = jnp.where(is_live[:, :, None, :], innovations, jnp.zeros((), BF16))
    row = cell_index >> 4
    column = cell_index & 15
    skewed = (row >> 3) * LANES + ((row + block_lane) & 7) * TILE + column
    used, rows = pack_rows(slots)
    spots = jnp.transpose(blocks, (1, 0, 2)).reshape(targets, 1, slots * tiles)
    spots = jnp.pad(spots, ((0, 0), (0, rows - used), (0, LANES - slots * tiles)))
    return jnp.concatenate(
        [
            jnp.transpose(values, (1, 0, 2, 3)).reshape(targets, slots * channels, width),
            jnp.transpose(fractions, (1, 0, 2, 3)).reshape(targets, slots * 2, width),
            jnp.transpose(skewed, (1, 0, 2)).astype(BF16),
            spots.astype(BF16),
        ],
        axis=1,
    )


def scatter_kernel(slots, batch, widths, blocks_ref, got_ref, out_ref, *rest):
    if widths:
        top_ref, bottom_ref, acc_ref, place_ref, below_ref = rest
    else:
        acc_ref, place_ref, below_ref = rest
    step = pl.program_id(0)
    rows_out = out_ref.shape[1]

    @pl.when(step == 0)
    def _():
        acc_ref[...] = jnp.zeros_like(acc_ref)
        place_ref[...] = lax.broadcasted_iota(jnp.int32, place_ref.shape, 0).astype(F32).astype(BF16)

    first = lax.broadcasted_iota(jnp.int32, (1, LANES), 1) < LANES // 2
    first_mask = jnp.where(first, 1.0, 0.0).astype(BF16)
    second_mask = jnp.where(first, 0.0, 1.0).astype(BF16)
    base = slots * CH

    def one(index, carry):
        sender = step * batch + index
        aux = got_ref[index, pl.ds(base, 3 * slots), :].astype(F32)
        for slot in range(slots):
            value = got_ref[index, pl.ds(slot * CH, CH), :].astype(F32)
            frac_y = aux[2 * slot : 2 * slot + 1, :]
            frac_x = aux[2 * slot + 1 : 2 * slot + 2, :]
            cell = aux[2 * slots + slot : 2 * slots + slot + 1, :].astype(BF16)
            by_x = value * frac_x
            by_y = value * frac_y
            both = jnp.concatenate([value, by_x, by_y, by_x * frac_y], axis=0)
            high = both.astype(BF16)
            low = (both - high.astype(F32)).astype(BF16)
            wide = jnp.concatenate([high, low], axis=1)
            mask_a = jnp.concatenate([first_mask, first_mask], axis=1)
            mask_b = jnp.concatenate([second_mask, second_mask], axis=1)
            left = jnp.concatenate([wide * mask_a, wide * mask_b], axis=0)
            onehot = jnp.where(place_ref[...] == cell, jnp.ones((), BF16), jnp.zeros((), BF16))
            right = jnp.concatenate([onehot, onehot], axis=1)
            sums = lax.dot_general(left, right, (((1,), (1,)), ((), ())), preferred_element_type=F32)
            spot = (sender * slots + slot) * 2
            acc_ref[slot, blocks_ref[spot]] += sums[: 4 * CH]
            acc_ref[slot, blocks_ref[spot + 1]] += sums[4 * CH :]
        return carry

    lax.fori_loop(0, batch, one, 0)

    @pl.when(step == pl.num_programs(0) - 1)
    def _():
        group = lax.broadcasted_iota(jnp.int32, (CH, LANES), 1) >> 4

        def part(number, carry):
            slot = number >> 2
            band = (number >> 1) & 1
            half = number & 1
            straight = [jnp.zeros((CH, LANES), F32)] * 8
            under = [jnp.zeros((CH, LANES), F32)] * 8
            for column in range(8):
                tile = acc_ref[slot, band * 8 + column, :, pl.ds(pl.multiple_of(half * LANES, LANES), LANES)]
                a_0, a_x = tile[:CH], tile[CH : 2 * CH]
                a_y, a_xy = tile[2 * CH : 3 * CH], tile[3 * CH :]
                here = a_0 - a_x - a_y + a_xy + pltpu.roll(a_x - a_xy, 1, 1)
                next_row = a_y - a_xy + pltpu.roll(a_xy, 1, 1)
                for y in range(8):
                    hit = group == ((y + column) & 7)
                    straight[y] = jnp.where(hit, here, straight[y])
                    under[y] = jnp.where(hit, next_row, under[y])
            for y in range(8):
                turn = (-16 * y) % LANES
                row = band * 16 + half * 8 + y
                out_ref[slot, row] = pltpu.roll(straight[y], turn, 1) if turn else straight[y]
                below_ref[slot, row] = pltpu.roll(under[y], turn, 1) if turn else under[y]
            return carry

        lax.fori_loop(0, 4 * slots, part, 0)

        def shift(slot, carry):
            out_ref[slot, 1:] += below_ref[slot, : rows_out - 1]
            return carry

        lax.fori_loop(0, slots, shift, 0)
        if widths:
            starts, _ = offsets_of(widths)
            for slot, (start, width) in enumerate(zip(starts, widths)):
                top_ref[start : start + width] = out_ref[slot, :width]
                bottom_ref[start : start + width] = out_ref[slot, rows_out - width :]


def scatter(got, slots, widths, rows_out):
    senders, rows, _ = got.shape
    base = slots * (CH + 3)
    blocks = got[:, base, : 2 * slots].astype(jnp.int32).reshape(-1)
    batch = 8
    _, total = offsets_of(widths)
    whole = lambda shape: pl.BlockSpec(shape, lambda i, b: (0,) * len(shape))
    shapes = [(slots, rows_out, CH, LANES)] + ([(total, CH, LANES)] * 2 if widths else [])
    return pl.pallas_call(
        functools.partial(scatter_kernel, slots, batch, widths),
        grid_spec=pltpu.PrefetchScalarGridSpec(
            num_scalar_prefetch=1,
            grid=(senders // batch,),
            in_specs=[pl.BlockSpec((batch, rows, LANES), lambda i, b: (i, 0, 0))],
            out_specs=[whole(s) for s in shapes],
            scratch_shapes=[
                pltpu.VMEM((slots, 16, 4 * CH, 2 * LANES), F32),
                pltpu.VMEM((2 * LANES, LANES), BF16),
                pltpu.VMEM((slots, rows_out, CH, LANES), F32),
            ],
        ),
        out_shape=[jax.ShapeDtypeStruct(s, F32) for s in shapes],
        name="scatter",
    )(blocks, got)


GROUPS = 4
SPAN = LANES // GROUPS


def lane_pack_kernel(widths, halo, forcing_ref, above_ref, below_ref, left_ref, right_ref, tall_ref):
    rows_own = forcing_ref.shape[1]
    per_group = left_ref.shape[0]
    starts, _ = offsets_of(widths)
    tall_ref[...] = jnp.zeros_like(tall_ref)
    for slot, (start, width) in enumerate(zip(starts, widths)):
        tall_ref[slot, halo - width : halo] = above_ref[start : start + width]
        tall_ref[slot, halo : halo + rows_own] = forcing_ref[slot]
        tall_ref[slot, halo + rows_own : halo + rows_own + width] = below_ref[start : start + width]
    lane = lax.broadcasted_iota(jnp.int32, (CH, LANES), 1)

    def one(row, carry):
        to_left = jnp.zeros((CH, LANES), F32)
        to_right = jnp.zeros((CH, LANES), F32)
        for group in range(GROUPS):
            for slot, (start, width) in enumerate(zip(starts, widths)):
                source = tall_ref[slot, group * per_group + row]
                begin = group * SPAN + start
                hit = (lane >= begin) & (lane < begin + width)
                to_left = jnp.where(hit, pltpu.roll(source, begin, 1) if begin else source, to_left)
                to_right = jnp.where(hit, pltpu.roll(source, (begin + width) % LANES, 1), to_right)
        left_ref[row] = to_left
        right_ref[row] = to_right
        return carry

    lax.fori_loop(0, per_group, one, 0)


def lane_pack(forcing, above, below, widths, halo):
    tall = forcing.shape[1] + 2 * halo
    shape = jax.ShapeDtypeStruct((tall // GROUPS, CH, LANES), F32)
    slots = len(widths)
    return pl.pallas_call(
        functools.partial(lane_pack_kernel, widths, halo),
        grid=(1,),
        in_specs=[
            pl.BlockSpec((slots,) + forcing.shape[1:], lambda i: (0, 0, 0, 0)),
            pl.BlockSpec(above.shape, lambda i: (0, 0, 0)),
            pl.BlockSpec(below.shape, lambda i: (0, 0, 0)),
        ],
        out_specs=[pl.BlockSpec(shape.shape, lambda i: (0, 0, 0))] * 2,
        out_shape=[shape, shape],
        scratch_shapes=[pltpu.VMEM((slots, tall, CH, LANES), F32)],
        name="lane_pack",
    )(forcing, above, below)


def march_kernel(
    widths, halo, edge_ref, forcing_ref, above_ref, below_ref, west_ref, east_ref, u_ref, v_ref, mix_ref, out_ref,
    field_ref, extra_ref, turn_ref,
):
    rows_own = forcing_ref.shape[1]
    tall = rows_own + 2 * halo
    per_group = west_ref.shape[0]
    starts, _ = offsets_of(widths)
    lane = lax.broadcasted_iota(jnp.int32, (CH, LANES), 1)
    main = pl.ds(0, LANES)
    side = pl.ds(LANES, LANES)

    for slot, (start, width) in enumerate(zip(starts, widths)):
        lo, hi = halo - width, halo + rows_own + width
        extra_ref[slot, lo:halo, :, main] = above_ref[start : start + width]
        extra_ref[slot, halo : halo + rows_own, :, main] = forcing_ref[slot]
        extra_ref[slot, halo + rows_own : hi, :, main] = below_ref[start : start + width]

    def edges(row, carry):
        west = west_ref[row]
        east = east_ref[row]
        for group in range(GROUPS):
            for slot, (start, width) in enumerate(zip(starts, widths)):
                begin = group * SPAN + start
                east_turn = (-begin) % LANES
                value = jnp.where(lane < width, pltpu.roll(east, east_turn, 1) if east_turn else east, 0.0)
                west_turn = (LANES - width - begin) % LANES
                value = jnp.where(
                    lane >= LANES - width, pltpu.roll(west, west_turn, 1) if west_turn else west, value
                )
                extra_ref[slot, group * per_group + row, :, side] = value
        return carry

    lax.fori_loop(0, per_group, edges, 0)

    first_row = jnp.where(edge_ref[0] == 1, halo, 0)
    last_row = jnp.where(edge_ref[1] == 1, halo + rows_own, tall)
    turns = [jnp.broadcast_to(mix_ref[:, d : d + 1], (CH, LANES)) for d in range(CH)]
    turn_ref[0] = jnp.zeros((CH, LANES), F32)

    slots = len(widths)
    for number in range(slots):
        reach = widths[number]
        source = extra_ref.at[0] if number == 0 else field_ref.at[number % 2]
        target = field_ref.at[(number + 1) % 2]
        begin, end = halo - reach, halo + rows_own + reach
        last = number == slots - 1
        tiles = 1 if last else 2

        def one(row, carry, source=source, target=target, last=last, number=number):
            done_before, flux_two, flux_one = carry
            inside = (row >= first_row) & (row < last_row)
            mixed = []
            for tile in (main, side):
                total = jnp.zeros((CH, LANES), F32)
                for d in range(CH):
                    total = total + turns[d] * jnp.broadcast_to(source[row, d : d + 1, tile], (CH, LANES))
                mixed.append(jnp.where(inside, total, 0.0))
            mixed = jnp.concatenate(mixed, axis=1)
            u_half = jnp.concatenate([u_ref[row]] * 2, axis=0) * 0.5
            v_half = jnp.concatenate([v_ref[row]] * 2, axis=0) * 0.5
            own = (1.0 - 4.0 * KAPPA) * mixed
            own = own + pltpu.roll((KAPPA + u_half) * mixed, 2 * LANES - 1, 1)
            own = own + pltpu.roll((KAPPA - u_half) * mixed, 1, 1)
            up = (KAPPA + v_half) * mixed
            down = (KAPPA - v_half) * mixed
            result = done_before + up + flux_two
            before = jnp.maximum(row - 1, 0)
            if last:
                turn_ref[jnp.clip(row - 1 - halo, 0, rows_own - 1)] = (
                    result[:, :LANES] + forcing_ref[slots, jnp.clip(row - 1 - halo, 0, rows_own - 1)]
                )
            else:
                target[before] = result + extra_ref[number + 1, before]
            return own, flux_one, down

        zero = jnp.concatenate([turn_ref[0], turn_ref[0]], axis=1)
        lax.fori_loop(begin, end, one, (zero, zero, zero))

    for channel in range(CH):
        out_ref[channel] = turn_ref[:, channel, :]


def march(edge, forcing, above, below, west, east, u_tall, v_tall, mix, widths, halo):
    rows_own = forcing.shape[1]
    tall = rows_own + 2 * halo
    slots = len(widths)
    vmem = pl.BlockSpec(memory_space=pltpu.VMEM)
    return pl.pallas_call(
        functools.partial(march_kernel, widths, halo),
        in_specs=[pl.BlockSpec(memory_space=pltpu.SMEM)] + [vmem] * 8,
        out_specs=vmem,
        out_shape=jax.ShapeDtypeStruct((CH, rows_own, LANES), F32),
        scratch_shapes=[
            pltpu.VMEM((2, tall, CH, 2 * LANES), F32),
            pltpu.VMEM((slots, tall, CH, 2 * LANES), F32),
            pltpu.VMEM((rows_own, CH, LANES), F32),
        ],
        name="march",
    )(edge, forcing, above, below, west, east, u_tall, v_tall, mix)


def ring(axis, wrap):
    count = lax.axis_size(axis)
    up = [(i, (i + 1) % count) for i in range(count if wrap else count - 1)]
    return up, [(j, i) for i, j in up]


def wind_tables(u_wind, v_wind, halo):
    both = jnp.stack([u_wind, v_wind])
    for axis, dim, wrap in (("lat", 2, False), ("lon", 3, True)):
        up, down = ring(axis, wrap)
        length = both.shape[dim]
        before = lax.ppermute(lax.slice_in_dim(both, length - halo, length, axis=dim), axis, up)
        after = lax.ppermute(lax.slice_in_dim(both, 0, halo, axis=dim), axis, down)
        if dim == 2:
            both = jnp.concatenate([before, both, after], axis=dim)
        else:
            gap = jnp.zeros(both.shape[:3] + (LANES - 2 * halo,), F32)
            both = jnp.concatenate([both, after, gap, before], axis=dim)
    both = jnp.transpose(both, (0, 2, 1, 3))
    return jnp.concatenate([both, both], axis=2)


def shards(innovations, fractions, cell_index, counts, blocks, u_wind, v_wind, channel_mix):
    slots = innovations.shape[0]
    rows_own = u_wind.shape[1]
    halo = slots - 1
    order = slice(None, None, -1)
    payload = build_payload(innovations[order], fractions[order], cell_index[order], counts[order], blocks[order])
    got = lax.all_to_all(payload, AXES, split_axis=0, concat_axis=0, tiled=True)
    winds = wind_tables(u_wind, v_wind, halo)
    widths = tuple(range(halo, 0, -1))
    forcing, top, bottom = scatter(got, slots, widths, rows_own)
    up, down = ring("lat", False)
    above = lax.ppermute(bottom, "lat", up)
    below = lax.ppermute(top, "lat", down)
    to_left, to_right = lane_pack(forcing, above, below, widths, halo)
    up, down = ring("lon", True)
    west = lax.ppermute(to_right, "lon", up)
    east = lax.ppermute(to_left, "lon", down)
    lat_index = lax.axis_index("lat")
    edge = jnp.stack([lat_index == 0, lat_index == lax.axis_size("lat") - 1]).astype(jnp.int32)
    field = march(edge, forcing, above, below, west, east, winds[0], winds[1], channel_mix.T, widths, halo)
    return field.reshape(VARS, LEV, rows_own, u_wind.shape[2])


def solution(mesh):
    in_specs = (
        P(None, ("lon", "lat"), None, None),
        P(None, ("lon", "lat"), None, None),
        P(None, ("lon", "lat"), None),
        P(None, ("lon", "lat"), None),
        P(None, ("lon", "lat"), None),
        P(None, "lat", "lon"),
        P(None, "lat", "lon"),
        P(),
    )
    out_specs = P(None, None, "lat", "lon")
    return jax.shard_map(shards, mesh=mesh, in_specs=in_specs, out_specs=out_specs, check_vma=False)
```

time: 1130 us -> 209 us (0.18)
  waiting for transfers between devices: 470 us -> 47.7 us
  matrix products: 368 us -> 0 us
  local copies, waits for them, and re-layouts: 153 us -> 8.12 us
  Pallas kernels: 0 us -> 104 us
  starting transfers between devices: 103 us -> 36.2 us
  other arithmetic: 24.8 us -> 10.4 us
    all_to_all x2 -> x1, waiting for transfers between devices: 420 us -> 0.01 us  [shards(): got = lax.all_to_all(payload, AXES, split_axis=0, concat_axis=0, tiled=True)]
    dot_general x14 -> x0, matrix products: 368 us -> none  [the longest x7 331 us: build_tiles(): return jnp.einsum('dcaj,dajp->dacp', innov_f32, weight, precision=HIGHEST)]
    pallas_call x0 -> x3, Pallas kernels: none -> 104 us  [the longest x1 71 us: scatter(): pl.pallas_call(functools.partial(scatter_kernel, slots, batch, widths), g...]
    ppermute x24 -> x8, starting transfers between devices: 81.5 us -> 25.3 us  [the longest x2 9.98 us: wind_tables(): after = lax.ppermute(lax.slice_in_dim(both, 0, halo, axis=dim), axis, down)]
    dynamic_update_slice x7 -> x0, local copies, waits for them, and re-layouts: 43.1 us -> none  [shards(): lax.map(build_slot, (innovations, fractions, cell_index, counts))]
    reshape x9 -> x3, local copies, waits for them, and re-layouts: 37.4 us -> 0.47 us  [the longest x1 0.31 us: build_payload(): jnp.transpose(fractions, (1, 0, 2, 3)).reshape(targets, slots * 2, width)]
    dynamic_slice x56 -> x0, local copies, waits for them, and re-layouts: 30.1 us -> none  [shards(): lax.map(build_slot, (innovations, fractions, cell_index, counts))]
    squeeze x6 -> x0, local copies, waits for them, and re-layouts: 19.1 us -> none  [shards(): forcing[later]]
  transfers between devices with their start and end apart: 26 -> 9, of which waited for: 14 -> 5; matrix products, arithmetic and copies ran while one was open for 40% -> 2% of each run, Pallas kernels for 0% -> 34%
where the time goes in v1:
time: 209 us; the launch traced here: 207 us
  Pallas kernels  104 us (50%)
  waiting for transfers between devices  47.7 us (23%)
  starting transfers between devices  36.2 us (17%)
  other arithmetic  10.4 us (5%)
  local copies, waits for them, and re-layouts  8.12 us (4%)
    pallas_call x1, Pallas kernels, scatter(): pl.pallas_call(functools.partial(scatter_kernel, slots, batch, widths), g...  71 us
    ppermute x2, waiting for transfers between devices, wind_tables(): after = lax.ppermute(lax.slice_in_dim(both, 0, halo, axis=dim), axis, down)  41.2 us
    pallas_call x1, Pallas kernels, march(): pl.pallas_call(functools.partial(march_kernel, widths, halo), in_specs=[p...  29.1 us
    all_to_all x1, starting transfers between devices, shards(): got = lax.all_to_all(payload, AXES, split_axis=0, concat_axis=0, tiled=True)  10.9 us
    ppermute x2, starting transfers between devices, wind_tables(): after = lax.ppermute(lax.slice_in_dim(both, 0, halo, axis=dim), axis, down)  9.98 us
    ppermute x1, starting transfers between devices, shards(): below = lax.ppermute(top, 'lat', down)  6.03 us
    ppermute x1, starting transfers between devices, shards(): east = lax.ppermute(to_left, 'lon', down)  5.36 us
    unnamed x23, local copies, waits for them, and re-layouts  4.38 us
  transfers between devices with their start and end apart: 9, of which 5 were waited for; matrix products, arithmetic and copies ran while one was open for 2% of the time, Pallas kernels for 34%

profile of v1, /device:TPU:2, one launch (start us, length us, event | category | flops | bytes accessed | tf_op | source)
XLA Modules:
  0.0 206.9 jit_solution(12390061100888288104)
XLA Ops:
  0.0 0.7 fusion.7
  0.7 0.8 fusion.10
  1.7 1.3 copy.46
  3.4 1.1 copy.45
  5.6 3.3 %select_bitcast_fusion = bf16[128,7,16,128]{3,2,0,1:T(8,128)(2,1)S(1)} fusion(bf16[7,128,16,128]{3,2,1,0:T(8,128)(2,1)} %param.8, pred[7,128,128]{2,1,0:T(8,128)(4,1)S(1)} %copy.43), kind=kLoop, calls=%fused_computation.3 | loop fusion | flops 1835008 | bytes 7454720 | tf_op jit(solution)/shard_map/transpose | solution.py:52
  9.9 2.7 %fusion.1 = bf16[128,136,128]{2,1,0:T(8,128)(2,1)} fusion(bf16[128,1,14]{2,1,0:T(2,128)(2,1)S(1)} %copy.51, bf16[128,7,128]{2,1,0:T(8,128)(2,1)S(1)} %fusion.5, bf16[128,14,128]{2,1,0:T(8,128)(2,1)S(1)} %copy.52, bf16[128,112,128]{2,1,0:T(8,128)(2,1)S(1)} %bitcast.30), kind=kLoop, calls=%fused_computation.2 | loop fusion | flops 22282240 | bytes 8818176 | tf_op jit(solution)/shard_map/concatenate | solution.py:50
  12.6 10.9 %all-to-all-start = ((bf16[128,136,128]{2,1,0:T(8,128)(2,1)}), bf16[128,136,128]{2,1,0:T(8,128)(2,1)}, u32[]{:S(2)}, u32[]{:S(2)}) async-start(bf16[128,136,128]{2,1,0:T(8,128)(2,1)} %fusion.1), calls=%async_computation | async-start | bytes 8912896 | tf_op jit(solution)/shard_map/all_to_all | solution.py:354
  23.6 4.6 %collective-permute-start.5 = (f32[2,4,6,128]{3,1,2,0:T(4,128)S(1)}, f32[2,4,6,128]{3,1,2,0:T(4,128)S(1)}, u32[]{:S(2)}, u32[]{:S(2)}) collective-permute-start(f32[2,4,6,128]{3,1,2,0:T(4,128)S(1)} %get-tuple-element.20), channel_id=1, source_target_pairs={{1,0},{2,1},{3,2},{4,3},{5,4},{6,5},{7,6},{9,8},{10,9},{11,10},{12... | collective-permute-start | bytes 73736 | tf_op jit(solution)/shard_map/ppermute | solution.py:338
  28.3 1.9 collective-permute-start.4
  31.6 41.2 %collective-permute-done.5 = f32[2,4,6,128]{3,1,2,0:T(4,128)S(1)} collective-permute-done((f32[2,4,6,128]{3,1,2,0:T(4,128)S(1)}, f32[2,4,6,128]{3,1,2,0:T(4,128)S(1)}, u32[]{:S(2)}, u32[]{:S(2)}) %collective-permute-start.5) | collective-permute-done | bytes 24608 | tf_op jit(solution)/shard_map/ppermute | solution.py:338
  72.8 2.0 collective-permute-done.4
  75.1 5.3 %collective-permute-start.6 = (f32[2,4,44,6]{3,1,2,0:T(4,128)S(1)}, f32[2,4,44,6]{3,1,2,0:T(4,128)S(1)}, u32[]{:S(2)}, u32[]{:S(2)}) collective-permute-start(f32[2,4,44,6]{3,1,2,0:T(4,128)S(1)} %get-tuple-element.17), channel_id=1, source_target_pairs={{8,0},{16,8},{24,16},{32,24},{40,32},{48,40},{56,48},{64,56},{72,6... | collective-permute-start | bytes 25352 | tf_op jit(solution)/shard_map/ppermute | solution.py:338
  80.4 1.2 fusion.6
  81.6 0.7 reshape.33.blocks_ref
  82.4 71.0 %scatter.1 = (f32[7,32,16,128]{3,2,1,0:T(8,128)}, f32[21,16,128]{2,1,0:T(8,128)}, f32[21,16,128]{2,1,0:T(8,128)}) custom-call(s32[1792]{0:T(1024)} %reshape.33.blocks_ref, bf16[128,136,128]{2,1,0:T(8,128)(2,1)} %all-to-all-done.got_ref), custom_call_target="tpu_custom_call" | custom-call | tf_op jit(solution)/shard_map/scatter/pallas_call | solution.py:155
  153.4 1.9 collective-permute-start
  155.3 6.0 %collective-permute-start.1 = (f32[21,16,128]{2,1,0:T(8,128)}, f32[21,16,128]{2,1,0:T(8,128)S(1)}, u32[]{:S(2)}, u32[]{:S(2)}) collective-permute-start(f32[21,16,128]{2,1,0:T(8,128)} %get-tuple-element.12), channel_id=1, source_target_pairs={{1,0},{2,1},{3,2},{4,3},{5,4},{6,5},{7,6},{9,8},{10,9},{11,10},{12... | collective-permute-start | bytes 516104 | tf_op jit(solution)/shard_map/ppermute | solution.py:360
  161.5 1.5 collective-permute-done.above_ref
  163.0 1.6 collective-permute-done.1.below_ref
  165.2 4.2 %lane_pack.1 = (f32[11,16,128]{2,1,0:T(8,128)}, f32[11,16,128]{2,1,0:T(8,128)}) custom-call(f32[7,32,16,128]{3,2,1,0:T(8,128)} %get-tuple-element.10.forcing_ref, f32[21,16,128]{2,1,0:T(8,128)} %copy-done, f32[21,16,128]{2,1,0:T(8,128)} %copy-done.1), custom_call_target="tpu_custom_call" | custom-call | tf_op jit(solution)/shard_map/lane_pack/pallas_call | solution.py:209
  169.4 5.4 %collective-permute-start.3 = (f32[11,16,128]{2,1,0:T(8,128)}, f32[11,16,128]{2,1,0:T(8,128)S(1)}, u32[]{:S(2)}, u32[]{:S(2)}) collective-permute-start(f32[11,16,128]{2,1,0:T(8,128)} %get-tuple-element.14), channel_id=1, source_target_pairs={{8,0},{16,8},{24,16},{32,24},{40,32},{48,40},{56,48},{64,56},{72,6... | collective-permute-start | bytes 270344 | tf_op jit(solution)/shard_map/ppermute | solution.py:364
  174.8 1.0 fusion.4
  175.8 1.4 collective-permute-done.2.west_ref
  177.8 29.1 %march.1 = f32[16,32,128]{2,1,0:T(8,128)} custom-call(s32[2]{0:T(128)} %add_convert_fusion.1.edge_ref, f32[7,32,16,128]{3,2,1,0:T(8,128)} %get-tuple-element.10.forcing_ref, f32[21,16,128]{2,1,0:T(8,128)} %copy-done, f32[21,16,128]{2,1,0:T(8,128)} %copy-done.1, f32[11,16,128]{2,1,0:T(8,128)} %copy-done.2, f32[11,16,128]{2,1,0:T(8,128)} %copy-done.3, ...), custom_call_target="tpu_custom_call" | custom-call | tf_op jit(solution)/shard_map/march/pallas_call | solution.py:312
  (55 shorter events, 5.8 us)
Async XLA Ops:
  0.0 4.9 %copy-start.7 = (s32[7,128,2]{1,2,0:T(2,128)S(1)}, s32[7,128,2]{1,2,0:T(2,128)}, u32[]{:S(2)}) copy-start(s32[7,128,2]{1,2,0:T(2,128)} %param.11) | copy-start | bytes 21508
  12.6 10.9 %copy-start.4 = (f32[4,32,128]{2,1,0:T(8,128)S(1)}, f32[4,32,128]{2,1,0:T(8,128)}, u32[]{:S(2)}) copy-start(f32[4,32,128]{2,1,0:T(8,128)} %param.14) | copy-start | bytes 196612
  12.6 11.0 %copy-start.5 = (f32[4,32,128]{2,1,0:T(8,128)S(1)}, f32[4,32,128]{2,1,0:T(8,128)}, u32[]{:S(2)}) copy-start(f32[4,32,128]{2,1,0:T(8,128)} %param.13) | copy-start | bytes 196612
  12.6 18.3 %copy-start.6 = (f32[16,16]{1,0:T(8,128)S(1)}, f32[16,16]{1,0:T(8,128)}, u32[]{:S(2)}) copy-start(f32[16,16]{1,0:T(8,128)} %param.15) | copy-start | bytes 3076
  12.6 67.9 %all-to-all-start = ((bf16[128,136,128]{2,1,0:T(8,128)(2,1)}), bf16[128,136,128]{2,1,0:T(8,128)(2,1)}, u32[]{:S(2)}, u32[]{:S(2)}) async-start(bf16[128,136,128]{2,1,0:T(8,128)(2,1)} %fusion.1), calls=%async_computation | async-start | bytes 8912896 | tf_op jit(solution)/shard_map/all_to_all | solution.py:354
  23.6 49.1 %collective-permute-start.5 = (f32[2,4,6,128]{3,1,2,0:T(4,128)S(1)}, f32[2,4,6,128]{3,1,2,0:T(4,128)S(1)}, u32[]{:S(2)}, u32[]{:S(2)}) collective-permute-start(f32[2,4,6,128]{3,1,2,0:T(4,128)S(1)} %get-tuple-element.20), channel_id=1, source_target_pairs={{1,0},{2,1},{3,2},{4,3},{5,4},{6,5},{7,6},{9,8},{10,9},{11,10},{12... | collective-permute-start | bytes 73736 | tf_op jit(solution)/shard_map/ppermute | solution.py:338
  28.3 46.5 %collective-permute-start.4 = (f32[2,4,6,128]{3,1,2,0:T(4,128)S(1)}, f32[2,4,6,128]{3,1,2,0:T(4,128)S(1)}, u32[]{:S(2)}, u32[]{:S(2)}) collective-permute-start(f32[2,4,6,128]{3,1,2,0:T(4,128)S(1)} %get-tuple-element.19), channel_id=1, source_target_pairs={{0,1},{1,2},{2,3},{3,4},{4,5},{5,6},{6,7},{8,9},{9,10},{10,11},{11... | collective-permute-start | bytes 73736 | tf_op jit(solution)/shard_map/ppermute | solution.py:337
  75.0 86.3 %collective-permute-start.7 = (f32[2,4,44,6]{3,1,2,0:T(4,128)S(1)}, f32[2,4,44,6]{3,1,2,0:T(4,128)S(1)}, u32[]{:S(2)}, u32[]{:S(2)}) collective-permute-start(f32[2,4,44,6]{3,1,2,0:T(4,128)S(1)} %get-tuple-element.18), channel_id=1, source_target_pairs={{0,8},{8,16},{16,24},{24,32},{32,40},{40,48},{48,56},{56,64},{64,7... | collective-permute-start | bytes 25352 | tf_op jit(solution)/shard_map/ppermute | solution.py:337
  75.1 86.3 %collective-permute-start.6 = (f32[2,4,44,6]{3,1,2,0:T(4,128)S(1)}, f32[2,4,44,6]{3,1,2,0:T(4,128)S(1)}, u32[]{:S(2)}, u32[]{:S(2)}) collective-permute-start(f32[2,4,44,6]{3,1,2,0:T(4,128)S(1)} %get-tuple-element.17), channel_id=1, source_target_pairs={{8,0},{16,8},{24,16},{32,24},{40,32},{48,40},{56,48},{64,56},{72,6... | collective-permute-start | bytes 25352 | tf_op jit(solution)/shard_map/ppermute | solution.py:338
  153.4 9.6 %collective-permute-start = (f32[21,16,128]{2,1,0:T(8,128)}, f32[21,16,128]{2,1,0:T(8,128)S(1)}, u32[]{:S(2)}, u32[]{:S(2)}) collective-permute-start(f32[21,16,128]{2,1,0:T(8,128)} %get-tuple-element.11), channel_id=1, source_target_pairs={{0,1},{1,2},{2,3},{3,4},{4,5},{5,6},{6,7},{8,9},{9,10},{10,11},{11... | collective-permute-start | bytes 516104 | tf_op jit(solution)/shard_map/ppermute | solution.py:359
  155.3 9.3 %collective-permute-start.1 = (f32[21,16,128]{2,1,0:T(8,128)}, f32[21,16,128]{2,1,0:T(8,128)S(1)}, u32[]{:S(2)}, u32[]{:S(2)}) collective-permute-start(f32[21,16,128]{2,1,0:T(8,128)} %get-tuple-element.12), channel_id=1, source_target_pairs={{1,0},{2,1},{3,2},{4,3},{5,4},{6,5},{7,6},{9,8},{10,9},{11,10},{12... | collective-permute-start | bytes 516104 | tf_op jit(solution)/shard_map/ppermute | solution.py:360
  163.0 1.6 copy-start
  164.6 0.7 copy-start.1
  169.4 7.8 %collective-permute-start.2 = (f32[11,16,128]{2,1,0:T(8,128)}, f32[11,16,128]{2,1,0:T(8,128)S(1)}, u32[]{:S(2)}, u32[]{:S(2)}) collective-permute-start(f32[11,16,128]{2,1,0:T(8,128)} %get-tuple-element.13), channel_id=1, source_target_pairs={{0,8},{8,16},{16,24},{24,32},{32,40},{40,48},{48,56},{56,64},{64,7... | collective-permute-start | bytes 270344 | tf_op jit(solution)/shard_map/ppermute | solution.py:363
  169.4 7.8 %collective-permute-start.3 = (f32[11,16,128]{2,1,0:T(8,128)}, f32[11,16,128]{2,1,0:T(8,128)S(1)}, u32[]{:S(2)}, u32[]{:S(2)}) collective-permute-start(f32[11,16,128]{2,1,0:T(8,128)} %get-tuple-element.14), channel_id=1, source_target_pairs={{8,0},{16,8},{24,16},{32,24},{40,32},{48,40},{56,48},{64,56},{72,6... | collective-permute-start | bytes 270344 | tf_op jit(solution)/shard_map/ppermute | solution.py:364
  177.2 0.6 copy-start.2
  177.2 0.6 copy-start.3

commit v2 on v0

v2 whole, which is shorter than its diff:
```python
import functools

import jax
import jax.numpy as jnp
from jax import lax
from jax.experimental import pallas as pl
from jax.experimental.pallas import tpu as pltpu
from jax.sharding import PartitionSpec as P


VARS = 4
LEV = 4
CH = 16
TILE = 16
LANES = 128
KAPPA = 0.125
AXES = ("lon", "lat")
F32 = jnp.float32
BF16 = jnp.bfloat16
CHUNK_A = 4


def offsets_of(widths):
    starts, total = [], 0
    for width in widths:
        starts.append(total)
        total += width
    return starts, total


def pack_rows(slots):
    used = slots * (CH + 3) + 1
    return used, -(-used // 8) * 8


def build_payload(innovations, fractions, cell_index, counts, blocks):
    slots, targets, channels, width = innovations.shape
    tiles = counts.shape[2]
    per_tile = width // tiles
    lane = lax.broadcasted_iota(jnp.int32, (1, 1, width), 2)
    first = lane < per_tile
    count_lane = jnp.where(first, counts[:, :, 0:1], counts[:, :, 1:2])
    block_lane = jnp.where(first, blocks[:, :, 0:1], blocks[:, :, 1:2])
    is_live = (lane & (per_tile - 1)) < count_lane
    values = jnp.where(is_live[:, :, None, :], innovations, jnp.zeros((), BF16))
    row = cell_index >> 4
    column = cell_index & 15
    skewed = (row >> 3) * LANES + ((row + block_lane) & 7) * TILE + column
    used, rows = pack_rows(slots)
    spots = jnp.transpose(blocks, (1, 0, 2)).reshape(targets, 1, slots * tiles)
    spots = jnp.pad(spots, ((0, 0), (0, rows - used), (0, LANES - slots * tiles)))
    return jnp.concatenate(
        [
            jnp.transpose(values, (1, 0, 2, 3)).reshape(targets, slots * channels, width),
            jnp.transpose(fractions, (1, 0, 2, 3)).reshape(targets, slots * 2, width),
            jnp.transpose(skewed, (1, 0, 2)).astype(BF16),
            spots.astype(BF16),
        ],
        axis=1,
    )


def scatter_kernel(slots, batch, widths, early, blocks_ref, got_ref, *rest):
    if widths:
        before_ref, wind_ref, out_ref, left_ref, right_ref, top_ref, bottom_ref = rest[:7]
        rest = rest[7:]
    else:
        out_ref, rest = rest[0], rest[1:]
    below_ref, acc_refs = rest[0], rest[1:]
    step = pl.program_id(0)
    rows_out = out_ref.shape[1]
    base = slots * CH
    tail = got_ref.shape[1] - base

    @pl.when(step == 0)
    def _():
        for acc_ref in acc_refs:
            acc_ref[...] = jnp.zeros_like(acc_ref)

    first = lax.broadcasted_iota(jnp.int32, (CH, LANES), 1) < LANES // 2
    mask_a = jnp.where(first, 1.0, 0.0).astype(BF16)
    mask_b = jnp.where(first, 0.0, 1.0).astype(BF16)
    sixteen = lax.broadcasted_iota(jnp.int32, (TILE, LANES), 0).astype(F32).astype(BF16)
    one_bf, zero_bf = jnp.ones((), BF16), jnp.zeros((), BF16)
    nothing = jnp.zeros((CH, LANES), BF16)

    def one(index, carry):
        sender = step * batch + index
        aux = got_ref[index, pl.ds(base, tail), :].astype(F32)
        major = jnp.floor(aux * (1.0 / TILE))
        minor = aux - TILE * major
        for slot in range(slots):
            value = got_ref[index, pl.ds(slot * CH, CH), :].astype(F32)
            spot = 2 * slots + slot
            by_x = value * aux[2 * slot + 1 : 2 * slot + 2, :]
            frac_y = aux[2 * slot : 2 * slot + 1, :]
            highs, lows = [value.astype(BF16)], [nothing]
            for part in (by_x, value * frac_y, by_x * frac_y):
                high = part.astype(BF16)
                highs.append(high)
                lows.append((part - high.astype(F32)).astype(BF16))
            left = jnp.concatenate(
                [
                    jnp.concatenate([h * m for m in (mask_a, mask_b) for h in highs], axis=0),
                    jnp.concatenate([h * m for m in (mask_a, mask_b) for h in lows], axis=0),
                ],
                axis=1,
            )
            unit = jnp.where(
                sixteen == jnp.broadcast_to(minor[spot : spot + 1], (TILE, LANES)).astype(BF16), one_bf, zero_bf
            )
            group = jnp.broadcast_to(major[spot : spot + 1], (TILE, LANES)).astype(BF16)
            onehot = jnp.concatenate(
                [jnp.where(group == jnp.asarray(k, BF16), unit, zero_bf) for k in range(TILE)], axis=0
            )
            right = jnp.concatenate([onehot, onehot], axis=1)
            sums = lax.dot_general(left, right, (((1,), (1,)), ((), ())), preferred_element_type=F32)
            acc_refs[slot][blocks_ref[sender, 2 * slot]] += sums[: 4 * CH]
            acc_refs[slot][blocks_ref[sender, 2 * slot + 1]] += sums[4 * CH :]
        return carry

    lax.fori_loop(0, batch, one, 0, unroll=4)

    @pl.when(step == pl.num_programs(0) - 1)
    def _():
        lane_group = lax.broadcasted_iota(jnp.int32, (CH, LANES), 1) >> 4
        for slot in range(slots):
            acc_ref = acc_refs[slot]

            def part(number, carry, slot=slot, acc_ref=acc_ref):
                band = number >> 1
                half = number & 1
                straight = [jnp.zeros((CH, LANES), F32)] * 8
                under = [jnp.zeros((CH, LANES), F32)] * 8
                for column in range(8):
                    tile = acc_ref[band * 8 + column, :, pl.ds(pl.multiple_of(half * LANES, LANES), LANES)]
                    a_0, a_x = tile[:CH], tile[CH : 2 * CH]
                    a_y, a_xy = tile[2 * CH : 3 * CH], tile[3 * CH :]
                    x_only, y_only = a_x - a_xy, a_y - a_xy
                    here = a_0 - a_x - y_only + pltpu.roll(x_only, 1, 1)
                    next_row = y_only + pltpu.roll(a_xy, 1, 1)
                    for y in range(8):
                        hit = lane_group == ((y + column) & 7)
                        straight[y] = jnp.where(hit, here, straight[y])
                        under[y] = jnp.where(hit, next_row, under[y])
                for y in range(8):
                    turn = (-16 * y) % LANES
                    row = band * 16 + half * 8 + y
                    out_ref[slot, row] = pltpu.roll(straight[y], turn, 1) if turn else straight[y]
                    below_ref[row] = pltpu.roll(under[y], turn, 1) if turn else under[y]
                return carry

            lax.fori_loop(0, 4, part, 0)
            out_ref[slot, 1:] += below_ref[: rows_out - 1]

        if widths:
            sources = [before_ref.at[k] for k in range(early)]
            sources += [out_ref.at[k] for k in range(len(widths) - 1 - early)] + [wind_ref]
            starts, _ = offsets_of(widths)
            for source, start, width in zip(sources, starts, widths):
                top_ref[start : start + width] = source[:width]
                bottom_ref[start : start + width] = source[rows_out - width :]
            lane = lax.broadcasted_iota(jnp.int32, (CH, LANES), 1)
            per_group = rows_out // GROUPS

            def pack(row, carry):
                to_left = jnp.zeros((CH, LANES), F32)
                to_right = jnp.zeros((CH, LANES), F32)
                for group in range(GROUPS):
                    for source, start, width in zip(sources, starts, widths):
                        value = source[group * per_group + row]
                        begin = group * SPAN + start
                        hit = (lane >= begin) & (lane < begin + width)
                        to_left = jnp.where(hit, pltpu.roll(value, begin, 1) if begin else value, to_left)
                        turn = (begin + width) % LANES
                        to_right = jnp.where(hit, pltpu.roll(value, turn, 1) if turn else value, to_right)
                left_ref[row] = to_left
                right_ref[row] = to_right
                return carry

            lax.fori_loop(0, per_group, pack, 0)


GROUPS = 4
SPAN = LANES // GROUPS


def scatter(got, slots, rows_out, widths=(), before=None, wind=None):
    senders, rows, _ = got.shape
    base = slots * (CH + 3)
    blocks = got[:, base, : 2 * slots].astype(jnp.int32)
    batch = 8
    _, total = offsets_of(widths)

    def whole(shape):
        return pl.BlockSpec(shape, lambda i, b: (0,) * len(shape))

    shapes = [(slots, rows_out, CH, LANES)]
    extra = []
    if widths:
        shapes += [(rows_out // GROUPS, CH, LANES)] * 2 + [(total, CH, LANES)] * 2
        extra = [before, wind]
    return pl.pallas_call(
        functools.partial(scatter_kernel, slots, batch, widths, 0 if before is None else before.shape[0]),
        grid_spec=pltpu.PrefetchScalarGridSpec(
            num_scalar_prefetch=1,
            grid=(senders // batch,),
            in_specs=[pl.BlockSpec((batch, rows, LANES), lambda i, b: (i, 0, 0))] + [whole(e.shape) for e in extra],
            out_specs=[whole(s) for s in shapes],
            scratch_shapes=[pltpu.VMEM((rows_out, CH, LANES), F32)]
            + [pltpu.VMEM((16, 4 * CH, 2 * LANES), F32)] * slots,
        ),
        out_shape=[jax.ShapeDtypeStruct(s, F32) for s in shapes],
        name="scatter",
    )(blocks, got, *extra)


def march_kernel(
    widths, halo, early, edge_ref, first_ref, second_ref, wind_ref, above_ref, below_ref, west_ref, east_ref, mix_ref,
    out_ref, field_ref, extra_ref, mixed_ref, turn_ref,
):
    rows_own = first_ref.shape[1]
    tall = rows_own + 2 * halo
    per_group = west_ref.shape[0]
    starts, total = offsets_of(widths)
    lane = lax.broadcasted_iota(jnp.int32, (CH, LANES), 1)
    main = pl.ds(0, LANES)
    side = pl.ds(LANES, LANES)
    steps = len(widths) - 1
    sources = [first_ref.at[k] for k in range(early)]
    sources += [second_ref.at[k] for k in range(steps - early)] + [wind_ref]

    for slot, (start, width) in enumerate(zip(starts, widths)):
        lo, hi = halo - width, halo + rows_own + width
        extra_ref[slot, hi : hi + 2] = jnp.zeros((2, CH, 2 * LANES), F32)
        extra_ref[slot, lo:halo, :, main] = above_ref[start : start + width]
        extra_ref[slot, halo : halo + rows_own, :, main] = sources[slot][...]
        extra_ref[slot, halo + rows_own : hi, :, main] = below_ref[start : start + width]

    def edge(west, east, group, start, width):
        begin = group * SPAN + start
        turn = (-begin) % LANES
        value = jnp.where(lane < width, pltpu.roll(east, turn, 1) if turn else east, 0.0)
        turn = (LANES - width - begin) % LANES
        return jnp.where(lane >= LANES - width, pltpu.roll(west, turn, 1) if turn else west, value)

    def edges(row, carry):
        west, east = west_ref[row], east_ref[row]
        for group in range(GROUPS):
            for slot, (start, width) in enumerate(zip(starts, widths)):
                extra_ref[slot, halo + group * per_group + row, :, side] = edge(west, east, group, start, width)
        return carry

    lax.fori_loop(0, per_group, edges, 0)
    for slot, (start, width) in enumerate(zip(starts, widths)):
        for i in range(width):
            spot = per_group - width + i
            extra_ref[slot, halo - width + i, :, side] = edge(
                above_ref[total + spot], above_ref[total + per_group + spot], GROUPS - 1, start, width
            )
            extra_ref[slot, halo + rows_own + i, :, side] = edge(
                below_ref[total + i], below_ref[total + per_group + i], 0, start, width
            )

    extra_ref[0, tall:] = jnp.zeros((extra_ref.shape[1] - tall, CH, 2 * LANES), F32)
    field_ref[...] = jnp.zeros_like(field_ref)
    mixed_ref[tall:] = jnp.zeros((mixed_ref.shape[0] - tall, CH, 2 * LANES), F32)
    matrix = mix_ref[...]
    wind = extra_ref.at[steps]
    half = CH // 2

    def mix(source, begin, count):
        for number in range(count):
            rows = pl.ds(begin + 8 * number, 8)
            field = source[rows].reshape(8 * CH, 2 * LANES)
            high = field.astype(BF16)
            low = (field - high.astype(F32)).astype(BF16)
            product = lax.dot_general(
                matrix, jnp.concatenate([high, high, low], axis=0), (((1,), (0,)), ((), ())),
                preferred_element_type=F32,
            )
            mixed_ref[rows] = product.reshape(8, CH, 2 * LANES)

    def twice(value):
        return jnp.concatenate([value, value], axis=0)

    for number in range(steps):
        reach = widths[number]
        source = extra_ref.at[0] if number == 0 else field_ref.at[number % 2]
        target = field_ref.at[(number + 1) % 2]
        begin, end = halo - reach, halo + rows_own + reach
        last = number == steps - 1
        mix(source, begin, -(-(end - begin) // 8))

        def pair(index, carry, target=target, begin=begin, last=last, number=number):
            for offset in range(4):
                row = begin + 1 + 4 * index + offset
                mixed = mixed_ref[row]
                u_half = twice(wind[row, :half]) * 0.5
                result = (1.0 - 4.0 * KAPPA) * mixed
                result = result + pltpu.roll((KAPPA + u_half) * mixed, 2 * LANES - 1, 1)
                result = result + pltpu.roll((KAPPA - u_half) * mixed, 1, 1)
                result = result + (KAPPA + 0.5 * twice(wind[row + 1, half:])) * mixed_ref[row + 1]
                result = result + (KAPPA - 0.5 * twice(wind[row - 1, half:])) * mixed_ref[row - 1]
                if last:
                    turn_ref[row - halo] = result[:, :LANES] + second_ref[steps - early, row - halo]
                else:
                    target[row] = result + extra_ref[number + 1, row]
            return carry

        lax.fori_loop(0, -(-(end - begin - 2) // 4), pair, 0)
        if not last:

            @pl.when(edge_ref[0] == 1)
            def _(target=target):
                target[:halo] = jnp.zeros((halo, CH, 2 * LANES), F32)

            @pl.when(edge_ref[1] == 1)
            def _(target=target):
                target[halo + rows_own : tall] = jnp.zeros((halo, CH, 2 * LANES), F32)

    for channel in range(CH):
        out_ref[channel] = turn_ref[:, channel, :]


def march(edge, first, second, wind, above, below, west, east, mix, widths, halo):
    rows_own = first.shape[1]
    tall = rows_own + 2 * halo
    vmem = pl.BlockSpec(memory_space=pltpu.VMEM)
    return pl.pallas_call(
        functools.partial(march_kernel, widths, halo, first.shape[0]),
        in_specs=[pl.BlockSpec(memory_space=pltpu.SMEM)] + [vmem] * 8,
        out_specs=vmem,
        out_shape=jax.ShapeDtypeStruct((CH, rows_own, LANES), F32),
        scratch_shapes=[
            pltpu.VMEM((2, tall + 8, CH, 2 * LANES), F32),
            pltpu.VMEM((len(widths), tall + 8, CH, 2 * LANES), F32),
            pltpu.VMEM((tall + 8, CH, 2 * LANES), F32),
            pltpu.VMEM((rows_own, CH, LANES), F32),
        ],
        name="march",
    )(edge, first, second, wind, above, below, west, east, mix)


def mix_matrix(channel_mix):
    rounded = lax.reduce_precision(channel_mix.T, 8, 7)
    high = rounded.astype(BF16)
    low = (channel_mix.T - rounded).astype(BF16)
    eye = jnp.eye(8, dtype=BF16)
    return jnp.concatenate([jnp.kron(eye, high), jnp.kron(eye, low), jnp.kron(eye, high)], axis=1)


def ring(axis, wrap):
    count = lax.axis_size(axis)
    up = [(i, (i + 1) % count) for i in range(count if wrap else count - 1)]
    return up, [(j, i) for i, j in up]


def program(innovations, fractions, cell_index, counts, blocks, u_wind, v_wind, channel_mix):
    slots = innovations.shape[0]
    rows_own = u_wind.shape[1]
    halo = slots - 1
    widths = tuple(range(halo, 0, -1)) + (halo,)
    early = CHUNK_A
    got = []
    for low, high in ((slots - early, slots), (0, slots - early)):
        parts = [x[low:high][::-1] for x in (innovations, fractions, cell_index, counts, blocks)]
        payload = build_payload(*parts)
        got.append(lax.all_to_all(payload, AXES, split_axis=0, concat_axis=0, tiled=True))
    u_rows, v_rows = jnp.transpose(u_wind, (1, 0, 2)), jnp.transpose(v_wind, (1, 0, 2))
    wind = jnp.concatenate([u_rows, u_rows, v_rows, v_rows], axis=1)
    (first,) = scatter(got[0], early, rows_own)
    second, to_left, to_right, top, bottom = scatter(got[1], slots - early, rows_own, widths, first, wind)
    up, down = ring("lon", True)
    west = lax.ppermute(to_right, "lon", up)
    east = lax.ppermute(to_left, "lon", down)
    up, down = ring("lat", False)
    above = lax.ppermute(jnp.concatenate([bottom, west, east]), "lat", up)
    below = lax.ppermute(jnp.concatenate([top, west, east]), "lat", down)
    lat_index = lax.axis_index("lat")
    edge = jnp.stack([lat_index == 0, lat_index == lax.axis_size("lat") - 1]).astype(jnp.int32)
    field = march(edge, first, second, wind, above, below, west, east, mix_matrix(channel_mix), widths, halo)
    return field.reshape(VARS, LEV, rows_own, u_wind.shape[2])


def solution(mesh):
    in_specs = (
        P(None, ("lon", "lat"), None, None),
        P(None, ("lon", "lat"), None, None),
        P(None, ("lon", "lat"), None),
        P(None, ("lon", "lat"), None),
        P(None, ("lon", "lat"), None),
        P(None, "lat", "lon"),
        P(None, "lat", "lon"),
        P(),
    )
    out_specs = P(None, None, "lat", "lon")
    return jax.shard_map(program, mesh=mesh, in_specs=in_specs, out_specs=out_specs, check_vma=False)
```

time: 1130 us -> 193 us (0.17)
  waiting for transfers between devices: 470 us -> 53.8 us
  matrix products: 368 us -> 0 us
  local copies, waits for them, and re-layouts: 153 us -> 13.7 us
  Pallas kernels: 0 us -> 76.8 us
  starting transfers between devices: 103 us -> 30.8 us
    all_to_all x2, waiting for transfers between devices: 420 us -> 45.9 us  [program(): lax.all_to_all(payload, AXES, split_axis=0, concat_axis=0, tiled=True)]
    dot_general x14 -> x0, matrix products: 368 us -> none  [the longest x7 331 us: build_tiles(): return jnp.einsum('dcaj,dajp->dacp', innov_f32, weight, precision=HIGHEST)]
    pallas_call x0 -> x3, Pallas kernels: none -> 76.8 us  [the longest x2 63.9 us: scatter(): pl.pallas_call(functools.partial(scatter_kernel, slots, batch, widths, 0...]
    ppermute x24 -> x4, starting transfers between devices: 81.5 us -> 13.3 us  [the longest x1 5.62 us: program(): below = lax.ppermute(jnp.concatenate([top, west, east]), 'lat', down)]
    dynamic_update_slice x7 -> x0, local copies, waits for them, and re-layouts: 43.1 us -> none  [shards(): lax.map(build_slot, (innovations, fractions, cell_index, counts))]
    ppermute x24 -> x4, waiting for transfers between devices: 49.5 us -> 7.91 us  [the longest x1 4.47 us: program(): above = lax.ppermute(jnp.concatenate([bottom, west, east]), 'lat', up)]
    reshape x9 -> x4, local copies, waits for them, and re-layouts: 37.4 us -> 0.43 us  [the longest x3 0.29 us: build_payload(): spots = jnp.transpose(blocks, (1, 0, 2)).reshape(targets, 1, slots * tiles)]
    dynamic_slice x56 -> x0, local copies, waits for them, and re-layouts: 30.1 us -> none  [shards(): lax.map(build_slot, (innovations, fractions, cell_index, counts))]
  transfers between devices with their start and end apart: 26 -> 6, of which waited for: 14 -> 5; matrix products, arithmetic and copies ran while one was open for 40% -> 9% of each run, Pallas kernels for 0% -> 0%
where the time goes in v2:
time: 193 us; the launch traced here: 191 us
  Pallas kernels  76.8 us (40%)
  waiting for transfers between devices  53.8 us (28%)
  starting transfers between devices  30.8 us (16%)
  other arithmetic  15.1 us (8%)
  local copies, waits for them, and re-layouts  13.7 us (7%)
    pallas_call x2, Pallas kernels, scatter(): pl.pallas_call(functools.partial(scatter_kernel, slots, batch, widths, 0...  63.9 us
    all_to_all x2, waiting for transfers between devices, program(): lax.all_to_all(payload, AXES, split_axis=0, concat_axis=0, tiled=True)  45.9 us
    all_to_all x2, starting transfers between devices, program(): lax.all_to_all(payload, AXES, split_axis=0, concat_axis=0, tiled=True)  17.4 us
    pallas_call x1, Pallas kernels, march(): pl.pallas_call(functools.partial(march_kernel, widths, halo, first.shape[...  12.9 us
    ppermute x1, starting transfers between devices, program(): below = lax.ppermute(jnp.concatenate([top, west, east]), 'lat', down)  5.62 us
    concatenate x2, other arithmetic, build_payload(): jnp.concatenate([jnp.transpose(values, (1, 0, 2, 3)).reshape(targets, slo...  4.96 us
    ppermute x1, starting transfers between devices, program(): east = lax.ppermute(to_left, 'lon', down)  4.91 us
    ppermute x1, waiting for transfers between devices, program(): above = lax.ppermute(jnp.concatenate([bottom, west, east]), 'lat', up)  4.47 us
  transfers between devices with their start and end apart: 6, of which 5 were waited for; matrix products, arithmetic and copies ran while one was open for 9% of the time, Pallas kernels for 0%

profile of v2, /device:TPU:2, one launch (start us, length us, event | category | flops | bytes accessed | tf_op | source)
XLA Modules:
  0.0 190.5 jit_solution(15958279084545730422)
XLA Ops:
  0.0 0.8 fusion.10
  0.8 0.8 fusion.9
  4.9 2.0 %fusion.3 = bf16[128,64,128]{2,1,0:T(8,128)(2,1)} fusion(bf16[128,1,6]{2,1,0:T(2,128)(2,1)S(1)} %copy.75, bf16[128,3,128]{2,1,0:T(4,128)(2,1)S(1)} %fusion.5, bf16[128,6,128]{2,1,0:T(8,128)(2,1)S(1)} %copy.76, bf16[128,48,128]{2,1,0:T(8,128)(2,1)S(1)} %bitcast.48), kind=kLoop, calls=%fused_computation.5 | loop fusion | flops 10485760 | bytes 3966464 | tf_op jit(solution)/shard_map/concatenate | solution.py:52
  6.9 10.5 %all-to-all-start.1 = ((bf16[128,64,128]{2,1,0:T(8,128)(2,1)}), bf16[128,64,128]{2,1,0:T(8,128)(2,1)S(1)}, u32[]{:S(2)}, u32[]{:S(2)}) async-start(bf16[128,64,128]{2,1,0:T(8,128)(2,1)} %fusion.3), calls=%async_computation.1 | async-start | bytes 4194304 | tf_op jit(solution)/shard_map/all_to_all | solution.py:369
  17.5 3.3 %slice.92 = bf16[4,128,16,128]{3,2,1,0:T(8,128)(2,1)} slice(bf16[7,128,16,128]{3,2,1,0:T(8,128)(2,1)} %param.8), slice={[3:7], [0:128], [0:16], [0:128]} | slice | bytes 4194304 | tf_op jit(solution)/shard_map/slice | solution.py:367
  21.4 2.3 %select_bitcast_fusion = bf16[128,4,16,128]{3,2,0,1:T(8,128)(2,1)S(1)} fusion(bf16[4,128,16,128]{3,2,1,0:T(8,128)(2,1)} %slice.92, pred[4,128,128]{2,1,0:T(8,128)(4,1)S(1)} %copy.57), kind=kLoop, calls=%fused_computation.6 | loop fusion | flops 1048576 | bytes 4259840 | tf_op jit(solution)/shard_map/transpose | solution.py:54
  23.8 2.0 %copy.58 = bf16[128,4,16,128]{3,2,1,0:T(8,128)(2,1)} copy(bf16[128,4,16,128]{3,2,0,1:T(8,128)(2,1)S(1)} %select_bitcast_fusion) | data formatting | bytes 4194304 | tf_op jit(solution)/shard_map/transpose | solution.py:54
  27.4 2.9 %fusion.2 = bf16[128,80,128]{2,1,0:T(8,128)(2,1)} fusion(bf16[128,1,8]{2,1,0:T(2,128)(2,1)S(1)} %copy.64, bf16[128,4,128]{2,1,0:T(4,128)(2,1)S(1)} %fusion.4, bf16[128,8,128]{2,1,0:T(8,128)(2,1)S(1)} %bitcast.49, bf16[128,64,128]{2,1,0:T(8,128)(2,1)} %bitcast.47), kind=kLoop, calls=%fused_computation.4 | loop fusion | flops 13107200 | bytes 5113856 | tf_op jit(solution)/shard_map/concatenate | solution.py:52
  30.4 15.0 %all-to-all-done.1.got_ref = bf16[128,64,128]{2,1,0:T(8,128)(2,1)S(1)} async-done(((bf16[128,64,128]{2,1,0:T(8,128)(2,1)}), bf16[128,64,128]{2,1,0:T(8,128)(2,1)S(1)}, u32[]{:S(2)}, u32[]{:S(2)}) %all-to-all-start.1) | async-done | bytes 2097184 | tf_op jit(solution)/shard_map/all_to_all | solution.py:369
  45.4 1.3 copy-done.1
  46.7 6.9 %all-to-all-start = ((bf16[128,80,128]{2,1,0:T(8,128)(2,1)}), bf16[128,80,128]{2,1,0:T(8,128)(2,1)S(1)}, u32[]{:S(2)}, u32[]{:S(2)}) async-start(bf16[128,80,128]{2,1,0:T(8,128)(2,1)} %fusion.2), calls=%async_computation | async-start | bytes 5242880 | tf_op jit(solution)/shard_map/all_to_all | solution.py:369
  54.7 1.7 slice_convert_fusion
  56.4 30.9 %all-to-all-done.got_ref = bf16[128,80,128]{2,1,0:T(8,128)(2,1)S(1)} async-done(((bf16[128,80,128]{2,1,0:T(8,128)(2,1)}), bf16[128,80,128]{2,1,0:T(8,128)(2,1)S(1)}, u32[]{:S(2)}, u32[]{:S(2)}) %all-to-all-start) | async-done | bytes 2621472 | tf_op jit(solution)/shard_map/all_to_all | solution.py:369
  87.3 0.9 slice_convert_fusion.1
  88.8 34.1 %scatter.2.rest_0_.first_ref = f32[4,32,16,128]{3,2,1,0:T(8,128)} custom-call(s32[128,8]{1,0:T(8,128)} %bitcast.51, bf16[128,80,128]{2,1,0:T(8,128)(2,1)} %copy-done), custom_call_target="tpu_custom_call" | custom-call | tf_op jit(solution)/shard_map/scatter/pallas_call | solution.py:203
  122.8 29.9 %scatter.3 = (f32[3,32,16,128]{3,2,1,0:T(8,128)}, f32[8,16,128]{2,1,0:T(8,128)}, f32[8,16,128]{2,1,0:T(8,128)}, f32[27,16,128]{2,1,0:T(8,128)}, f32[27,16,128]{2,1,0:T(8,128)}) custom-call(s32[128,6]{1,0:T(8,128)} %bitcast.54, bf16[128,64,128]{2,1,0:T(8,128)(2,1)} %copy-done.1, f32[4,32,16,128]{3,2,1,0:T(8,128)} %scatter.2.rest_0_.first_ref, ...), custom_call_target="tpu_custom_call" | custom-call | tf_op jit(solution)/shard_map/scatter/pallas_call | solution.py:203
  153.2 4.9 %collective-permute-start.1 = (f32[8,16,128]{2,1,0:T(8,128)}, f32[8,16,128]{2,1,0:T(8,128)S(1)}, u32[]{:S(2)}, u32[]{:S(2)}) collective-permute-start(f32[8,16,128]{2,1,0:T(8,128)} %get-tuple-element.13), channel_id=1, source_target_pairs={{8,0},{16,8},{24,16},{32,24},{40,32},{48,40},{56,48},{64,56},{72,6... | collective-permute-start | bytes 196616 | tf_op jit(solution)/shard_map/ppermute | solution.py:376
  158.1 2.3 %collective-permute-done.west_ref = f32[8,16,128]{2,1,0:T(8,128)S(1)} collective-permute-done((f32[8,16,128]{2,1,0:T(8,128)}, f32[8,16,128]{2,1,0:T(8,128)S(1)}, u32[]{:S(2)}, u32[]{:S(2)}) %collective-permute-start) | collective-permute-done | bytes 65568 | tf_op jit(solution)/shard_map/ppermute | solution.py:375
  160.4 1.1 pad_maximum_fusion
  161.5 2.3 %collective-permute-start.2 = (f32[43,16,128]{2,1,0:T(8,128)S(1)}, f32[43,16,128]{2,1,0:T(8,128)S(1)}, u32[]{:S(2)}, u32[]{:S(2)}) collective-permute-start(f32[43,16,128]{2,1,0:T(8,128)S(1)} %get-tuple-element.16), channel_id=1, source_target_pairs={{0,1},{1,2},{2,3},{3,4},{4,5},{5,6},{6,7},{8,9},{9,10},{10,11},{11... | collective-permute-start | bytes 1056776 | tf_op jit(solution)/shard_map/ppermute | solution.py:378
  163.8 5.6 %collective-permute-start.3 = (f32[43,16,128]{2,1,0:T(8,128)S(1)}, f32[43,16,128]{2,1,0:T(8,128)S(1)}, u32[]{:S(2)}, u32[]{:S(2)}) collective-permute-start(f32[43,16,128]{2,1,0:T(8,128)S(1)} %get-tuple-element.15), channel_id=1, source_target_pairs={{1,0},{2,1},{3,2},{4,3},{5,4},{6,5},{7,6},{9,8},{10,9},{11,10},{12... | collective-permute-start | bytes 1056776 | tf_op jit(solution)/shard_map/ppermute | solution.py:379
  171.3 4.5 %collective-permute-done.2.above_ref = f32[43,16,128]{2,1,0:T(8,128)S(1)} collective-permute-done((f32[43,16,128]{2,1,0:T(8,128)S(1)}, f32[43,16,128]{2,1,0:T(8,128)S(1)}, u32[]{:S(2)}, u32[]{:S(2)}) %collective-permute-start.2) | collective-permute-done | bytes 352288 | tf_op jit(solution)/shard_map/ppermute | solution.py:378
  175.7 1.2 collective-permute-done.3.below_ref
  177.6 12.9 %march.1 = f32[16,32,128]{2,1,0:T(8,128)} custom-call(s32[2]{0:T(128)} %add_convert_fusion.2.edge_ref, f32[4,32,16,128]{3,2,1,0:T(8,128)} %scatter.2.rest_0_.first_ref, f32[3,32,16,128]{3,2,1,0:T(8,128)} %get-tuple-element.10.second_ref, f32[32,16,128]{2,1,0:T(8,128)} %pad_maximum_fusion.4.rest_1_.wind_ref, f32[43,16,128]{2,1,0:T(8,128)} %copy-done.2, ...), custom_call_target="tpu_custom_call" | custom-call | tf_op jit(solution)/shard_map/march/pallas_call | solution.py:330
  (90 shorter events, 10.0 us)
Async XLA Ops:
  0.0 2.2 %slice-start = ((bf16[7,128,16,128]{3,2,1,0:T(8,128)(2,1)}), bf16[3,128,16,128]{3,2,1,0:T(8,128)(2,1)S(1)}, s32[]{:S(2)}) async-start(bf16[7,128,16,128]{3,2,1,0:T(8,128)(2,1)} %param.8), calls=%async_computation.2 | async-start | bytes 3145728 | tf_op jit(solution)/shard_map/slice | solution.py:367
  2.8 0.9 slice-start.3
  2.8 1.4 slice-start.1
  2.8 1.6 slice-start.5
  6.9 38.5 %all-to-all-start.1 = ((bf16[128,64,128]{2,1,0:T(8,128)(2,1)}), bf16[128,64,128]{2,1,0:T(8,128)(2,1)S(1)}, u32[]{:S(2)}, u32[]{:S(2)}) async-start(bf16[128,64,128]{2,1,0:T(8,128)(2,1)} %fusion.3), calls=%async_computation.1 | async-start | bytes 4194304 | tf_op jit(solution)/shard_map/all_to_all | solution.py:369
  17.5 3.3 %copy-start.10 = (s32[7,128,2]{1,2,0:T(2,128)S(1)}, s32[7,128,2]{1,2,0:T(2,128)}, u32[]{:S(2)}) copy-start(s32[7,128,2]{1,2,0:T(2,128)} %param.11) | copy-start | bytes 21508
  23.8 2.1 %copy-start.8 = (s32[7,128,2]{1,2,0:T(2,128)S(1)}, s32[7,128,2]{1,2,0:T(2,128)}, u32[]{:S(2)}) copy-start(s32[7,128,2]{1,2,0:T(2,128)} %param.12) | copy-start | bytes 21508
  23.8 2.3 %slice-start.4 = ((s32[7,128,128]{2,1,0:T(8,128)}), s32[4,128,128]{2,1,0:T(8,128)S(1)}, s32[]{:S(2)}) async-start(s32[7,128,128]{2,1,0:T(8,128)} %param.10), calls=%async_computation.6 | async-start | bytes 524288 | tf_op jit(solution)/shard_map/slice | solution.py:367
  23.8 2.8 %slice-start.2 = ((bf16[7,128,2,128]{3,2,1,0:T(2,128)(2,1)}), bf16[4,128,2,128]{3,2,1,0:T(2,128)(2,1)S(1)}, s32[]{:S(2)}) async-start(bf16[7,128,2,128]{3,2,1,0:T(2,128)(2,1)} %param.9), calls=%async_computation.4 | async-start | bytes 524288 | tf_op jit(solution)/shard_map/slice | solution.py:367
  23.8 3.1 %slice-start.6 = ((s32[7,128,2]{1,2,0:T(2,128)}), s32[4,128,2]{1,2,0:T(2,128)S(1)}, s32[]{:S(2)}) async-start(s32[7,128,2]{1,2,0:T(2,128)} %param.12), calls=%async_computation.8 | async-start | bytes 8192 | tf_op jit(solution)/shard_map/slice | solution.py:367
  30.4 23.3 %copy-start.9 = (f32[16,16]{1,0:T(8,128)S(1)}, f32[16,16]{1,0:T(8,128)}, u32[]{:S(2)}) copy-start(f32[16,16]{1,0:T(8,128)} %param.15) | copy-start | bytes 3076
  30.4 23.5 %copy-start.6 = (f32[4,32,128]{2,1,0:T(8,128)S(1)}, f32[4,32,128]{2,1,0:T(8,128)}, u32[]{:S(2)}) copy-start(f32[4,32,128]{2,1,0:T(8,128)} %param.14) | copy-start | bytes 196612
  30.4 23.5 %copy-start.7 = (f32[4,32,128]{2,1,0:T(8,128)S(1)}, f32[4,32,128]{2,1,0:T(8,128)}, u32[]{:S(2)}) copy-start(f32[4,32,128]{2,1,0:T(8,128)} %param.13) | copy-start | bytes 196612
  45.4 1.3 copy-start.1
  46.7 40.5 %all-to-all-start = ((bf16[128,80,128]{2,1,0:T(8,128)(2,1)}), bf16[128,80,128]{2,1,0:T(8,128)(2,1)S(1)}, u32[]{:S(2)}, u32[]{:S(2)}) async-start(bf16[128,80,128]{2,1,0:T(8,128)(2,1)} %fusion.2), calls=%async_computation | async-start | bytes 5242880 | tf_op jit(solution)/shard_map/all_to_all | solution.py:369
  87.3 1.5 copy-start
  152.7 7.6 %collective-permute-start = (f32[8,16,128]{2,1,0:T(8,128)}, f32[8,16,128]{2,1,0:T(8,128)S(1)}, u32[]{:S(2)}, u32[]{:S(2)}) collective-permute-start(f32[8,16,128]{2,1,0:T(8,128)} %get-tuple-element.12), channel_id=1, source_target_pairs={{0,8},{8,16},{16,24},{24,32},{32,40},{40,48},{48,56},{56,64},{64,7... | collective-permute-start | bytes 196616 | tf_op jit(solution)/shard_map/ppermute | solution.py:375
  153.2 7.2 %collective-permute-start.1 = (f32[8,16,128]{2,1,0:T(8,128)}, f32[8,16,128]{2,1,0:T(8,128)S(1)}, u32[]{:S(2)}, u32[]{:S(2)}) collective-permute-start(f32[8,16,128]{2,1,0:T(8,128)} %get-tuple-element.13), channel_id=1, source_target_pairs={{8,0},{16,8},{24,16},{32,24},{40,32},{48,40},{56,48},{64,56},{72,6... | collective-permute-start | bytes 196616 | tf_op jit(solution)/shard_map/ppermute | solution.py:376
  160.3 16.6 %copy-start.4 = (f32[8,16,128]{2,1,0:T(8,128)}, f32[8,16,128]{2,1,0:T(8,128)S(1)}, u32[]{:S(2)}) copy-start(f32[8,16,128]{2,1,0:T(8,128)S(1)} %collective-permute-done.west_ref) | copy-start | bytes 196612
  160.4 16.6 %copy-start.5 = (f32[8,16,128]{2,1,0:T(8,128)}, f32[8,16,128]{2,1,0:T(8,128)S(1)}, u32[]{:S(2)}) copy-start(f32[8,16,128]{2,1,0:T(8,128)S(1)} %collective-permute-done.1.east_ref) | copy-start | bytes 196612
  161.5 14.2 %collective-permute-start.2 = (f32[43,16,128]{2,1,0:T(8,128)S(1)}, f32[43,16,128]{2,1,0:T(8,128)S(1)}, u32[]{:S(2)}, u32[]{:S(2)}) collective-permute-start(f32[43,16,128]{2,1,0:T(8,128)S(1)} %get-tuple-element.16), channel_id=1, source_target_pairs={{0,1},{1,2},{2,3},{3,4},{4,5},{5,6},{6,7},{8,9},{9,10},{10,11},{11... | collective-permute-start | bytes 1056776 | tf_op jit(solution)/shard_map/ppermute | solution.py:378
  163.8 13.1 %collective-permute-start.3 = (f32[43,16,128]{2,1,0:T(8,128)S(1)}, f32[43,16,128]{2,1,0:T(8,128)S(1)}, u32[]{:S(2)}, u32[]{:S(2)}) collective-permute-start(f32[43,16,128]{2,1,0:T(8,128)S(1)} %get-tuple-element.15), channel_id=1, source_target_pairs={{1,0},{2,1},{3,2},{4,3},{5,4},{6,5},{7,6},{9,8},{10,9},{11,10},{12... | collective-permute-start | bytes 1056776 | tf_op jit(solution)/shard_map/ppermute | solution.py:379
  175.7 1.2 copy-start.2
  176.9 0.7 copy-start.3

commit v3 on v2

v3 whole, which is shorter than its diff:
```python
import functools

import jax
import jax.numpy as jnp
from jax import lax
from jax.experimental import pallas as pl
from jax.experimental.pallas import tpu as pltpu
from jax.sharding import PartitionSpec as P


VARS = 4
LEV = 4
CH = 16
TILE = 16
LANES = 128
KAPPA = 0.125
AXES = ("lon", "lat")
F32 = jnp.float32
BF16 = jnp.bfloat16
CHUNK_A = 3


def offsets_of(widths):
    starts, total = [], 0
    for width in widths:
        starts.append(total)
        total += width
    return starts, total


def aux_row(slots, slot):
    return slots * CH + 8 * (slot // 2) + 3 * (slot % 2)


def build_payload(innovations, fractions, cell_index, counts, blocks, every_block):
    slots, targets, channels, width = innovations.shape
    tiles = counts.shape[2]
    per_tile = width // tiles
    lane = lax.broadcasted_iota(jnp.int32, (1, 1, width), 2)
    first = lane < per_tile
    count_lane = jnp.where(first, counts[:, :, 0:1], counts[:, :, 1:2])
    block_lane = jnp.where(first, blocks[:, :, 0:1], blocks[:, :, 1:2])
    is_live = (lane & (per_tile - 1)) < count_lane
    values = jnp.where(is_live[:, :, None, :], innovations, jnp.zeros((), BF16))
    row = cell_index >> 4
    column = cell_index & 15
    skewed = (row >> 3) * LANES + ((row + block_lane) & 7) * TILE + column
    triple = jnp.concatenate([fractions, skewed.astype(BF16)[:, :, None, :]], axis=2)
    pairs = -(-slots // 2)
    triple = jnp.pad(jnp.transpose(triple, (1, 0, 2, 3)), ((0, 0), (0, 2 * pairs - slots), (0, 0), (0, 0)))
    spots = jnp.transpose(every_block, (1, 0, 2)).reshape(targets, 1, 1, -1).astype(BF16)
    spots = jnp.pad(spots, ((0, 0), (0, pairs - 1), (0, 1), (0, LANES - spots.shape[3])))
    aux = jnp.concatenate([triple.reshape(targets, pairs, 6, width), spots], axis=2)
    return jnp.concatenate(
        [
            jnp.transpose(values, (1, 0, 2, 3)).reshape(targets, slots * channels, width),
            aux.reshape(targets, pairs * 8, width),
        ],
        axis=1,
    )


BLOCKS = 16
PARTS = 2
GROUP = 4
UNITS = 2


def group_limit(tiles):
    return (tiles + BLOCKS * (GROUP - 1)) // GROUP


def plan_kernel(slots, spot_row, got_ref, out_ref):
    senders = got_ref.shape[0]
    tiles = 2 * senders
    spots = jnp.transpose(got_ref[:, spot_row, :].astype(F32))
    kind = lax.broadcasted_iota(jnp.int32, (BLOCKS, tiles), 0).astype(F32)
    hits = []
    for slot in range(slots):
        row = jnp.concatenate([spots[2 * slot : 2 * slot + 1], spots[2 * slot + 1 : 2 * slot + 2]], axis=1)
        hits.append(jnp.where(kind == row, 1.0, 0.0))
    hit = jnp.concatenate(hits, axis=0)
    earlier = lax.broadcasted_iota(jnp.int32, (tiles, tiles), 0) < lax.broadcasted_iota(jnp.int32, (tiles, tiles), 1)
    rank = jnp.dot(hit.astype(BF16), jnp.where(earlier, 1.0, 0.0).astype(BF16), preferred_element_type=F32)
    count = jnp.sum(hit, axis=1, keepdims=True)
    groups = jnp.broadcast_to(jnp.floor((count + (GROUP - 1)) * (1.0 / GROUP)), (slots * BLOCKS, LANES))
    above = lax.broadcasted_iota(jnp.int32, (slots * BLOCKS,) * 2, 0)
    across = lax.broadcasted_iota(jnp.int32, (slots * BLOCKS,) * 2, 1)
    lower = jnp.where((above > across) & ((above >> 4) == (across >> 4)), 1.0, 0.0).astype(BF16)
    begin = jnp.dot(lower, groups.astype(BF16), preferred_element_type=F32)
    number = lax.broadcasted_iota(jnp.int32, (BLOCKS, LANES), 1).astype(F32)
    index = lax.broadcasted_iota(jnp.int32, (8, tiles), 1)
    kinds = jnp.where(lax.broadcasted_iota(jnp.int32, (8, tiles), 0) == 0, index, 1).astype(F32).astype(BF16)
    place = lax.broadcasted_iota(jnp.int32, (GROUP * LANES, tiles), 0).astype(F32)
    most = jnp.zeros((1, LANES), F32)
    rows = []
    for slot in range(slots):
        part = slice(slot * BLOCKS, (slot + 1) * BLOCKS)
        start, size = begin[part], groups[part]
        wide = jnp.concatenate([start, start], axis=1)
        fours = jnp.floor(rank[part] * (1.0 / GROUP))
        spot = wide + fours + LANES * (rank[part] - GROUP * fours)
        spot = jnp.sum(hit[part] * spot, axis=0, keepdims=True)
        chosen = jnp.where(place == spot, 1.0, 0.0).astype(BF16)
        order = lax.dot_general(kinds, chosen, (((1,), (1,)), ((), ())), preferred_element_type=F32)
        taken = jnp.zeros((1, LANES), F32)
        for j in range(GROUP):
            tile = order[0:1, j * LANES : (j + 1) * LANES]
            second = jnp.where(tile >= LANES, 1.0, 0.0)
            turned = 1.0 - second if j & 1 else second
            rows.append(tile - LANES * second + LANES * turned)
            taken = taken + order[1:2, j * LANES : (j + 1) * LANES]
        block = jnp.sum(jnp.where(start + size <= number, 1.0, 0.0), axis=0, keepdims=True)
        rows.append(jnp.minimum(block, BLOCKS - 1.0) + BLOCKS * taken)
        most = jnp.maximum(most, start[BLOCKS - 1 :] + size[BLOCKS - 1 :])
    rows += [jnp.zeros((LANES - 1 - len(rows), LANES), F32), most]
    table = jnp.transpose(jnp.concatenate(rows, axis=0))
    out_ref[...] = table[: out_ref.shape[0]].astype(jnp.int32)


def plan(got, slots_all, slots_here):
    senders = got.shape[0]
    spot_row = aux_row(slots_here, 0) + 6
    limit = -(-(group_limit(2 * senders) + 2 * UNITS) // 8) * 8
    return pl.pallas_call(
        functools.partial(plan_kernel, slots_all, spot_row),
        in_specs=[pl.BlockSpec(memory_space=pltpu.VMEM)],
        out_specs=pl.BlockSpec(memory_space=pltpu.VMEM),
        out_shape=jax.ShapeDtypeStruct((limit, LANES), jnp.int32),
        name="plan",
    )(got)


def scatter_kernel(slots, offset, widths, plan_ref, got_ref, *rest):
    late = offset > 0
    if late:
        base_left, base_right = rest[:2]
        rest = rest[2:]
    else:
        wind_ref, rest = rest[0], rest[1:]
    out_ref, left_ref, right_ref, top_ref, bottom_ref, below_ref, held_ref = rest[:7]
    acc_refs = rest[7:]
    rows_out = out_ref.shape[1]

    lane = lax.broadcasted_iota(jnp.int32, (CH, LANES), 1)
    first = lane < LANES // 2
    first_aux = first[:8]
    sixteen = lax.broadcasted_iota(jnp.int32, (TILE, LANES), 0).astype(F32).astype(BF16)
    one_bf, zero_bf = jnp.ones((), BF16), jnp.zeros((), BF16)

    def gather(slot, number, held):
        values, auxes = [], []
        column = 5 * (offset + slot)
        info = plan_ref[number, column + 4]
        for j in range(GROUP):
            entry = plan_ref[number, column + j]
            sender = entry & (LANES - 1)
            turn = (entry & LANES) >> 1
            value = got_ref[sender, pl.ds(slot * CH, CH), :].astype(F32)
            aux = got_ref[sender, pl.ds(aux_row(slots, slot) // 8 * 8, 8), :].astype(F32)
            values.append(pltpu.roll(value, turn, 1))
            auxes.append(pltpu.roll(aux, turn, 1))
        live = (info >> 4) << 6
        for h in range(2):
            value = jnp.where(first, values[2 * h], values[2 * h + 1])
            held[h, :CH] = jnp.where(lane < live - h * LANES, value, 0.0)
            held[h, CH:] = jnp.where(first_aux, auxes[2 * h], auxes[2 * h + 1])

    def unit(slot, held):
        row = aux_row(slots, slot) % 8
        lefts, rights = [], []
        for h in range(2):
            value, aux = held[h, :CH], held[h, CH:]
            major = jnp.floor(aux * (1.0 / TILE))
            minor = aux - TILE * major
            by_x = value * aux[row + 1 : row + 2]
            frac_y = aux[row : row + 1]
            highs, lows = [value.astype(BF16)], []
            for part in (by_x, value * frac_y, by_x * frac_y):
                high = part.astype(BF16)
                highs.append(high)
                lows.append((part - high.astype(F32)).astype(BF16))
            lefts.append(jnp.concatenate(highs + lows, axis=0))
            spot = row + 2
            small = jnp.broadcast_to(minor[spot : spot + 1], (TILE, LANES)).astype(BF16)
            large = jnp.broadcast_to(major[spot : spot + 1], (TILE, LANES)).astype(BF16)
            one_hot = jnp.where(sixteen == small, one_bf, zero_bf)
            rights.append(
                jnp.concatenate(
                    [jnp.where(large == jnp.asarray(k, BF16), one_hot, zero_bf) for k in range(TILE)], axis=0
                )
            )
        return lax.dot_general(
            jnp.concatenate(lefts, axis=1), jnp.concatenate(rights, axis=1), (((1,), (1,)), ((), ())),
            preferred_element_type=F32,
        )

    def add(slot, info, sums):
        block = info & (BLOCKS - 1)
        for part in range(4):
            rows = pl.ds(part * CH, CH)
            total = sums[part * CH : (part + 1) * CH]
            if part:
                total = total + sums[(part + 3) * CH : (part + 4) * CH]
            acc_refs[slot][block, rows] += total

    units = [(slot, k) for k in range(UNITS) for slot in range(slots)]

    def fetch(number):
        for place, (slot, k) in enumerate(units):
            gather(slot, UNITS * number + k, held_ref.at[place])

    def several(number, carry):
        for place, (slot, k) in enumerate(units):
            sums = unit(slot, held_ref.at[place])
            add(slot, plan_ref[UNITS * number + k, 5 * (offset + slot) + 4], sums)
        fetch(number + 1)
        return carry

    for acc_ref in acc_refs:
        acc_ref[...] = jnp.zeros_like(acc_ref)
    fetch(0)
    lax.fori_loop(0, (plan_ref[0, LANES - 1] + UNITS - 1) // UNITS, several, 0)

    lane_group = lane >> 4
    for slot in range(slots):
        acc_ref = acc_refs[slot]

        def part(number, carry, slot=slot, acc_ref=acc_ref):
            band = number >> 1
            half = number & 1
            straight = [jnp.zeros((CH, LANES), F32)] * 8
            under = [jnp.zeros((CH, LANES), F32)] * 8
            for column in range(8):
                tile = acc_ref[band * 8 + column, :, pl.ds(pl.multiple_of(half * LANES, LANES), LANES)]
                a_0, a_x = tile[:CH], tile[CH : 2 * CH]
                a_y, a_xy = tile[2 * CH : 3 * CH], tile[3 * CH :]
                x_only, y_only = a_x - a_xy, a_y - a_xy
                here = a_0 - a_x - y_only + pltpu.roll(x_only, 1, 1)
                next_row = y_only + pltpu.roll(a_xy, 1, 1)
                for y in range(8):
                    hit = lane_group == ((y + column) & 7)
                    straight[y] = jnp.where(hit, here, straight[y])
                    under[y] = jnp.where(hit, next_row, under[y])
            for y in range(8):
                turn = (-16 * y) % LANES
                row = band * 16 + half * 8 + y
                out_ref[slot, row] = pltpu.roll(straight[y], turn, 1) if turn else straight[y]
                below_ref[row] = pltpu.roll(under[y], turn, 1) if turn else under[y]
            return carry

        lax.fori_loop(0, 4, part, 0, unroll=PARTS)
        out_ref[slot, 1:] += below_ref[: rows_out - 1]

    starts, _ = offsets_of(widths)
    jobs = [(out_ref.at[k], starts[offset + k], widths[offset + k]) for k in range(min(slots, len(widths) - 1 - offset))]
    if not late:
        jobs.append((wind_ref, starts[-1], widths[-1]))
    spot = 0
    for source, _, width in jobs:
        top_ref[spot : spot + width] = source[:width]
        bottom_ref[spot : spot + width] = source[rows_out - width :]
        spot += width
    per_group = rows_out // GROUPS

    def pack(row, carry):
        to_left = base_left[row] if late else jnp.zeros((CH, LANES), F32)
        to_right = base_right[row] if late else jnp.zeros((CH, LANES), F32)
        for group in range(GROUPS):
            for source, start, width in jobs:
                value = source[group * per_group + row]
                begin = group * SPAN + start
                hit = (lane >= begin) & (lane < begin + width)
                to_left = jnp.where(hit, pltpu.roll(value, begin, 1) if begin else value, to_left)
                turn = (begin + width) % LANES
                to_right = jnp.where(hit, pltpu.roll(value, turn, 1) if turn else value, to_right)
        left_ref[row] = to_left
        right_ref[row] = to_right
        return carry

    lax.fori_loop(0, per_group, pack, 0)


ROWS = 8
GROUPS = 4
SPAN = LANES // GROUPS


def scatter(got, table, slots, offset, rows_out, widths, *extra):
    carried = sum(widths[offset:-1]) if offset else sum(widths[:slots]) + widths[-1]
    shapes = [(slots, rows_out, CH, LANES)]
    shapes += [(rows_out // GROUPS, CH, LANES)] * 2 + [(carried, CH, LANES)] * 2
    vmem = pl.BlockSpec(memory_space=pltpu.VMEM)
    return pl.pallas_call(
        functools.partial(scatter_kernel, slots, offset, widths),
        in_specs=[pl.BlockSpec(memory_space=pltpu.SMEM), vmem] + [vmem for e in extra],
        out_specs=[vmem for s in shapes],
        scratch_shapes=[
            pltpu.VMEM((rows_out, CH, LANES), F32),
            pltpu.VMEM((UNITS * slots, 2, CH + 8, LANES), F32),
        ]
        + [pltpu.VMEM((BLOCKS, 4 * CH, 2 * LANES), F32)] * slots,
        out_shape=[jax.ShapeDtypeStruct(s, F32) for s in shapes],
        name="scatter",
    )(table, got, *extra)


def march_kernel(
    widths, halo, early, edge_ref, first_ref, second_ref, wind_ref, above_a, above_b, below_a, below_b,
    west_ref, east_ref, mix_ref, out_ref, field_ref, extra_ref, mixed_ref, turn_ref,
):
    rows_own = first_ref.shape[1]
    tall = rows_own + 2 * halo
    per_group = west_ref.shape[0]
    starts, _ = offsets_of(widths)
    lane = lax.broadcasted_iota(jnp.int32, (CH, LANES), 1)
    main = pl.ds(0, LANES)
    side = pl.ds(LANES, LANES)
    steps = len(widths) - 1
    sources = [first_ref.at[k] for k in range(early)]
    sources += [second_ref.at[k] for k in range(steps - early)] + [wind_ref]

    for slot, (start, width) in enumerate(zip(starts, widths)):
        lo, hi = halo - width, halo + rows_own + width
        extra_ref[slot, hi : hi + ROWS] = jnp.zeros((ROWS, CH, 2 * LANES), F32)
        from_a = slot < early or slot == steps
        spot = sum(widths[:early]) if slot == steps else start if from_a else start - sum(widths[:early]) + 2 * halo
        extra_ref[slot, lo:halo, :, main] = (above_a if from_a else above_b)[spot : spot + width]
        extra_ref[slot, halo : halo + rows_own, :, main] = sources[slot][...]
        extra_ref[slot, halo + rows_own : hi, :, main] = (below_a if from_a else below_b)[spot : spot + width]

    def edge(west, east, group, start, width):
        begin = group * SPAN + start
        turn = (-begin) % LANES
        value = jnp.where(lane < width, pltpu.roll(east, turn, 1) if turn else east, 0.0)
        turn = (LANES - width - begin) % LANES
        return jnp.where(lane >= LANES - width, pltpu.roll(west, turn, 1) if turn else west, value)

    def edges(row, carry):
        west, east = west_ref[row], east_ref[row]
        for group in range(GROUPS):
            for slot, (start, width) in enumerate(zip(starts, widths)):
                extra_ref[slot, halo + group * per_group + row, :, side] = edge(west, east, group, start, width)
        return carry

    lax.fori_loop(0, per_group, edges, 0)
    for slot, (start, width) in enumerate(zip(starts, widths)):
        for i in range(width):
            spot = halo - width + i
            extra_ref[slot, spot, :, side] = edge(above_b[spot], above_b[spot + halo], GROUPS - 1, start, width)
            extra_ref[slot, halo + rows_own + i, :, side] = edge(below_b[i], below_b[halo + i], 0, start, width)

    extra_ref[0, tall:] = jnp.zeros((extra_ref.shape[1] - tall, CH, 2 * LANES), F32)
    field_ref[...] = jnp.zeros_like(field_ref)
    mixed_ref[tall:] = jnp.zeros((mixed_ref.shape[0] - tall, CH, 2 * LANES), F32)
    matrix = mix_ref[...]
    wind = extra_ref.at[steps]
    half = CH // 2

    def mix(source, begin, count):
        for number in range(count):
            rows = pl.ds(begin + 8 * number, 8)
            field = source[rows].reshape(8 * CH, 2 * LANES)
            high = field.astype(BF16)
            low = (field - high.astype(F32)).astype(BF16)
            product = lax.dot_general(
                matrix, jnp.concatenate([high, high, low], axis=0), (((1,), (0,)), ((), ())),
                preferred_element_type=F32,
            )
            mixed_ref[rows] = product.reshape(8, CH, 2 * LANES)

    def twice(value):
        return jnp.concatenate([value, value], axis=0)

    for number in range(steps):
        reach = widths[number]
        source = extra_ref.at[0] if number == 0 else field_ref.at[number % 2]
        target = field_ref.at[(number + 1) % 2]
        begin, end = halo - reach, halo + rows_own + reach
        last = number == steps - 1
        mix(source, begin, -(-(end - begin) // 8))

        def pair(index, carry, target=target, begin=begin, last=last, number=number):
            for offset in range(ROWS):
                row = begin + 1 + ROWS * index + offset
                mixed = mixed_ref[row]
                u_half = twice(wind[row, :half]) * 0.5
                result = (1.0 - 4.0 * KAPPA) * mixed
                result = result + pltpu.roll((KAPPA + u_half) * mixed, 2 * LANES - 1, 1)
                result = result + pltpu.roll((KAPPA - u_half) * mixed, 1, 1)
                result = result + (KAPPA + 0.5 * twice(wind[row + 1, half:])) * mixed_ref[row + 1]
                result = result + (KAPPA - 0.5 * twice(wind[row - 1, half:])) * mixed_ref[row - 1]
                if last:
                    turn_ref[row - halo] = result[:, :LANES] + second_ref[steps - early, row - halo]
                else:
                    target[row] = result + extra_ref[number + 1, row]
            return carry

        lax.fori_loop(0, -(-(end - begin - 2) // ROWS), pair, 0)
        if not last:

            @pl.when(edge_ref[0] == 1)
            def _(target=target):
                target[:halo] = jnp.zeros((halo, CH, 2 * LANES), F32)

            @pl.when(edge_ref[1] == 1)
            def _(target=target):
                target[halo + rows_own : tall] = jnp.zeros((halo, CH, 2 * LANES), F32)

    for channel in range(CH):
        out_ref[channel] = turn_ref[:, channel, :]


def march(edge, first, second, wind, above, below, west, east, mix, widths, halo):
    rows_own = first.shape[1]
    tall = rows_own + 2 * halo
    vmem = pl.BlockSpec(memory_space=pltpu.VMEM)
    return pl.pallas_call(
        functools.partial(march_kernel, widths, halo, first.shape[0]),
        in_specs=[pl.BlockSpec(memory_space=pltpu.SMEM)] + [vmem] * 10,
        out_specs=vmem,
        out_shape=jax.ShapeDtypeStruct((CH, rows_own, LANES), F32),
        scratch_shapes=[
            pltpu.VMEM((2, tall + 8, CH, 2 * LANES), F32),
            pltpu.VMEM((len(widths), tall + 8, CH, 2 * LANES), F32),
            pltpu.VMEM((tall + 8, CH, 2 * LANES), F32),
            pltpu.VMEM((rows_own, CH, LANES), F32),
        ],
        name="march",
    )(edge, first, second, wind, *above, *below, west, east, mix)


def mix_matrix(channel_mix):
    rounded = lax.reduce_precision(channel_mix.T, 8, 7)
    high = rounded.astype(BF16)
    low = (channel_mix.T - rounded).astype(BF16)
    eye = jnp.eye(8, dtype=BF16)
    return jnp.concatenate([jnp.kron(eye, high), jnp.kron(eye, low), jnp.kron(eye, high)], axis=1)


def ring(axis, wrap):
    count = lax.axis_size(axis)
    up = [(i, (i + 1) % count) for i in range(count if wrap else count - 1)]
    return up, [(j, i) for i, j in up]


def program(innovations, fractions, cell_index, counts, blocks, u_wind, v_wind, channel_mix):
    slots = innovations.shape[0]
    rows_own = u_wind.shape[1]
    halo = slots - 1
    widths = tuple(range(halo, 0, -1)) + (halo,)
    early = CHUNK_A
    got = []
    for name, low, high in (("move_a", slots - early, slots), ("move_b", 0, slots - early)):
        parts = [x[low:high][::-1] for x in (innovations, fractions, cell_index, counts, blocks)]
        payload = build_payload(*parts, blocks[::-1] if name == "move_a" else parts[4])
        got.append(lax.all_to_all(payload, AXES, split_axis=0, concat_axis=0, tiled=True))
    u_rows, v_rows = jnp.transpose(u_wind, (1, 0, 2)), jnp.transpose(v_wind, (1, 0, 2))
    wind = jnp.concatenate([u_rows, u_rows, v_rows, v_rows], axis=1)
    table = plan(got[0], slots, early)
    first, left_a, right_a, top_a, bottom_a = scatter(got[0], table, early, 0, rows_own, widths, wind)
    up, down = ring("lat", False)
    above_a, below_a = lax.ppermute(bottom_a, "lat", up), lax.ppermute(top_a, "lat", down)
    second, to_left, to_right, top_b, bottom_b = scatter(
        got[1], table, slots - early, early, rows_own, widths, left_a, right_a
    )
    per_group = to_left.shape[0]
    up, down = ring("lon", True)
    west = lax.ppermute(to_right, "lon", up)
    east = lax.ppermute(to_left, "lon", down)
    up, down = ring("lat", False)
    last_up = jnp.concatenate([west[per_group - halo :], east[per_group - halo :], bottom_b])
    last_down = jnp.concatenate([west[:halo], east[:halo], top_b])
    above = [above_a, lax.ppermute(last_up, "lat", up)]
    below = [below_a, lax.ppermute(last_down, "lat", down)]
    lat_index = lax.axis_index("lat")
    edge = jnp.stack([lat_index == 0, lat_index == lax.axis_size("lat") - 1]).astype(jnp.int32)
    field = march(edge, first, second, wind, above, below, west, east, mix_matrix(channel_mix), widths, halo)
    return field.reshape(VARS, LEV, rows_own, u_wind.shape[2])


def solution(mesh):
    in_specs = (
        P(None, ("lon", "lat"), None, None),
        P(None, ("lon", "lat"), None, None),
        P(None, ("lon", "lat"), None),
        P(None, ("lon", "lat"), None),
        P(None, ("lon", "lat"), None),
        P(None, "lat", "lon"),
        P(None, "lat", "lon"),
        P(),
    )
    out_specs = P(None, None, "lat", "lon")
    return jax.shard_map(program, mesh=mesh, in_specs=in_specs, out_specs=out_specs, check_vma=False)
```

time: 193 us -> 154 us (0.80)
  waiting for transfers between devices: 53.8 us -> 33.3 us
  Pallas kernels: 76.8 us -> 58.1 us
  starting transfers between devices: 30.8 us -> 37.3 us
  other arithmetic: 15.1 us -> 11.6 us
    all_to_all x2, waiting for transfers between devices: 45.9 us -> 25.6 us  [program(): lax.all_to_all(payload, AXES, split_axis=0, concat_axis=0, tiled=True)]
    pallas_call x2 -> x3, Pallas kernels: 63.9 us -> 47.1 us  [the longest x2 43.9 us: scatter(): pl.pallas_call(functools.partial(scatter_kernel, slots, offset, widths),...]
    ppermute x2 -> x4, starting transfers between devices: 7.95 us -> 14 us  [the longest x1 5.2 us: program(): lax.ppermute(top_a, 'lat', down)]
    convert_element_type x4 -> x2, other arithmetic: 3.25 us -> 0.7 us  [build_payload(): jnp.transpose(every_block, (1, 0, 2)).reshape(targets, 1, 1, -1)]
    ppermute x1, waiting for transfers between devices: 2.26 us -> 0.01 us  [program(): west = lax.ppermute(to_right, 'lon', up)]
    ppermute x1, waiting for transfers between devices: 0.01 us -> 2.2 us  [program(): east = lax.ppermute(to_left, 'lon', down)]
    slice x15 -> x13, local copies, waits for them, and re-layouts: 3.72 us -> 3.93 us  [program(): x[low:high][::-1]]
    ppermute x2 -> x4, waiting for transfers between devices: 5.64 us -> 5.44 us  [the longest x1 5.43 us: program(): above = [above_a, lax.ppermute(last_up, 'lat', up)]]
  transfers between devices with their start and end apart: 6 -> 8, of which waited for: 5 -> 4; matrix products, arithmetic and copies ran while one was open for 9% -> 10% of each run, Pallas kernels for 0% -> 15%
where the time goes in v3:
time: 154 us; the launch traced here: 153 us
  Pallas kernels  58.1 us (38%)
  starting transfers between devices  37.3 us (24%)
  waiting for transfers between devices  33.3 us (22%)
  local copies, waits for them, and re-layouts  12.5 us (8%)
  other arithmetic  11.6 us (8%)
    pallas_call x2, Pallas kernels, scatter(): pl.pallas_call(functools.partial(scatter_kernel, slots, offset, widths),...  43.9 us
    all_to_all x2, waiting for transfers between devices, program(): lax.all_to_all(payload, AXES, split_axis=0, concat_axis=0, tiled=True)  25.6 us
    all_to_all x2, starting transfers between devices, program(): lax.all_to_all(payload, AXES, split_axis=0, concat_axis=0, tiled=True)  18.4 us
    pallas_call x1, Pallas kernels, march(): pl.pallas_call(functools.partial(march_kernel, widths, halo, first.shape[...  11 us
    ppermute x1, waiting for transfers between devices, program(): above = [above_a, lax.ppermute(last_up, 'lat', up)]  5.43 us
    ppermute x1, starting transfers between devices, program(): lax.ppermute(top_a, 'lat', down)  5.2 us
    ppermute x1, starting transfers between devices, program(): east = lax.ppermute(to_left, 'lon', down)  4.57 us
    slice x13, local copies, waits for them, and re-layouts, program(): x[low:high][::-1]  3.93 us
  transfers between devices with their start and end apart: 8, of which 4 were waited for; matrix products, arithmetic and copies ran while one was open for 10% of the time, Pallas kernels for 15%

profile of v3, /device:TPU:2, one launch (start us, length us, event | category | flops | bytes accessed | tf_op | source)
XLA Modules:
  0.0 153.3 jit_solution(12076145351938738996)
XLA Ops:
  0.0 0.8 fusion.14
  4.9 1.6 %pad_maximum_fusion.1 = bf16[128,64,128]{2,1,0:T(8,128)(2,1)} fusion(bf16[128,16,128]{2,1,0:T(8,128)(2,1)S(1)} %bitcast.58, bf16[128,48,128]{2,1,0:T(8,128)(2,1)S(1)} %bitcast.56), kind=kLoop, calls=%fused_computation.1 | loop fusion | flops 4194304 | bytes 4194304 | tf_op jit(solution)/shard_map/concatenate | solution.py:54
  6.5 10.5 %all-to-all-start = ((bf16[128,64,128]{2,1,0:T(8,128)(2,1)}), bf16[128,64,128]{2,1,0:T(8,128)(2,1)S(1)}, u32[]{:S(2)}, u32[]{:S(2)}) async-start(bf16[128,64,128]{2,1,0:T(8,128)(2,1)} %pad_maximum_fusion.1), calls=%async_computation | async-start | bytes 4194304 | tf_op jit(solution)/shard_map/all_to_all | solution.py:457
  17.0 3.3 %slice.107 = bf16[4,128,16,128]{3,2,1,0:T(8,128)(2,1)} slice(bf16[7,128,16,128]{3,2,1,0:T(8,128)(2,1)} %param.8), slice={[0:4], [0:128], [0:16], [0:128]} | slice | bytes 4194304 | tf_op jit(solution)/shard_map/slice | solution.py:455
  20.6 2.3 %select_bitcast_fusion = bf16[128,4,16,128]{3,2,0,1:T(8,128)(2,1)S(1)} fusion(bf16[4,128,16,128]{3,2,1,0:T(8,128)(2,1)} %slice.107, pred[4,128,128]{2,1,0:T(8,128)(4,1)S(1)} %select_compare_fusion), kind=kLoop, calls=%fused_computation.2 | loop fusion | flops 1048576 | bytes 4259840 | tf_op jit(solution)/shard_map/transpose | solution.py:56
  23.0 2.0 %copy.37 = bf16[128,4,16,128]{3,2,1,0:T(8,128)(2,1)} copy(bf16[128,4,16,128]{3,2,0,1:T(8,128)(2,1)S(1)} %select_bitcast_fusion) | data formatting | bytes 4194304 | tf_op jit(solution)/shard_map/transpose | solution.py:56
  25.9 0.9 copy-done.1
  26.8 1.7 %pad_maximum_fusion = bf16[128,80,128]{2,1,0:T(8,128)(2,1)} fusion(bf16[128,16,128]{2,1,0:T(8,128)(2,1)S(1)} %bitcast.57, bf16[128,64,128]{2,1,0:T(8,128)(2,1)S(1)} %bitcast.55), kind=kLoop, calls=%fused_computation | loop fusion | flops 5242880 | bytes 5242880 | tf_op jit(solution)/shard_map/concatenate | solution.py:54
  28.5 16.5 %all-to-all-done.got_ref = bf16[128,64,128]{2,1,0:T(8,128)(2,1)S(1)} async-done(((bf16[128,64,128]{2,1,0:T(8,128)(2,1)}), bf16[128,64,128]{2,1,0:T(8,128)(2,1)S(1)}, u32[]{:S(2)}, u32[]{:S(2)}) %all-to-all-start) | async-done | bytes 2097184 | tf_op jit(solution)/shard_map/all_to_all | solution.py:457
  45.0 1.3 copy-done
  46.3 7.9 %all-to-all-start.1 = ((bf16[128,80,128]{2,1,0:T(8,128)(2,1)}), bf16[128,80,128]{2,1,0:T(8,128)(2,1)}, u32[]{:S(2)}, u32[]{:S(2)}) async-start(bf16[128,80,128]{2,1,0:T(8,128)(2,1)} %pad_maximum_fusion), calls=%async_computation.1 | async-start | bytes 5242880 | tf_op jit(solution)/shard_map/all_to_all | solution.py:457
  55.3 3.2 %plan.1.plan_ref = s32[80,128]{1,0:T(8,128)} custom-call(bf16[128,64,128]{2,1,0:T(8,128)(2,1)} %copy-done), custom_call_target="tpu_custom_call" | custom-call | tf_op jit(solution)/shard_map/plan/pallas_call | solution.py:125
  58.5 20.0 %scatter.2 = (f32[3,32,16,128]{3,2,1,0:T(8,128)}, f32[8,16,128]{2,1,0:T(8,128)}, f32[8,16,128]{2,1,0:T(8,128)}, f32[21,16,128]{2,1,0:T(8,128)}, f32[21,16,128]{2,1,0:T(8,128)}) custom-call(s32[80,128]{1,0:T(8,128)} %plan.1.plan_ref, bf16[128,64,128]{2,1,0:T(8,128)(2,1)} %copy-done, f32[32,16,128]{2,1,0:T(8,128)} %pad_maximum_fusion.3.rest_0_.wind_ref), custom_call_target="tpu_custom_call" | custom-call | tf_op jit(solution)/shard_map/scatter/pallas_call | solution.py:294
  78.5 9.1 %all-to-all-done.1.got_ref = bf16[128,80,128]{2,1,0:T(8,128)(2,1)} async-done(((bf16[128,80,128]{2,1,0:T(8,128)(2,1)}), bf16[128,80,128]{2,1,0:T(8,128)(2,1)}, u32[]{:S(2)}, u32[]{:S(2)}) %all-to-all-start.1) | async-done | bytes 2621472 | tf_op jit(solution)/shard_map/all_to_all | solution.py:457
  87.7 23.9 %scatter.3 = (f32[4,32,16,128]{3,2,1,0:T(8,128)}, f32[8,16,128]{2,1,0:T(8,128)}, f32[8,16,128]{2,1,0:T(8,128)}, f32[6,16,128]{2,1,0:T(8,128)}, f32[6,16,128]{2,1,0:T(8,128)}) custom-call(s32[80,128]{1,0:T(8,128)} %plan.1.plan_ref, bf16[128,80,128]{2,1,0:T(8,128)(2,1)} %all-to-all-done.1.got_ref, f32[8,16,128]{2,1,0:T(8,128)} %get-tuple-element.16.rest_0_, ...), custom_call_target="tpu_custom_call" | custom-call | tf_op jit(solution)/shard_map/scatter/pallas_call | solution.py:294
  112.0 2.8 %collective-permute-start = (f32[21,16,128]{2,1,0:T(8,128)S(1)}, f32[21,16,128]{2,1,0:T(8,128)S(1)}, u32[]{:S(2)}, u32[]{:S(2)}) collective-permute-start(f32[21,16,128]{2,1,0:T(8,128)S(1)} %copy-done.14), channel_id=1, source_target_pairs={{0,1},{1,2},{2,3},{3,4},{4,5},{5,6},{6,7},{8,9},{9,10},{10,11},{11... | collective-permute-start | bytes 516104 | tf_op jit(solution)/shard_map/ppermute | solution.py:463
  114.8 5.2 %collective-permute-start.4 = (f32[21,16,128]{2,1,0:T(8,128)S(1)}, f32[21,16,128]{2,1,0:T(8,128)S(1)}, u32[]{:S(2)}, u32[]{:S(2)}) collective-permute-start(f32[21,16,128]{2,1,0:T(8,128)S(1)} %copy-done.13), channel_id=1, source_target_pairs={{1,0},{2,1},{3,2},{4,3},{5,4},{6,5},{7,6},{9,8},{10,9},{11,10},{12... | collective-permute-start | bytes 516104 | tf_op jit(solution)/shard_map/ppermute | solution.py:463
  120.0 4.6 %collective-permute-start.2 = (f32[8,16,128]{2,1,0:T(8,128)}, f32[8,16,128]{2,1,0:T(8,128)S(1)}, u32[]{:S(2)}, u32[]{:S(2)}) collective-permute-start(f32[8,16,128]{2,1,0:T(8,128)} %get-tuple-element.21), channel_id=1, source_target_pairs={{8,0},{16,8},{24,16},{32,24},{40,32},{48,40},{56,48},{64,56},{72,6... | collective-permute-start | bytes 196616 | tf_op jit(solution)/shard_map/ppermute | solution.py:470
  124.6 2.2 %collective-permute-done.2.east_ref = f32[8,16,128]{2,1,0:T(8,128)S(1)} collective-permute-done((f32[8,16,128]{2,1,0:T(8,128)}, f32[8,16,128]{2,1,0:T(8,128)S(1)}, u32[]{:S(2)}, u32[]{:S(2)}) %collective-permute-start.2) | collective-permute-done | bytes 65568 | tf_op jit(solution)/shard_map/ppermute | solution.py:470
  126.8 0.8 pad_maximum_fusion.5
  127.6 3.0 %collective-permute-start.5 = (f32[18,16,128]{2,1,0:T(8,128)S(1)}, f32[18,16,128]{2,1,0:T(8,128)S(1)}, u32[]{:S(2)}, u32[]{:S(2)}) collective-permute-start(f32[18,16,128]{2,1,0:T(8,128)S(1)} %pad_maximum_fusion.5), channel_id=1, source_target_pairs={{1,0},{2,1},{3,2},{4,3},{5,4},{6,5},{7,6},{9,8},{10,9},{11,10},{12... | collective-permute-start | bytes 442376 | tf_op jit(solution)/shard_map/ppermute | solution.py:475
  131.5 3.0 %collective-permute-start.3 = (f32[18,16,128]{2,1,0:T(8,128)S(1)}, f32[18,16,128]{2,1,0:T(8,128)S(1)}, u32[]{:S(2)}, u32[]{:S(2)}) collective-permute-start(f32[18,16,128]{2,1,0:T(8,128)S(1)} %pad_maximum_fusion.4), channel_id=1, source_target_pairs={{0,1},{1,2},{2,3},{3,4},{4,5},{5,6},{6,7},{8,9},{9,10},{10,11},{11... | collective-permute-start | bytes 442376 | tf_op jit(solution)/shard_map/ppermute | solution.py:474
  136.2 5.4 %collective-permute-done.3.above_b = f32[18,16,128]{2,1,0:T(8,128)S(1)} collective-permute-done((f32[18,16,128]{2,1,0:T(8,128)S(1)}, f32[18,16,128]{2,1,0:T(8,128)S(1)}, u32[]{:S(2)}, u32[]{:S(2)}) %collective-permute-start.3) | collective-permute-done | bytes 147488 | tf_op jit(solution)/shard_map/ppermute | solution.py:474
  142.3 11.0 %march.1 = f32[16,32,128]{2,1,0:T(8,128)} custom-call(s32[2]{0:T(128)} %add_convert_fusion.2.edge_ref, f32[3,32,16,128]{3,2,1,0:T(8,128)} %get-tuple-element.15.first_ref, f32[4,32,16,128]{3,2,1,0:T(8,128)} %get-tuple-element.18.second_ref, f32[32,16,128]{2,1,0:T(8,128)} %pad_maximum_fusion.3.rest_0_.wind_ref, f32[21,16,128]{2,1,0:T(8,128)} %copy-done.4, ...), custom_call_target="tpu_custom_call" | custom-call | tf_op jit(solution)/shard_map/march/pallas_call | solution.py:418
  (96 shorter events, 9.6 us)
Async XLA Ops:
  0.0 2.5 %slice-start = ((bf16[7,128,16,128]{3,2,1,0:T(8,128)(2,1)}), bf16[3,128,16,128]{3,2,1,0:T(8,128)(2,1)S(1)}, s32[]{:S(2)}) async-start(bf16[7,128,16,128]{3,2,1,0:T(8,128)(2,1)} %param.8), calls=%async_computation.2 | async-start | bytes 3145728 | tf_op jit(solution)/shard_map/slice | solution.py:455
  6.5 38.5 %all-to-all-start = ((bf16[128,64,128]{2,1,0:T(8,128)(2,1)}), bf16[128,64,128]{2,1,0:T(8,128)(2,1)S(1)}, u32[]{:S(2)}, u32[]{:S(2)}) async-start(bf16[128,64,128]{2,1,0:T(8,128)(2,1)} %pad_maximum_fusion.1), calls=%async_computation | async-start | bytes 4194304 | tf_op jit(solution)/shard_map/all_to_all | solution.py:457
  17.0 3.3 %copy-start.12 = (s32[7,128,2]{1,2,0:T(2,128)S(1)}, s32[7,128,2]{1,2,0:T(2,128)}, u32[]{:S(2)}) copy-start(s32[7,128,2]{1,2,0:T(2,128)} %param.11) | copy-start | bytes 21508
  22.9 2.0 %copy-start.10 = (s32[7,128,2]{1,2,0:T(2,128)S(1)}, s32[7,128,2]{1,2,0:T(2,128)}, u32[]{:S(2)}) copy-start(s32[7,128,2]{1,2,0:T(2,128)} %param.12) | copy-start | bytes 21508
  22.9 2.1 %slice-start.4 = ((bf16[7,128,2,128]{3,2,1,0:T(2,128)(2,1)}), bf16[4,128,2,128]{3,2,1,0:T(2,128)(2,1)S(1)}, s32[]{:S(2)}) async-start(bf16[7,128,2,128]{3,2,1,0:T(2,128)(2,1)} %param.9), calls=%async_computation.6 | async-start | bytes 524288 | tf_op jit(solution)/shard_map/slice | solution.py:455
  22.9 2.1 %slice-start.5 = ((s32[7,128,2]{1,2,0:T(2,128)}), s32[4,128,2]{1,2,0:T(2,128)S(1)}, s32[]{:S(2)}) async-start(s32[7,128,2]{1,2,0:T(2,128)} %param.12), calls=%async_computation.7 | async-start | bytes 8192 | tf_op jit(solution)/shard_map/slice | solution.py:455
  22.9 2.3 %slice-start.2 = ((s32[7,128,128]{2,1,0:T(8,128)}), s32[4,128,128]{2,1,0:T(8,128)S(1)}, s32[]{:S(2)}) async-start(s32[7,128,128]{2,1,0:T(8,128)} %param.10), calls=%async_computation.4 | async-start | bytes 524288 | tf_op jit(solution)/shard_map/slice | solution.py:455
  28.5 25.7 %copy-start.11 = (f32[16,16]{1,0:T(8,128)S(1)}, f32[16,16]{1,0:T(8,128)}, u32[]{:S(2)}) copy-start(f32[16,16]{1,0:T(8,128)} %param.15) | copy-start | bytes 3076
  28.5 25.9 %copy-start.8 = (f32[4,32,128]{2,1,0:T(8,128)S(1)}, f32[4,32,128]{2,1,0:T(8,128)}, u32[]{:S(2)}) copy-start(f32[4,32,128]{2,1,0:T(8,128)} %param.14) | copy-start | bytes 196612
  28.5 25.9 %copy-start.9 = (f32[4,32,128]{2,1,0:T(8,128)S(1)}, f32[4,32,128]{2,1,0:T(8,128)}, u32[]{:S(2)}) copy-start(f32[4,32,128]{2,1,0:T(8,128)} %param.13) | copy-start | bytes 196612
  46.3 41.4 %all-to-all-start.1 = ((bf16[128,80,128]{2,1,0:T(8,128)(2,1)}), bf16[128,80,128]{2,1,0:T(8,128)(2,1)}, u32[]{:S(2)}, u32[]{:S(2)}) async-start(bf16[128,80,128]{2,1,0:T(8,128)(2,1)} %pad_maximum_fusion), calls=%async_computation.1 | async-start | bytes 5242880 | tf_op jit(solution)/shard_map/all_to_all | solution.py:457
  78.5 33.5 %copy-start.14 = (f32[21,16,128]{2,1,0:T(8,128)S(1)}, f32[21,16,128]{2,1,0:T(8,128)}, u32[]{:S(2)}) copy-start(f32[21,16,128]{2,1,0:T(8,128)} %get-tuple-element.19) | copy-start | bytes 516100
  78.5 36.3 %copy-start.13 = (f32[21,16,128]{2,1,0:T(8,128)S(1)}, f32[21,16,128]{2,1,0:T(8,128)}, u32[]{:S(2)}) copy-start(f32[21,16,128]{2,1,0:T(8,128)} %get-tuple-element.23) | copy-start | bytes 516100
  111.6 13.0 %collective-permute-start.1 = (f32[8,16,128]{2,1,0:T(8,128)}, f32[8,16,128]{2,1,0:T(8,128)S(1)}, u32[]{:S(2)}, u32[]{:S(2)}) collective-permute-start(f32[8,16,128]{2,1,0:T(8,128)} %get-tuple-element.20), channel_id=1, source_target_pairs={{0,8},{8,16},{16,24},{24,32},{32,40},{40,48},{48,56},{56,64},{64,7... | collective-permute-start | bytes 196616 | tf_op jit(solution)/shard_map/ppermute | solution.py:469
  112.0 24.1 %collective-permute-start = (f32[21,16,128]{2,1,0:T(8,128)S(1)}, f32[21,16,128]{2,1,0:T(8,128)S(1)}, u32[]{:S(2)}, u32[]{:S(2)}) collective-permute-start(f32[21,16,128]{2,1,0:T(8,128)S(1)} %copy-done.14), channel_id=1, source_target_pairs={{0,1},{1,2},{2,3},{3,4},{4,5},{5,6},{6,7},{8,9},{9,10},{10,11},{11... | collective-permute-start | bytes 516104 | tf_op jit(solution)/shard_map/ppermute | solution.py:463
  114.8 21.3 %collective-permute-start.4 = (f32[21,16,128]{2,1,0:T(8,128)S(1)}, f32[21,16,128]{2,1,0:T(8,128)S(1)}, u32[]{:S(2)}, u32[]{:S(2)}) collective-permute-start(f32[21,16,128]{2,1,0:T(8,128)S(1)} %copy-done.13), channel_id=1, source_target_pairs={{1,0},{2,1},{3,2},{4,3},{5,4},{6,5},{7,6},{9,8},{10,9},{11,10},{12... | collective-permute-start | bytes 516104 | tf_op jit(solution)/shard_map/ppermute | solution.py:463
  120.0 6.8 %collective-permute-start.2 = (f32[8,16,128]{2,1,0:T(8,128)}, f32[8,16,128]{2,1,0:T(8,128)S(1)}, u32[]{:S(2)}, u32[]{:S(2)}) collective-permute-start(f32[8,16,128]{2,1,0:T(8,128)} %get-tuple-element.21), channel_id=1, source_target_pairs={{8,0},{16,8},{24,16},{32,24},{40,32},{48,40},{56,48},{64,56},{72,6... | collective-permute-start | bytes 196616 | tf_op jit(solution)/shard_map/ppermute | solution.py:470
  124.6 17.0 %copy-start.2 = (f32[8,16,128]{2,1,0:T(8,128)}, f32[8,16,128]{2,1,0:T(8,128)S(1)}, u32[]{:S(2)}) copy-start(f32[8,16,128]{2,1,0:T(8,128)S(1)} %collective-permute-done.1.west_ref) | copy-start | bytes 196612
  126.8 14.8 %copy-start.3 = (f32[8,16,128]{2,1,0:T(8,128)}, f32[8,16,128]{2,1,0:T(8,128)S(1)}, u32[]{:S(2)}) copy-start(f32[8,16,128]{2,1,0:T(8,128)S(1)} %collective-permute-done.2.east_ref) | copy-start | bytes 196612
  127.6 8.5 %collective-permute-start.5 = (f32[18,16,128]{2,1,0:T(8,128)S(1)}, f32[18,16,128]{2,1,0:T(8,128)S(1)}, u32[]{:S(2)}, u32[]{:S(2)}) collective-permute-start(f32[18,16,128]{2,1,0:T(8,128)S(1)} %pad_maximum_fusion.5), channel_id=1, source_target_pairs={{1,0},{2,1},{3,2},{4,3},{5,4},{6,5},{7,6},{9,8},{10,9},{11,10},{12... | collective-permute-start | bytes 442376 | tf_op jit(solution)/shard_map/ppermute | solution.py:475
  131.5 10.1 %collective-permute-start.3 = (f32[18,16,128]{2,1,0:T(8,128)S(1)}, f32[18,16,128]{2,1,0:T(8,128)S(1)}, u32[]{:S(2)}, u32[]{:S(2)}) collective-permute-start(f32[18,16,128]{2,1,0:T(8,128)S(1)} %pad_maximum_fusion.4), channel_id=1, source_target_pairs={{0,1},{1,2},{2,3},{3,4},{4,5},{5,6},{6,7},{8,9},{9,10},{10,11},{11... | collective-permute-start | bytes 442376 | tf_op jit(solution)/shard_map/ppermute | solution.py:474
  136.1 5.5 %copy-start.4 = (f32[21,16,128]{2,1,0:T(8,128)}, f32[21,16,128]{2,1,0:T(8,128)S(1)}, u32[]{:S(2)}) copy-start(f32[21,16,128]{2,1,0:T(8,128)S(1)} %collective-permute-done.above_a) | copy-start | bytes 516100
  136.1 5.5 %copy-start.5 = (f32[21,16,128]{2,1,0:T(8,128)}, f32[21,16,128]{2,1,0:T(8,128)S(1)}, u32[]{:S(2)}) copy-start(f32[21,16,128]{2,1,0:T(8,128)S(1)} %collective-permute-done.4.below_a) | copy-start | bytes 516100
  136.2 5.5 %copy-start.6 = (f32[18,16,128]{2,1,0:T(8,128)}, f32[18,16,128]{2,1,0:T(8,128)S(1)}, u32[]{:S(2)}) copy-start(f32[18,16,128]{2,1,0:T(8,128)S(1)} %collective-permute-done.5.below_b) | copy-start | bytes 442372
  (5 other events, 5.6 us)

commit v4 on v3

--- a/solution.py
+++ b/solution.py
@@ -61,9 +61,9 @@
 
 
 BLOCKS = 16
-PARTS = 2
+PARTS = 4
 GROUP = 4
-UNITS = 2
+UNITS = 4
 
 
 def group_limit(tiles):
@@ -133,12 +133,7 @@
 
 def scatter_kernel(slots, offset, widths, plan_ref, got_ref, *rest):
     late = offset > 0
-    if late:
-        base_left, base_right = rest[:2]
-        rest = rest[2:]
-    else:
-        wind_ref, rest = rest[0], rest[1:]
-    out_ref, left_ref, right_ref, top_ref, bottom_ref, below_ref, held_ref = rest[:7]
+    extra_ref, out_ref, pack_ref, top_ref, bottom_ref, below_ref, held_ref = rest[:7]
     acc_refs = rest[7:]
     rows_out = out_ref.shape[1]
 
@@ -255,7 +250,7 @@
     starts, _ = offsets_of(widths)
     jobs = [(out_ref.at[k], starts[offset + k], widths[offset + k]) for k in range(min(slots, len(widths) - 1 - offset))]
     if not late:
-        jobs.append((wind_ref, starts[-1], widths[-1]))
+        jobs.append((extra_ref, starts[-1], widths[-1]))
     spot = 0
     for source, _, width in jobs:
         top_ref[spot : spot + width] = source[:width]
@@ -264,32 +259,29 @@
     per_group = rows_out // GROUPS
 
     def pack(row, carry):
-        to_left = base_left[row] if late else jnp.zeros((CH, LANES), F32)
-        to_right = base_right[row] if late else jnp.zeros((CH, LANES), F32)
+        total = extra_ref[row] if late else jnp.zeros((CH, LANES), F32)
         for group in range(GROUPS):
             for source, start, width in jobs:
                 value = source[group * per_group + row]
-                begin = group * SPAN + start
-                hit = (lane >= begin) & (lane < begin + width)
-                to_left = jnp.where(hit, pltpu.roll(value, begin, 1) if begin else value, to_left)
+                begin = group * SPAN + 2 * start
+                hit = (lane >= begin) & (lane < begin + 2 * width)
                 turn = (begin + width) % LANES
-                to_right = jnp.where(hit, pltpu.roll(value, turn, 1) if turn else value, to_right)
-        left_ref[row] = to_left
-        right_ref[row] = to_right
+                total = jnp.where(hit, pltpu.roll(value, turn, 1) if turn else value, total)
+        pack_ref[row] = total
         return carry
 
-    lax.fori_loop(0, per_group, pack, 0)
+    lax.fori_loop(0, per_group, pack, 0, unroll=4)
 
 
 ROWS = 8
-GROUPS = 4
+GROUPS = 2
 SPAN = LANES // GROUPS
 
 
 def scatter(got, table, slots, offset, rows_out, widths, *extra):
     carried = sum(widths[offset:-1]) if offset else sum(widths[:slots]) + widths[-1]
     shapes = [(slots, rows_out, CH, LANES)]
-    shapes += [(rows_out // GROUPS, CH, LANES)] * 2 + [(carried, CH, LANES)] * 2
+    shapes += [(rows_out // GROUPS, CH, LANES)] + [(carried, CH, LANES)] * 2
     vmem = pl.BlockSpec(memory_space=pltpu.VMEM)
     return pl.pallas_call(
         functools.partial(scatter_kernel, slots, offset, widths),
@@ -307,11 +299,11 @@
 
 def march_kernel(
     widths, halo, early, edge_ref, first_ref, second_ref, wind_ref, above_a, above_b, below_a, below_b,
-    west_ref, east_ref, mix_ref, out_ref, field_ref, extra_ref, mixed_ref, turn_ref,
+    ends_ref, mix_ref, out_ref, field_ref, extra_ref, mixed_ref, turn_ref,
 ):
     rows_own = first_ref.shape[1]
     tall = rows_own + 2 * halo
-    per_group = west_ref.shape[0]
+    per_group = ends_ref.shape[0]
     starts, _ = offsets_of(widths)
     lane = lax.broadcasted_iota(jnp.int32, (CH, LANES), 1)
     main = pl.ds(0, LANES)
@@ -324,31 +316,29 @@
         lo, hi = halo - width, halo + rows_own + width
         extra_ref[slot, hi : hi + ROWS] = jnp.zeros((ROWS, CH, 2 * LANES), F32)
         from_a = slot < early or slot == steps
-        spot = sum(widths[:early]) if slot == steps else start if from_a else start - sum(widths[:early]) + 2 * halo
+        spot = sum(widths[:early]) if slot == steps else start if from_a else start - sum(widths[:early]) + halo
         extra_ref[slot, lo:halo, :, main] = (above_a if from_a else above_b)[spot : spot + width]
         extra_ref[slot, halo : halo + rows_own, :, main] = sources[slot][...]
         extra_ref[slot, halo + rows_own : hi, :, main] = (below_a if from_a else below_b)[spot : spot + width]
 
-    def edge(west, east, group, start, width):
-        begin = group * SPAN + start
-        turn = (-begin) % LANES
-        value = jnp.where(lane < width, pltpu.roll(east, turn, 1) if turn else east, 0.0)
-        turn = (LANES - width - begin) % LANES
-        return jnp.where(lane >= LANES - width, pltpu.roll(west, turn, 1) if turn else west, value)
+    def edge(ends, group, start, width):
+        turn = -(group * SPAN + 2 * start + width) % LANES
+        kept = (lane < width) | (lane >= LANES - width)
+        return jnp.where(kept, pltpu.roll(ends, turn, 1) if turn else ends, 0.0)
 
     def edges(row, carry):
-        west, east = west_ref[row], east_ref[row]
+        ends = ends_ref[row]
         for group in range(GROUPS):
             for slot, (start, width) in enumerate(zip(starts, widths)):
-                extra_ref[slot, halo + group * per_group + row, :, side] = edge(west, east, group, start, width)
+                extra_ref[slot, halo + group * per_group + row, :, side] = edge(ends, group, start, width)
         return carry
 
-    lax.fori_loop(0, per_group, edges, 0)
+    lax.fori_loop(0, per_group, edges, 0, unroll=4)
     for slot, (start, width) in enumerate(zip(starts, widths)):
         for i in range(width):
             spot = halo - width + i
-            extra_ref[slot, spot, :, side] = edge(above_b[spot], above_b[spot + halo], GROUPS - 1, start, width)
-            extra_ref[slot, halo + rows_own + i, :, side] = edge(below_b[i], below_b[halo + i], 0, start, width)
+            extra_ref[slot, spot, :, side] = edge(above_b[spot], GROUPS - 1, start, width)
+            extra_ref[slot, halo + rows_own + i, :, side] = edge(below_b[i], 0, start, width)
 
     extra_ref[0, tall:] = jnp.zeros((extra_ref.shape[1] - tall, CH, 2 * LANES), F32)
     field_ref[...] = jnp.zeros_like(field_ref)
@@ -411,13 +401,13 @@
         out_ref[channel] = turn_ref[:, channel, :]
 
 
-def march(edge, first, second, wind, above, below, west, east, mix, widths, halo):
+def march(edge, first, second, wind, above, below, ends, mix, widths, halo):
     rows_own = first.shape[1]
     tall = rows_own + 2 * halo
     vmem = pl.BlockSpec(memory_space=pltpu.VMEM)
     return pl.pallas_call(
         functools.partial(march_kernel, widths, halo, first.shape[0]),
-        in_specs=[pl.BlockSpec(memory_space=pltpu.SMEM)] + [vmem] * 10,
+        in_specs=[pl.BlockSpec(memory_space=pltpu.SMEM)] + [vmem] * 9,
         out_specs=vmem,
         out_shape=jax.ShapeDtypeStruct((CH, rows_own, LANES), F32),
         scratch_shapes=[
@@ -427,7 +417,16 @@
             pltpu.VMEM((rows_own, CH, LANES), F32),
         ],
         name="march",
-    )(edge, first, second, wind, *above, *below, west, east, mix)
+    )(edge, first, second, wind, *above, *below, ends, mix)
+
+
+def west_lanes(widths):
+    lane = lax.broadcasted_iota(jnp.int32, (1, 1, LANES), 2) % SPAN
+    starts, _ = offsets_of(widths)
+    found = lane < 0
+    for start, width in zip(starts, widths):
+        found = found | ((lane >= 2 * start) & (lane < 2 * start + width))
+    return found
 
 
 def mix_matrix(channel_mix):
@@ -458,24 +457,21 @@
     u_rows, v_rows = jnp.transpose(u_wind, (1, 0, 2)), jnp.transpose(v_wind, (1, 0, 2))
     wind = jnp.concatenate([u_rows, u_rows, v_rows, v_rows], axis=1)
     table = plan(got[0], slots, early)
-    first, left_a, right_a, top_a, bottom_a = scatter(got[0], table, early, 0, rows_own, widths, wind)
+    first, pack_a, top_a, bottom_a = scatter(got[0], table, early, 0, rows_own, widths, wind)
     up, down = ring("lat", False)
     above_a, below_a = lax.ppermute(bottom_a, "lat", up), lax.ppermute(top_a, "lat", down)
-    second, to_left, to_right, top_b, bottom_b = scatter(
-        got[1], table, slots - early, early, rows_own, widths, left_a, right_a
-    )
-    per_group = to_left.shape[0]
-    up, down = ring("lon", True)
-    west = lax.ppermute(to_right, "lon", up)
-    east = lax.ppermute(to_left, "lon", down)
-    up, down = ring("lat", False)
-    last_up = jnp.concatenate([west[per_group - halo :], east[per_group - halo :], bottom_b])
-    last_down = jnp.concatenate([west[:halo], east[:halo], top_b])
+    second, pack, top_b, bottom_b = scatter(got[1], table, slots - early, early, rows_own, widths, pack_a)
+    around, back = ring("lon", True)
+    west = lax.ppermute(pack, "lon", around)
+    east = lax.ppermute(pack, "lon", back)
+    ends = jnp.where(west_lanes(widths), west, east)
+    last_up = jnp.concatenate([ends[-halo:], bottom_b])
+    last_down = jnp.concatenate([ends[:halo], top_b])
     above = [above_a, lax.ppermute(last_up, "lat", up)]
     below = [below_a, lax.ppermute(last_down, "lat", down)]
     lat_index = lax.axis_index("lat")
     edge = jnp.stack([lat_index == 0, lat_index == lax.axis_size("lat") - 1]).astype(jnp.int32)
-    field = march(edge, first, second, wind, above, below, west, east, mix_matrix(channel_mix), widths, halo)
+    field = march(edge, first, second, wind, above, below, ends, mix_matrix(channel_mix), widths, halo)
     return field.reshape(VARS, LEV, rows_own, u_wind.shape[2])
 
 

time: 154 us -> 148 us (0.961)
  Pallas kernels: 58.1 us -> 51.2 us
    pallas_call x2, Pallas kernels: 43.9 us -> 37.7 us  [scatter(): pl.pallas_call(functools.partial(scatter_kernel, slots, offset, widths),...]
    all_to_all x2, waiting for transfers between devices: 25.6 us -> 28.8 us  [program(): lax.all_to_all(payload, AXES, split_axis=0, concat_axis=0, tiled=True)]
    ppermute x2, waiting for transfers between devices: 2.21 us -> 0.01 us  [the longest x1 0.01 us: program(): east = lax.ppermute(pack, 'lon', back)]
  transfers between devices with their start and end apart: 8 -> 8, of which waited for: 4 -> 3; matrix products, arithmetic and copies ran while one was open for 10% -> 10% of each run, Pallas kernels for 15% -> 14%
where the time goes in v4:
time: 148 us; the launch traced here: 147 us
  Pallas kernels  51.2 us (35%)
  starting transfers between devices  37.6 us (25%)
  waiting for transfers between devices  33.9 us (23%)
  local copies, waits for them, and re-layouts  12.5 us (8%)
  other arithmetic  11.7 us (8%)
    pallas_call x2, Pallas kernels, scatter(): pl.pallas_call(functools.partial(scatter_kernel, slots, offset, widths),...  37.7 us
    all_to_all x2, waiting for transfers between devices, program(): lax.all_to_all(payload, AXES, split_axis=0, concat_axis=0, tiled=True)  28.8 us
    all_to_all x2, starting transfers between devices, program(): lax.all_to_all(payload, AXES, split_axis=0, concat_axis=0, tiled=True)  18.4 us
    pallas_call x1, Pallas kernels, march(): pl.pallas_call(functools.partial(march_kernel, widths, halo, first.shape[...  10.2 us
    ppermute x1, starting transfers between devices, program(): lax.ppermute(top_a, 'lat', down)  5.72 us
    ppermute x1, waiting for transfers between devices, program(): above = [above_a, lax.ppermute(last_up, 'lat', up)]  5.12 us
    ppermute x1, starting transfers between devices, program(): east = lax.ppermute(pack, 'lon', back)  5.05 us
    slice x13, local copies, waits for them, and re-layouts, program(): x[low:high][::-1]  3.94 us
  transfers between devices with their start and end apart: 8, of which 3 were waited for; matrix products, arithmetic and copies ran while one was open for 10% of the time, Pallas kernels for 14%

profile of v4, /device:TPU:2, one launch (start us, length us, event | category | flops | bytes accessed | tf_op | source)
XLA Modules:
  0.0 147.3 jit_solution(13527485148695144578)
XLA Ops:
  0.0 0.8 fusion.13
  4.9 1.6 %pad_maximum_fusion.1 = bf16[128,64,128]{2,1,0:T(8,128)(2,1)} fusion(bf16[128,16,128]{2,1,0:T(8,128)(2,1)S(1)} %bitcast.58, bf16[128,48,128]{2,1,0:T(8,128)(2,1)S(1)} %bitcast.56), kind=kLoop, calls=%fused_computation.1 | loop fusion | flops 4194304 | bytes 4194304 | tf_op jit(solution)/shard_map/concatenate | solution.py:54
  6.5 10.5 %all-to-all-start = ((bf16[128,64,128]{2,1,0:T(8,128)(2,1)}), bf16[128,64,128]{2,1,0:T(8,128)(2,1)S(1)}, u32[]{:S(2)}, u32[]{:S(2)}) async-start(bf16[128,64,128]{2,1,0:T(8,128)(2,1)} %pad_maximum_fusion.1), calls=%async_computation | async-start | bytes 4194304 | tf_op jit(solution)/shard_map/all_to_all | solution.py:456
  17.1 3.3 %slice.101 = bf16[4,128,16,128]{3,2,1,0:T(8,128)(2,1)} slice(bf16[7,128,16,128]{3,2,1,0:T(8,128)(2,1)} %param.8), slice={[0:4], [0:128], [0:16], [0:128]} | slice | bytes 4194304 | tf_op jit(solution)/shard_map/slice | solution.py:454
  20.6 2.3 %select_bitcast_fusion = bf16[128,4,16,128]{3,2,0,1:T(8,128)(2,1)S(1)} fusion(bf16[4,128,16,128]{3,2,1,0:T(8,128)(2,1)} %slice.101, pred[4,128,128]{2,1,0:T(8,128)(4,1)S(1)} %select_compare_fusion), kind=kLoop, calls=%fused_computation.2 | loop fusion | flops 1048576 | bytes 4259840 | tf_op jit(solution)/shard_map/transpose | solution.py:56
  23.0 2.0 %copy.37 = bf16[128,4,16,128]{3,2,1,0:T(8,128)(2,1)} copy(bf16[128,4,16,128]{3,2,0,1:T(8,128)(2,1)S(1)} %select_bitcast_fusion) | data formatting | bytes 4194304 | tf_op jit(solution)/shard_map/transpose | solution.py:56
  25.9 0.9 copy-done.1
  26.8 1.7 %pad_maximum_fusion = bf16[128,80,128]{2,1,0:T(8,128)(2,1)} fusion(bf16[128,16,128]{2,1,0:T(8,128)(2,1)S(1)} %bitcast.57, bf16[128,64,128]{2,1,0:T(8,128)(2,1)S(1)} %bitcast.55), kind=kLoop, calls=%fused_computation | loop fusion | flops 5242880 | bytes 5242880 | tf_op jit(solution)/shard_map/concatenate | solution.py:54
  28.5 16.5 %all-to-all-done.got_ref = bf16[128,64,128]{2,1,0:T(8,128)(2,1)S(1)} async-done(((bf16[128,64,128]{2,1,0:T(8,128)(2,1)}), bf16[128,64,128]{2,1,0:T(8,128)(2,1)S(1)}, u32[]{:S(2)}, u32[]{:S(2)}) %all-to-all-start) | async-done | bytes 2097184 | tf_op jit(solution)/shard_map/all_to_all | solution.py:456
  45.0 1.3 copy-done
  46.3 7.9 %all-to-all-start.1 = ((bf16[128,80,128]{2,1,0:T(8,128)(2,1)}), bf16[128,80,128]{2,1,0:T(8,128)(2,1)}, u32[]{:S(2)}, u32[]{:S(2)}) async-start(bf16[128,80,128]{2,1,0:T(8,128)(2,1)} %pad_maximum_fusion), calls=%async_computation.1 | async-start | bytes 5242880 | tf_op jit(solution)/shard_map/all_to_all | solution.py:456
  55.4 3.2 %plan.1.plan_ref = s32[88,128]{1,0:T(8,128)} custom-call(bf16[128,64,128]{2,1,0:T(8,128)(2,1)} %copy-done), custom_call_target="tpu_custom_call" | custom-call | tf_op jit(solution)/shard_map/plan/pallas_call | solution.py:125
  58.7 16.7 %scatter.2 = (f32[3,32,16,128]{3,2,1,0:T(8,128)}, f32[16,16,128]{2,1,0:T(8,128)}, f32[21,16,128]{2,1,0:T(8,128)}, f32[21,16,128]{2,1,0:T(8,128)}) custom-call(s32[88,128]{1,0:T(8,128)} %plan.1.plan_ref, bf16[128,64,128]{2,1,0:T(8,128)(2,1)} %copy-done, f32[32,16,128]{2,1,0:T(8,128)} %pad_maximum_fusion.3.rest_0_.wind_ref), custom_call_target="tpu_custom_call" | custom-call | tf_op jit(solution)/shard_map/scatter/pallas_call | solution.py:286
  75.3 12.3 %all-to-all-done.1.got_ref = bf16[128,80,128]{2,1,0:T(8,128)(2,1)} async-done(((bf16[128,80,128]{2,1,0:T(8,128)(2,1)}), bf16[128,80,128]{2,1,0:T(8,128)(2,1)}, u32[]{:S(2)}, u32[]{:S(2)}) %all-to-all-start.1) | async-done | bytes 2621472 | tf_op jit(solution)/shard_map/all_to_all | solution.py:456
  87.7 21.1 %scatter.3 = (f32[4,32,16,128]{3,2,1,0:T(8,128)}, f32[16,16,128]{2,1,0:T(8,128)}, f32[6,16,128]{2,1,0:T(8,128)}, f32[6,16,128]{2,1,0:T(8,128)}) custom-call(s32[88,128]{1,0:T(8,128)} %plan.1.plan_ref, bf16[128,80,128]{2,1,0:T(8,128)(2,1)} %all-to-all-done.1.got_ref, f32[16,16,128]{2,1,0:T(8,128)} %get-tuple-element.14.rest_0_), custom_call_target="tpu_custom_call" | custom-call | tf_op jit(solution)/shard_map/scatter/pallas_call | solution.py:286
  109.0 5.1 %collective-permute-start.2 = (f32[16,16,128]{2,1,0:T(8,128)}, f32[16,16,128]{2,1,0:T(8,128)S(1)}, u32[]{:S(2)}, u32[]{:S(2)}) collective-permute-start(f32[16,16,128]{2,1,0:T(8,128)} %get-tuple-element.17), channel_id=1, source_target_pairs={{8,0},{16,8},{24,16},{32,24},{40,32},{48,40},{56,48},{64,56},{72,6... | collective-permute-start | bytes 393224 | tf_op jit(solution)/shard_map/ppermute | solution.py:466
  115.1 2.2 %collective-permute-start = (f32[21,16,128]{2,1,0:T(8,128)S(1)}, f32[21,16,128]{2,1,0:T(8,128)S(1)}, u32[]{:S(2)}, u32[]{:S(2)}) collective-permute-start(f32[21,16,128]{2,1,0:T(8,128)S(1)} %copy-done.13), channel_id=1, source_target_pairs={{0,1},{1,2},{2,3},{3,4},{4,5},{5,6},{6,7},{8,9},{9,10},{10,11},{11... | collective-permute-start | bytes 516104 | tf_op jit(solution)/shard_map/ppermute | solution.py:462
  117.4 5.7 %collective-permute-start.4 = (f32[21,16,128]{2,1,0:T(8,128)S(1)}, f32[21,16,128]{2,1,0:T(8,128)S(1)}, u32[]{:S(2)}, u32[]{:S(2)}) collective-permute-start(f32[21,16,128]{2,1,0:T(8,128)S(1)} %copy-done.12), channel_id=1, source_target_pairs={{1,0},{2,1},{3,2},{4,3},{5,4},{6,5},{7,6},{9,8},{10,9},{11,10},{12... | collective-permute-start | bytes 516104 | tf_op jit(solution)/shard_map/ppermute | solution.py:462
  123.2 0.8 pad_maximum_fusion.5
  124.0 3.0 %collective-permute-start.5 = (f32[12,16,128]{2,1,0:T(8,128)S(1)}, f32[12,16,128]{2,1,0:T(8,128)S(1)}, u32[]{:S(2)}, u32[]{:S(2)}) collective-permute-start(f32[12,16,128]{2,1,0:T(8,128)S(1)} %pad_maximum_fusion.5), channel_id=1, source_target_pairs={{1,0},{2,1},{3,2},{4,3},{5,4},{6,5},{7,6},{9,8},{10,9},{11,10},{12... | collective-permute-start | bytes 294920 | tf_op jit(solution)/shard_map/ppermute | solution.py:471
  127.0 0.8 pad_maximum_fusion.4
  127.8 2.8 %collective-permute-start.3 = (f32[12,16,128]{2,1,0:T(8,128)S(1)}, f32[12,16,128]{2,1,0:T(8,128)S(1)}, u32[]{:S(2)}, u32[]{:S(2)}) collective-permute-start(f32[12,16,128]{2,1,0:T(8,128)S(1)} %pad_maximum_fusion.4), channel_id=1, source_target_pairs={{0,1},{1,2},{2,3},{3,4},{4,5},{5,6},{6,7},{8,9},{9,10},{10,11},{11... | collective-permute-start | bytes 294920 | tf_op jit(solution)/shard_map/ppermute | solution.py:470
  131.3 5.1 %collective-permute-done.3.above_b = f32[12,16,128]{2,1,0:T(8,128)S(1)} collective-permute-done((f32[12,16,128]{2,1,0:T(8,128)S(1)}, f32[12,16,128]{2,1,0:T(8,128)S(1)}, u32[]{:S(2)}, u32[]{:S(2)}) %collective-permute-start.3) | collective-permute-done | bytes 98336 | tf_op jit(solution)/shard_map/ppermute | solution.py:470
  137.1 10.2 %march.1 = f32[16,32,128]{2,1,0:T(8,128)} custom-call(s32[2]{0:T(128)} %add_convert_fusion.2.edge_ref, f32[3,32,16,128]{3,2,1,0:T(8,128)} %get-tuple-element.13.first_ref, f32[4,32,16,128]{3,2,1,0:T(8,128)} %get-tuple-element.15.second_ref, f32[32,16,128]{2,1,0:T(8,128)} %pad_maximum_fusion.3.rest_0_.wind_ref, f32[21,16,128]{2,1,0:T(8,128)} %copy-done.3, ...), custom_call_target="tpu_custom_call" | custom-call | tf_op jit(solution)/shard_map/march/pallas_call | solution.py:408
  (95 shorter events, 8.8 us)
Async XLA Ops:
  0.0 2.5 %slice-start = ((bf16[7,128,16,128]{3,2,1,0:T(8,128)(2,1)}), bf16[3,128,16,128]{3,2,1,0:T(8,128)(2,1)S(1)}, s32[]{:S(2)}) async-start(bf16[7,128,16,128]{3,2,1,0:T(8,128)(2,1)} %param.8), calls=%async_computation.2 | async-start | bytes 3145728 | tf_op jit(solution)/shard_map/slice | solution.py:454
  6.5 38.5 %all-to-all-start = ((bf16[128,64,128]{2,1,0:T(8,128)(2,1)}), bf16[128,64,128]{2,1,0:T(8,128)(2,1)S(1)}, u32[]{:S(2)}, u32[]{:S(2)}) async-start(bf16[128,64,128]{2,1,0:T(8,128)(2,1)} %pad_maximum_fusion.1), calls=%async_computation | async-start | bytes 4194304 | tf_op jit(solution)/shard_map/all_to_all | solution.py:456
  17.0 3.3 %copy-start.11 = (s32[7,128,2]{1,2,0:T(2,128)S(1)}, s32[7,128,2]{1,2,0:T(2,128)}, u32[]{:S(2)}) copy-start(s32[7,128,2]{1,2,0:T(2,128)} %param.11) | copy-start | bytes 21508
  22.9 2.1 %copy-start.9 = (s32[7,128,2]{1,2,0:T(2,128)S(1)}, s32[7,128,2]{1,2,0:T(2,128)}, u32[]{:S(2)}) copy-start(s32[7,128,2]{1,2,0:T(2,128)} %param.12) | copy-start | bytes 21508
  22.9 2.1 %slice-start.4 = ((bf16[7,128,2,128]{3,2,1,0:T(2,128)(2,1)}), bf16[4,128,2,128]{3,2,1,0:T(2,128)(2,1)S(1)}, s32[]{:S(2)}) async-start(bf16[7,128,2,128]{3,2,1,0:T(2,128)(2,1)} %param.9), calls=%async_computation.6 | async-start | bytes 524288 | tf_op jit(solution)/shard_map/slice | solution.py:454
  23.0 2.1 %slice-start.5 = ((s32[7,128,2]{1,2,0:T(2,128)}), s32[4,128,2]{1,2,0:T(2,128)S(1)}, s32[]{:S(2)}) async-start(s32[7,128,2]{1,2,0:T(2,128)} %param.12), calls=%async_computation.7 | async-start | bytes 8192 | tf_op jit(solution)/shard_map/slice | solution.py:454
  23.0 2.3 %slice-start.2 = ((s32[7,128,128]{2,1,0:T(8,128)}), s32[4,128,128]{2,1,0:T(8,128)S(1)}, s32[]{:S(2)}) async-start(s32[7,128,128]{2,1,0:T(8,128)} %param.10), calls=%async_computation.4 | async-start | bytes 524288 | tf_op jit(solution)/shard_map/slice | solution.py:454
  25.2 1.6 %copy-start.1 = (bf16[128,4,16,128]{3,2,1,0:T(8,128)(2,1)S(1)}, bf16[128,4,16,128]{3,2,1,0:T(8,128)(2,1)}, u32[]{:S(2)}) copy-start(bf16[128,4,16,128]{3,2,1,0:T(8,128)(2,1)} %copy.37) | copy-start | bytes 6291460
  28.5 25.7 %copy-start.10 = (f32[16,16]{1,0:T(8,128)S(1)}, f32[16,16]{1,0:T(8,128)}, u32[]{:S(2)}) copy-start(f32[16,16]{1,0:T(8,128)} %param.15) | copy-start | bytes 3076
  28.5 25.9 %copy-start.7 = (f32[4,32,128]{2,1,0:T(8,128)S(1)}, f32[4,32,128]{2,1,0:T(8,128)}, u32[]{:S(2)}) copy-start(f32[4,32,128]{2,1,0:T(8,128)} %param.14) | copy-start | bytes 196612
  28.5 25.9 %copy-start.8 = (f32[4,32,128]{2,1,0:T(8,128)S(1)}, f32[4,32,128]{2,1,0:T(8,128)}, u32[]{:S(2)}) copy-start(f32[4,32,128]{2,1,0:T(8,128)} %param.13) | copy-start | bytes 196612
  46.3 41.4 %all-to-all-start.1 = ((bf16[128,80,128]{2,1,0:T(8,128)(2,1)}), bf16[128,80,128]{2,1,0:T(8,128)(2,1)}, u32[]{:S(2)}, u32[]{:S(2)}) async-start(bf16[128,80,128]{2,1,0:T(8,128)(2,1)} %pad_maximum_fusion), calls=%async_computation.1 | async-start | bytes 5242880 | tf_op jit(solution)/shard_map/all_to_all | solution.py:456
  75.3 39.8 %copy-start.13 = (f32[21,16,128]{2,1,0:T(8,128)S(1)}, f32[21,16,128]{2,1,0:T(8,128)}, u32[]{:S(2)}) copy-start(f32[21,16,128]{2,1,0:T(8,128)} %get-tuple-element.16) | copy-start | bytes 516100
  75.3 42.0 %copy-start.12 = (f32[21,16,128]{2,1,0:T(8,128)S(1)}, f32[21,16,128]{2,1,0:T(8,128)}, u32[]{:S(2)}) copy-start(f32[21,16,128]{2,1,0:T(8,128)} %get-tuple-element.19) | copy-start | bytes 516100
  108.7 14.4 %collective-permute-start.1 = (f32[16,16,128]{2,1,0:T(8,128)}, f32[16,16,128]{2,1,0:T(8,128)S(1)}, u32[]{:S(2)}, u32[]{:S(2)}) collective-permute-start(f32[16,16,128]{2,1,0:T(8,128)} %get-tuple-element.17), channel_id=1, source_target_pairs={{0,8},{8,16},{16,24},{24,32},{32,40},{40,48},{48,56},{56,64},{64,7... | collective-permute-start | bytes 393224 | tf_op jit(solution)/shard_map/ppermute | solution.py:465
  109.0 14.1 %collective-permute-start.2 = (f32[16,16,128]{2,1,0:T(8,128)}, f32[16,16,128]{2,1,0:T(8,128)S(1)}, u32[]{:S(2)}, u32[]{:S(2)}) collective-permute-start(f32[16,16,128]{2,1,0:T(8,128)} %get-tuple-element.17), channel_id=1, source_target_pairs={{8,0},{16,8},{24,16},{32,24},{40,32},{48,40},{56,48},{64,56},{72,6... | collective-permute-start | bytes 393224 | tf_op jit(solution)/shard_map/ppermute | solution.py:466
  115.1 16.2 %collective-permute-start = (f32[21,16,128]{2,1,0:T(8,128)S(1)}, f32[21,16,128]{2,1,0:T(8,128)S(1)}, u32[]{:S(2)}, u32[]{:S(2)}) collective-permute-start(f32[21,16,128]{2,1,0:T(8,128)S(1)} %copy-done.13), channel_id=1, source_target_pairs={{0,1},{1,2},{2,3},{3,4},{4,5},{5,6},{6,7},{8,9},{9,10},{10,11},{11... | collective-permute-start | bytes 516104 | tf_op jit(solution)/shard_map/ppermute | solution.py:462
  117.4 13.9 %collective-permute-start.4 = (f32[21,16,128]{2,1,0:T(8,128)S(1)}, f32[21,16,128]{2,1,0:T(8,128)S(1)}, u32[]{:S(2)}, u32[]{:S(2)}) collective-permute-start(f32[21,16,128]{2,1,0:T(8,128)S(1)} %copy-done.12), channel_id=1, source_target_pairs={{1,0},{2,1},{3,2},{4,3},{5,4},{6,5},{7,6},{9,8},{10,9},{11,10},{12... | collective-permute-start | bytes 516104 | tf_op jit(solution)/shard_map/ppermute | solution.py:462
  123.2 13.3 %copy-start.2 = (f32[16,16,128]{2,1,0:T(8,128)}, f32[16,16,128]{2,1,0:T(8,128)S(1)}, u32[]{:S(2)}) copy-start(f32[16,16,128]{2,1,0:T(8,128)S(1)} %broadcast_select_fusion.ends_ref) | copy-start | bytes 393220
  124.0 7.3 %collective-permute-start.5 = (f32[12,16,128]{2,1,0:T(8,128)S(1)}, f32[12,16,128]{2,1,0:T(8,128)S(1)}, u32[]{:S(2)}, u32[]{:S(2)}) collective-permute-start(f32[12,16,128]{2,1,0:T(8,128)S(1)} %pad_maximum_fusion.5), channel_id=1, source_target_pairs={{1,0},{2,1},{3,2},{4,3},{5,4},{6,5},{7,6},{9,8},{10,9},{11,10},{12... | collective-permute-start | bytes 294920 | tf_op jit(solution)/shard_map/ppermute | solution.py:471
  127.8 8.6 %collective-permute-start.3 = (f32[12,16,128]{2,1,0:T(8,128)S(1)}, f32[12,16,128]{2,1,0:T(8,128)S(1)}, u32[]{:S(2)}, u32[]{:S(2)}) collective-permute-start(f32[12,16,128]{2,1,0:T(8,128)S(1)} %pad_maximum_fusion.4), channel_id=1, source_target_pairs={{0,1},{1,2},{2,3},{3,4},{4,5},{5,6},{6,7},{8,9},{9,10},{10,11},{11... | collective-permute-start | bytes 294920 | tf_op jit(solution)/shard_map/ppermute | solution.py:470
  131.3 5.2 %copy-start.3 = (f32[21,16,128]{2,1,0:T(8,128)}, f32[21,16,128]{2,1,0:T(8,128)S(1)}, u32[]{:S(2)}) copy-start(f32[21,16,128]{2,1,0:T(8,128)S(1)} %collective-permute-done.above_a) | copy-start | bytes 516100
  131.3 5.2 %copy-start.4 = (f32[21,16,128]{2,1,0:T(8,128)}, f32[21,16,128]{2,1,0:T(8,128)S(1)}, u32[]{:S(2)}) copy-start(f32[21,16,128]{2,1,0:T(8,128)S(1)} %collective-permute-done.4.below_a) | copy-start | bytes 516100
  131.3 5.1 %copy-start.5 = (f32[12,16,128]{2,1,0:T(8,128)}, f32[12,16,128]{2,1,0:T(8,128)S(1)}, u32[]{:S(2)}) copy-start(f32[12,16,128]{2,1,0:T(8,128)S(1)} %collective-permute-done.5.below_b) | copy-start | bytes 294916
  (4 other events, 4.0 us)

commit v5 on v4

--- a/solution.py
+++ b/solution.py
@@ -70,7 +70,7 @@
     return (tiles + BLOCKS * (GROUP - 1)) // GROUP
 
 
-def plan_kernel(slots, spot_row, got_ref, out_ref):
+def plan_kernel(slots, early, spot_row, got_ref, out_ref):
     senders = got_ref.shape[0]
     tiles = 2 * senders
     spots = jnp.transpose(got_ref[:, spot_row, :].astype(F32))
@@ -92,7 +92,7 @@
     index = lax.broadcasted_iota(jnp.int32, (8, tiles), 1)
     kinds = jnp.where(lax.broadcasted_iota(jnp.int32, (8, tiles), 0) == 0, index, 1).astype(F32).astype(BF16)
     place = lax.broadcasted_iota(jnp.int32, (GROUP * LANES, tiles), 0).astype(F32)
-    most = jnp.zeros((1, LANES), F32)
+    most = [jnp.zeros((1, LANES), F32)] * 2
     rows = []
     for slot in range(slots):
         part = slice(slot * BLOCKS, (slot + 1) * BLOCKS)
@@ -112,8 +112,9 @@
             taken = taken + order[1:2, j * LANES : (j + 1) * LANES]
         block = jnp.sum(jnp.where(start + size <= number, 1.0, 0.0), axis=0, keepdims=True)
         rows.append(jnp.minimum(block, BLOCKS - 1.0) + BLOCKS * taken)
-        most = jnp.maximum(most, start[BLOCKS - 1 :] + size[BLOCKS - 1 :])
-    rows += [jnp.zeros((LANES - 1 - len(rows), LANES), F32), most]
+        which = 0 if slot < early else 1
+        most[which] = jnp.maximum(most[which], start[BLOCKS - 1 :] + size[BLOCKS - 1 :])
+    rows += [jnp.zeros((LANES - 2 - len(rows), LANES), F32)] + most
     table = jnp.transpose(jnp.concatenate(rows, axis=0))
     out_ref[...] = table[: out_ref.shape[0]].astype(jnp.int32)
 
@@ -123,7 +124,7 @@
     spot_row = aux_row(slots_here, 0) + 6
     limit = -(-(group_limit(2 * senders) + 2 * UNITS) // 8) * 8
     return pl.pallas_call(
-        functools.partial(plan_kernel, slots_all, spot_row),
+        functools.partial(plan_kernel, slots_all, slots_here, spot_row),
         in_specs=[pl.BlockSpec(memory_space=pltpu.VMEM)],
         out_specs=pl.BlockSpec(memory_space=pltpu.VMEM),
         out_shape=jax.ShapeDtypeStruct((limit, LANES), jnp.int32),
@@ -215,7 +216,7 @@
     for acc_ref in acc_refs:
         acc_ref[...] = jnp.zeros_like(acc_ref)
     fetch(0)
-    lax.fori_loop(0, (plan_ref[0, LANES - 1] + UNITS - 1) // UNITS, several, 0)
+    lax.fori_loop(0, (plan_ref[0, LANES - 1 if late else LANES - 2] + UNITS - 1) // UNITS, several, 0)
 
     lane_group = lane >> 4
     for slot in range(slots):

time: 148 us -> 148 us (level)
  no operation moved by 1% of the time
where the time goes in v5:
time: 148 us; the launch traced here: 147 us
  Pallas kernels  51.2 us (35%)
  starting transfers between devices  37.6 us (25%)
  waiting for transfers between devices  33.9 us (23%)
  local copies, waits for them, and re-layouts  12.5 us (8%)
  other arithmetic  11.7 us (8%)
    pallas_call x2, Pallas kernels, scatter(): pl.pallas_call(functools.partial(scatter_kernel, slots, offset, widths),...  37.7 us
    all_to_all x2, waiting for transfers between devices, program(): lax.all_to_all(payload, AXES, split_axis=0, concat_axis=0, tiled=True)  28.8 us
    all_to_all x2, starting transfers between devices, program(): lax.all_to_all(payload, AXES, split_axis=0, concat_axis=0, tiled=True)  18.4 us
    pallas_call x1, Pallas kernels, march(): pl.pallas_call(functools.partial(march_kernel, widths, halo, first.shape[...  10.2 us
    ppermute x1, starting transfers between devices, program(): lax.ppermute(top_a, 'lat', down)  5.72 us
    ppermute x1, waiting for transfers between devices, program(): above = [above_a, lax.ppermute(last_up, 'lat', up)]  5.12 us
    ppermute x1, starting transfers between devices, program(): east = lax.ppermute(pack, 'lon', back)  5.05 us
    slice x13, local copies, waits for them, and re-layouts, program(): x[low:high][::-1]  3.94 us
  transfers between devices with their start and end apart: 8, of which 3 were waited for; matrix products, arithmetic and copies ran while one was open for 10% of the time, Pallas kernels for 14%

profile of v5, /device:TPU:2, one launch (start us, length us, event | category | flops | bytes accessed | tf_op | source)
XLA Modules:
  0.0 147.3 jit_solution(5237305780331795709)
XLA Ops:
  0.0 0.8 fusion.13
  4.9 1.6 %pad_maximum_fusion.1 = bf16[128,64,128]{2,1,0:T(8,128)(2,1)} fusion(bf16[128,16,128]{2,1,0:T(8,128)(2,1)S(1)} %bitcast.58, bf16[128,48,128]{2,1,0:T(8,128)(2,1)S(1)} %bitcast.56), kind=kLoop, calls=%fused_computation.1 | loop fusion | flops 4194304 | bytes 4194304 | tf_op jit(solution)/shard_map/concatenate | solution.py:54
  6.5 10.5 %all-to-all-start = ((bf16[128,64,128]{2,1,0:T(8,128)(2,1)}), bf16[128,64,128]{2,1,0:T(8,128)(2,1)S(1)}, u32[]{:S(2)}, u32[]{:S(2)}) async-start(bf16[128,64,128]{2,1,0:T(8,128)(2,1)} %pad_maximum_fusion.1), calls=%async_computation | async-start | bytes 4194304 | tf_op jit(solution)/shard_map/all_to_all | solution.py:457
  17.1 3.3 %slice.101 = bf16[4,128,16,128]{3,2,1,0:T(8,128)(2,1)} slice(bf16[7,128,16,128]{3,2,1,0:T(8,128)(2,1)} %param.8), slice={[0:4], [0:128], [0:16], [0:128]} | slice | bytes 4194304 | tf_op jit(solution)/shard_map/slice | solution.py:455
  20.6 2.3 %select_bitcast_fusion = bf16[128,4,16,128]{3,2,0,1:T(8,128)(2,1)S(1)} fusion(bf16[4,128,16,128]{3,2,1,0:T(8,128)(2,1)} %slice.101, pred[4,128,128]{2,1,0:T(8,128)(4,1)S(1)} %select_compare_fusion), kind=kLoop, calls=%fused_computation.2 | loop fusion | flops 1048576 | bytes 4259840 | tf_op jit(solution)/shard_map/transpose | solution.py:56
  23.0 2.0 %copy.37 = bf16[128,4,16,128]{3,2,1,0:T(8,128)(2,1)} copy(bf16[128,4,16,128]{3,2,0,1:T(8,128)(2,1)S(1)} %select_bitcast_fusion) | data formatting | bytes 4194304 | tf_op jit(solution)/shard_map/transpose | solution.py:56
  25.9 0.9 copy-done.1
  26.8 1.7 %pad_maximum_fusion = bf16[128,80,128]{2,1,0:T(8,128)(2,1)} fusion(bf16[128,16,128]{2,1,0:T(8,128)(2,1)S(1)} %bitcast.57, bf16[128,64,128]{2,1,0:T(8,128)(2,1)S(1)} %bitcast.55), kind=kLoop, calls=%fused_computation | loop fusion | flops 5242880 | bytes 5242880 | tf_op jit(solution)/shard_map/concatenate | solution.py:54
  28.5 16.5 %all-to-all-done.got_ref = bf16[128,64,128]{2,1,0:T(8,128)(2,1)S(1)} async-done(((bf16[128,64,128]{2,1,0:T(8,128)(2,1)}), bf16[128,64,128]{2,1,0:T(8,128)(2,1)S(1)}, u32[]{:S(2)}, u32[]{:S(2)}) %all-to-all-start) | async-done | bytes 2097184 | tf_op jit(solution)/shard_map/all_to_all | solution.py:457
  45.0 1.3 copy-done
  46.3 7.9 %all-to-all-start.1 = ((bf16[128,80,128]{2,1,0:T(8,128)(2,1)}), bf16[128,80,128]{2,1,0:T(8,128)(2,1)}, u32[]{:S(2)}, u32[]{:S(2)}) async-start(bf16[128,80,128]{2,1,0:T(8,128)(2,1)} %pad_maximum_fusion), calls=%async_computation.1 | async-start | bytes 5242880 | tf_op jit(solution)/shard_map/all_to_all | solution.py:457
  55.4 3.2 %plan.1.plan_ref = s32[88,128]{1,0:T(8,128)} custom-call(bf16[128,64,128]{2,1,0:T(8,128)(2,1)} %copy-done), custom_call_target="tpu_custom_call" | custom-call | tf_op jit(solution)/shard_map/plan/pallas_call | solution.py:126
  58.7 16.7 %scatter.2 = (f32[3,32,16,128]{3,2,1,0:T(8,128)}, f32[16,16,128]{2,1,0:T(8,128)}, f32[21,16,128]{2,1,0:T(8,128)}, f32[21,16,128]{2,1,0:T(8,128)}) custom-call(s32[88,128]{1,0:T(8,128)} %plan.1.plan_ref, bf16[128,64,128]{2,1,0:T(8,128)(2,1)} %copy-done, f32[32,16,128]{2,1,0:T(8,128)} %pad_maximum_fusion.3.rest_0_.wind_ref), custom_call_target="tpu_custom_call" | custom-call | tf_op jit(solution)/shard_map/scatter/pallas_call | solution.py:287
  75.3 12.3 %all-to-all-done.1.got_ref = bf16[128,80,128]{2,1,0:T(8,128)(2,1)} async-done(((bf16[128,80,128]{2,1,0:T(8,128)(2,1)}), bf16[128,80,128]{2,1,0:T(8,128)(2,1)}, u32[]{:S(2)}, u32[]{:S(2)}) %all-to-all-start.1) | async-done | bytes 2621472 | tf_op jit(solution)/shard_map/all_to_all | solution.py:457
  87.7 21.1 %scatter.3 = (f32[4,32,16,128]{3,2,1,0:T(8,128)}, f32[16,16,128]{2,1,0:T(8,128)}, f32[6,16,128]{2,1,0:T(8,128)}, f32[6,16,128]{2,1,0:T(8,128)}) custom-call(s32[88,128]{1,0:T(8,128)} %plan.1.plan_ref, bf16[128,80,128]{2,1,0:T(8,128)(2,1)} %all-to-all-done.1.got_ref, f32[16,16,128]{2,1,0:T(8,128)} %get-tuple-element.14.rest_0_), custom_call_target="tpu_custom_call" | custom-call | tf_op jit(solution)/shard_map/scatter/pallas_call | solution.py:287
  109.0 5.1 %collective-permute-start.2 = (f32[16,16,128]{2,1,0:T(8,128)}, f32[16,16,128]{2,1,0:T(8,128)S(1)}, u32[]{:S(2)}, u32[]{:S(2)}) collective-permute-start(f32[16,16,128]{2,1,0:T(8,128)} %get-tuple-element.17), channel_id=1, source_target_pairs={{8,0},{16,8},{24,16},{32,24},{40,32},{48,40},{56,48},{64,56},{72,6... | collective-permute-start | bytes 393224 | tf_op jit(solution)/shard_map/ppermute | solution.py:467
  115.1 2.2 %collective-permute-start = (f32[21,16,128]{2,1,0:T(8,128)S(1)}, f32[21,16,128]{2,1,0:T(8,128)S(1)}, u32[]{:S(2)}, u32[]{:S(2)}) collective-permute-start(f32[21,16,128]{2,1,0:T(8,128)S(1)} %copy-done.13), channel_id=1, source_target_pairs={{0,1},{1,2},{2,3},{3,4},{4,5},{5,6},{6,7},{8,9},{9,10},{10,11},{11... | collective-permute-start | bytes 516104 | tf_op jit(solution)/shard_map/ppermute | solution.py:463
  117.4 5.7 %collective-permute-start.4 = (f32[21,16,128]{2,1,0:T(8,128)S(1)}, f32[21,16,128]{2,1,0:T(8,128)S(1)}, u32[]{:S(2)}, u32[]{:S(2)}) collective-permute-start(f32[21,16,128]{2,1,0:T(8,128)S(1)} %copy-done.12), channel_id=1, source_target_pairs={{1,0},{2,1},{3,2},{4,3},{5,4},{6,5},{7,6},{9,8},{10,9},{11,10},{12... | collective-permute-start | bytes 516104 | tf_op jit(solution)/shard_map/ppermute | solution.py:463
  123.2 0.8 pad_maximum_fusion.5
  124.0 3.0 %collective-permute-start.5 = (f32[12,16,128]{2,1,0:T(8,128)S(1)}, f32[12,16,128]{2,1,0:T(8,128)S(1)}, u32[]{:S(2)}, u32[]{:S(2)}) collective-permute-start(f32[12,16,128]{2,1,0:T(8,128)S(1)} %pad_maximum_fusion.5), channel_id=1, source_target_pairs={{1,0},{2,1},{3,2},{4,3},{5,4},{6,5},{7,6},{9,8},{10,9},{11,10},{12... | collective-permute-start | bytes 294920 | tf_op jit(solution)/shard_map/ppermute | solution.py:472
  127.0 0.8 pad_maximum_fusion.4
  127.8 2.8 %collective-permute-start.3 = (f32[12,16,128]{2,1,0:T(8,128)S(1)}, f32[12,16,128]{2,1,0:T(8,128)S(1)}, u32[]{:S(2)}, u32[]{:S(2)}) collective-permute-start(f32[12,16,128]{2,1,0:T(8,128)S(1)} %pad_maximum_fusion.4), channel_id=1, source_target_pairs={{0,1},{1,2},{2,3},{3,4},{4,5},{5,6},{6,7},{8,9},{9,10},{10,11},{11... | collective-permute-start | bytes 294920 | tf_op jit(solution)/shard_map/ppermute | solution.py:471
  131.3 5.1 %collective-permute-done.3.above_b = f32[12,16,128]{2,1,0:T(8,128)S(1)} collective-permute-done((f32[12,16,128]{2,1,0:T(8,128)S(1)}, f32[12,16,128]{2,1,0:T(8,128)S(1)}, u32[]{:S(2)}, u32[]{:S(2)}) %collective-permute-start.3) | collective-permute-done | bytes 98336 | tf_op jit(solution)/shard_map/ppermute | solution.py:471
  137.1 10.2 %march.1 = f32[16,32,128]{2,1,0:T(8,128)} custom-call(s32[2]{0:T(128)} %add_convert_fusion.2.edge_ref, f32[3,32,16,128]{3,2,1,0:T(8,128)} %get-tuple-element.13.first_ref, f32[4,32,16,128]{3,2,1,0:T(8,128)} %get-tuple-element.15.second_ref, f32[32,16,128]{2,1,0:T(8,128)} %pad_maximum_fusion.3.rest_0_.wind_ref, f32[21,16,128]{2,1,0:T(8,128)} %copy-done.3, ...), custom_call_target="tpu_custom_call" | custom-call | tf_op jit(solution)/shard_map/march/pallas_call | solution.py:409
  (95 shorter events, 8.8 us)
Async XLA Ops:
  0.0 2.5 %slice-start = ((bf16[7,128,16,128]{3,2,1,0:T(8,128)(2,1)}), bf16[3,128,16,128]{3,2,1,0:T(8,128)(2,1)S(1)}, s32[]{:S(2)}) async-start(bf16[7,128,16,128]{3,2,1,0:T(8,128)(2,1)} %param.8), calls=%async_computation.2 | async-start | bytes 3145728 | tf_op jit(solution)/shard_map/slice | solution.py:455
  6.5 38.5 %all-to-all-start = ((bf16[128,64,128]{2,1,0:T(8,128)(2,1)}), bf16[128,64,128]{2,1,0:T(8,128)(2,1)S(1)}, u32[]{:S(2)}, u32[]{:S(2)}) async-start(bf16[128,64,128]{2,1,0:T(8,128)(2,1)} %pad_maximum_fusion.1), calls=%async_computation | async-start | bytes 4194304 | tf_op jit(solution)/shard_map/all_to_all | solution.py:457
  17.0 3.3 %copy-start.11 = (s32[7,128,2]{1,2,0:T(2,128)S(1)}, s32[7,128,2]{1,2,0:T(2,128)}, u32[]{:S(2)}) copy-start(s32[7,128,2]{1,2,0:T(2,128)} %param.11) | copy-start | bytes 21508
  22.9 2.1 %copy-start.9 = (s32[7,128,2]{1,2,0:T(2,128)S(1)}, s32[7,128,2]{1,2,0:T(2,128)}, u32[]{:S(2)}) copy-start(s32[7,128,2]{1,2,0:T(2,128)} %param.12) | copy-start | bytes 21508
  22.9 2.1 %slice-start.4 = ((bf16[7,128,2,128]{3,2,1,0:T(2,128)(2,1)}), bf16[4,128,2,128]{3,2,1,0:T(2,128)(2,1)S(1)}, s32[]{:S(2)}) async-start(bf16[7,128,2,128]{3,2,1,0:T(2,128)(2,1)} %param.9), calls=%async_computation.6 | async-start | bytes 524288 | tf_op jit(solution)/shard_map/slice | solution.py:455
  23.0 2.1 %slice-start.5 = ((s32[7,128,2]{1,2,0:T(2,128)}), s32[4,128,2]{1,2,0:T(2,128)S(1)}, s32[]{:S(2)}) async-start(s32[7,128,2]{1,2,0:T(2,128)} %param.12), calls=%async_computation.7 | async-start | bytes 8192 | tf_op jit(solution)/shard_map/slice | solution.py:455
  23.0 2.3 %slice-start.2 = ((s32[7,128,128]{2,1,0:T(8,128)}), s32[4,128,128]{2,1,0:T(8,128)S(1)}, s32[]{:S(2)}) async-start(s32[7,128,128]{2,1,0:T(8,128)} %param.10), calls=%async_computation.4 | async-start | bytes 524288 | tf_op jit(solution)/shard_map/slice | solution.py:455
  25.2 1.6 %copy-start.1 = (bf16[128,4,16,128]{3,2,1,0:T(8,128)(2,1)S(1)}, bf16[128,4,16,128]{3,2,1,0:T(8,128)(2,1)}, u32[]{:S(2)}) copy-start(bf16[128,4,16,128]{3,2,1,0:T(8,128)(2,1)} %copy.37) | copy-start | bytes 6291460
  28.5 25.7 %copy-start.10 = (f32[16,16]{1,0:T(8,128)S(1)}, f32[16,16]{1,0:T(8,128)}, u32[]{:S(2)}) copy-start(f32[16,16]{1,0:T(8,128)} %param.15) | copy-start | bytes 3076
  28.5 25.9 %copy-start.7 = (f32[4,32,128]{2,1,0:T(8,128)S(1)}, f32[4,32,128]{2,1,0:T(8,128)}, u32[]{:S(2)}) copy-start(f32[4,32,128]{2,1,0:T(8,128)} %param.14) | copy-start | bytes 196612
  28.5 25.9 %copy-start.8 = (f32[4,32,128]{2,1,0:T(8,128)S(1)}, f32[4,32,128]{2,1,0:T(8,128)}, u32[]{:S(2)}) copy-start(f32[4,32,128]{2,1,0:T(8,128)} %param.13) | copy-start | bytes 196612
  46.3 41.4 %all-to-all-start.1 = ((bf16[128,80,128]{2,1,0:T(8,128)(2,1)}), bf16[128,80,128]{2,1,0:T(8,128)(2,1)}, u32[]{:S(2)}, u32[]{:S(2)}) async-start(bf16[128,80,128]{2,1,0:T(8,128)(2,1)} %pad_maximum_fusion), calls=%async_computation.1 | async-start | bytes 5242880 | tf_op jit(solution)/shard_map/all_to_all | solution.py:457
  75.3 39.8 %copy-start.13 = (f32[21,16,128]{2,1,0:T(8,128)S(1)}, f32[21,16,128]{2,1,0:T(8,128)}, u32[]{:S(2)}) copy-start(f32[21,16,128]{2,1,0:T(8,128)} %get-tuple-element.16) | copy-start | bytes 516100
  75.3 42.0 %copy-start.12 = (f32[21,16,128]{2,1,0:T(8,128)S(1)}, f32[21,16,128]{2,1,0:T(8,128)}, u32[]{:S(2)}) copy-start(f32[21,16,128]{2,1,0:T(8,128)} %get-tuple-element.19) | copy-start | bytes 516100
  108.7 14.4 %collective-permute-start.1 = (f32[16,16,128]{2,1,0:T(8,128)}, f32[16,16,128]{2,1,0:T(8,128)S(1)}, u32[]{:S(2)}, u32[]{:S(2)}) collective-permute-start(f32[16,16,128]{2,1,0:T(8,128)} %get-tuple-element.17), channel_id=1, source_target_pairs={{0,8},{8,16},{16,24},{24,32},{32,40},{40,48},{48,56},{56,64},{64,7... | collective-permute-start | bytes 393224 | tf_op jit(solution)/shard_map/ppermute | solution.py:466
  109.0 14.1 %collective-permute-start.2 = (f32[16,16,128]{2,1,0:T(8,128)}, f32[16,16,128]{2,1,0:T(8,128)S(1)}, u32[]{:S(2)}, u32[]{:S(2)}) collective-permute-start(f32[16,16,128]{2,1,0:T(8,128)} %get-tuple-element.17), channel_id=1, source_target_pairs={{8,0},{16,8},{24,16},{32,24},{40,32},{48,40},{56,48},{64,56},{72,6... | collective-permute-start | bytes 393224 | tf_op jit(solution)/shard_map/ppermute | solution.py:467
  115.1 16.2 %collective-permute-start = (f32[21,16,128]{2,1,0:T(8,128)S(1)}, f32[21,16,128]{2,1,0:T(8,128)S(1)}, u32[]{:S(2)}, u32[]{:S(2)}) collective-permute-start(f32[21,16,128]{2,1,0:T(8,128)S(1)} %copy-done.13), channel_id=1, source_target_pairs={{0,1},{1,2},{2,3},{3,4},{4,5},{5,6},{6,7},{8,9},{9,10},{10,11},{11... | collective-permute-start | bytes 516104 | tf_op jit(solution)/shard_map/ppermute | solution.py:463
  117.4 13.9 %collective-permute-start.4 = (f32[21,16,128]{2,1,0:T(8,128)S(1)}, f32[21,16,128]{2,1,0:T(8,128)S(1)}, u32[]{:S(2)}, u32[]{:S(2)}) collective-permute-start(f32[21,16,128]{2,1,0:T(8,128)S(1)} %copy-done.12), channel_id=1, source_target_pairs={{1,0},{2,1},{3,2},{4,3},{5,4},{6,5},{7,6},{9,8},{10,9},{11,10},{12... | collective-permute-start | bytes 516104 | tf_op jit(solution)/shard_map/ppermute | solution.py:463
  123.2 13.3 %copy-start.2 = (f32[16,16,128]{2,1,0:T(8,128)}, f32[16,16,128]{2,1,0:T(8,128)S(1)}, u32[]{:S(2)}) copy-start(f32[16,16,128]{2,1,0:T(8,128)S(1)} %broadcast_select_fusion.ends_ref) | copy-start | bytes 393220
  124.0 7.3 %collective-permute-start.5 = (f32[12,16,128]{2,1,0:T(8,128)S(1)}, f32[12,16,128]{2,1,0:T(8,128)S(1)}, u32[]{:S(2)}, u32[]{:S(2)}) collective-permute-start(f32[12,16,128]{2,1,0:T(8,128)S(1)} %pad_maximum_fusion.5), channel_id=1, source_target_pairs={{1,0},{2,1},{3,2},{4,3},{5,4},{6,5},{7,6},{9,8},{10,9},{11,10},{12... | collective-permute-start | bytes 294920 | tf_op jit(solution)/shard_map/ppermute | solution.py:472
  127.8 8.6 %collective-permute-start.3 = (f32[12,16,128]{2,1,0:T(8,128)S(1)}, f32[12,16,128]{2,1,0:T(8,128)S(1)}, u32[]{:S(2)}, u32[]{:S(2)}) collective-permute-start(f32[12,16,128]{2,1,0:T(8,128)S(1)} %pad_maximum_fusion.4), channel_id=1, source_target_pairs={{0,1},{1,2},{2,3},{3,4},{4,5},{5,6},{6,7},{8,9},{9,10},{10,11},{11... | collective-permute-start | bytes 294920 | tf_op jit(solution)/shard_map/ppermute | solution.py:471
  131.3 5.2 %copy-start.3 = (f32[21,16,128]{2,1,0:T(8,128)}, f32[21,16,128]{2,1,0:T(8,128)S(1)}, u32[]{:S(2)}) copy-start(f32[21,16,128]{2,1,0:T(8,128)S(1)} %collective-permute-done.above_a) | copy-start | bytes 516100
  131.3 5.2 %copy-start.4 = (f32[21,16,128]{2,1,0:T(8,128)}, f32[21,16,128]{2,1,0:T(8,128)S(1)}, u32[]{:S(2)}) copy-start(f32[21,16,128]{2,1,0:T(8,128)S(1)} %collective-permute-done.4.below_a) | copy-start | bytes 516100
  131.3 5.1 %copy-start.5 = (f32[12,16,128]{2,1,0:T(8,128)}, f32[12,16,128]{2,1,0:T(8,128)S(1)}, u32[]{:S(2)}) copy-start(f32[12,16,128]{2,1,0:T(8,128)S(1)} %collective-permute-done.5.below_b) | copy-start | bytes 294916
  (4 other events, 4.0 us)
